TPU v7x, 512 devices: a whole 4x8x8 slice. The times are simulated.
512 devices in a mesh: dp: 16 (over z, core), head: 8 (over y), tok: 4 (over x).
Axes of the slice: x: 4, y: 8, z: 8, core: 2. Of those that a mesh axis runs over, the one named last changes fastest.
Arguments:
- mamba_input: bfloat16 [32, 64, 8192], P('dp', 'tok', 'head'), may hold values from -6 to 6
- gate_input: bfloat16 [32, 64, 8192], P('dp', 'tok', 'head'), may hold values from -6 to 6
- in_b: bfloat16 [32, 64, 1024], P('dp', 'tok', 'head'), may hold values from -0.75 to 0.75
- in_c: bfloat16 [32, 64, 1024], P('dp', 'tok', 'head'), may hold values from -0.75 to 0.75
- step_size: bfloat16 [32, 64, 128], P('dp', 'tok', 'head'), may hold values from 0.019897461 to 1
- decay_rate: float32 [128], P('head'), may hold values from 0.01 to 1
- skip_weight: float32 [128], P('head'), may hold values from 0.5 to 1.5
- norm_gain: float32 [8192], P('head'), may hold values from 0.1 to 1.9
- ssm_state: bfloat16 [32, 128, 64, 128], P('dp', 'head', None, 'tok'), may hold values from -6 to 6
- out_weight: bfloat16 [8192, 4096], P(('head', 'tok')), may hold values from -0.0625 to 0.0625
- queries: bfloat16 [32, 64, 4096], P('dp', 'tok', 'head'), may hold values from -6 to 6
- draft_token_keys: bfloat16 [32, 64, 1024], P('dp', 'tok', 'head'), may hold values from -6 to 6
- draft_values: bfloat16 [32, 64, 1024], P('dp', 'tok', 'head'), may hold values from -6 to 6
- cached_key_rows: bfloat16 [32, 4096, 1024], P('dp', 'tok', 'head'), may hold values from -4 to 4
- cache_values: bfloat16 [32, 4096, 1024], P('dp', 'tok', 'head'), may hold values from -6 to 6
- cache_len: int32 [32], P('dp'), may hold values from 2 to 4096
- accepted: int32 [32], P('dp'), may hold values from 0 to 64
Outputs:
- mamba_out: bfloat16 [64, 32, 4096], P(('head', 'tok'), 'dp')
- attn_context: bfloat16 [32, 64, 4096], P('dp', 'tok', 'head')
- committed_state: bfloat16 [32, 128, 64, 128], P('dp', 'head', None, 'tok')
Inputs may be any that keep to these rules, and one draw needn't show every extreme that they name: Each sequence's cached positions 0 to cache_len - 1 are valid.
All inputs are finite; a program needn't handle non-finite values.
Results may differ from a plain program's by a relative error of at most 0.018.
Values may be sent and summed in bfloat16 or wider, within the bound.
No kernel may reach another device: no remote copies, remote signals or barrier semaphores. Data moves between devices by JAX's collectives and lax.ppermute only.
A program may use at most 64 MiB of HBM per device.

v0:
```python
import jax
import jax.numpy as jnp
from jax import lax
from jax.sharding import PartitionSpec as P

EPSILON = 1e-05
MASKED = -1e30


def in_one_piece(arrays, axis, split_dim, concat_dim, along):
    widths = [a.shape[along] for a in arrays]
    both = jnp.concatenate(arrays, axis=along)
    filled = lax.all_to_all(both, axis, split_axis=split_dim, concat_axis=concat_dim, tiled=True)
    return tuple(jnp.split(filled, [sum(widths[:k]) for k in range(1, len(widths))], axis=along))


def sent_together(arrays, axis, dim, along):
    widths = [a.shape[along] for a in arrays]
    both = jnp.concatenate(arrays, axis=along)
    filled = lax.all_gather(both, axis, axis=dim, tiled=True)
    return tuple(jnp.split(filled, [sum(widths[:k]) for k in range(1, len(widths))], axis=along))


def in_blocks(array, dim, count):
    before, after = (array.shape[:dim], array.shape[dim + 1 :])
    return jnp.moveaxis(array.reshape(*before, count, -1, *after), dim, 0)


def summed_on_arrival(array, axis, dim):
    parts = in_blocks(array, dim, lax.axis_size(axis))
    arrived = lax.all_to_all(parts, axis, split_axis=0, concat_axis=0, tiled=True)
    return arrived.astype(jnp.float32).sum(axis=0)


def from_everyone(array, axis):
    copies = jnp.broadcast_to(array, (lax.axis_size(axis), *array.shape))
    return lax.all_to_all(copies, axis, split_axis=0, concat_axis=0, tiled=True)


def laid_out(parts, dim):
    parts = jnp.moveaxis(parts, 0, dim)
    shape = parts.shape
    return parts.reshape(*shape[:dim], shape[dim] * shape[dim + 1], *shape[dim + 2 :])


def gather_directly(array, axis, dim):
    parts = from_everyone(array, axis)
    return laid_out(parts, dim)


def within_block(running, step_sizes, feature_values, inflow, readout):
    count = running.shape[1]
    position = jnp.arange(count)
    causal = (position[:, None] >= position[None, :])[None, :, :, None]
    log_gaps = jnp.where(causal, running[:, :, None, :] - running[:, None, :, :], 0.0)
    decays = jnp.where(causal, jnp.exp(log_gaps), 0.0)
    affinity = jnp.einsum("bsn,brn->bsr", readout, inflow)
    mixing = affinity[..., None] * decays * step_sizes[:, None, :, :]
    return jnp.einsum("bsrh,brhp->bshp", mixing, feature_values)


def select_state(limit, log_decay, running, step_sizes, feature_values, inflow, start_state):
    count = running.shape[1]
    alive = (jnp.arange(count)[None, :] < limit[:, None])[..., None]
    end_log = jnp.sum(jnp.where(alive, log_decay, 0.0), axis=1)
    weights = jnp.where(
        alive, jnp.exp(jnp.where(alive, end_log[:, None, :] - running, 0.0)) * step_sizes, 0.0
    )
    return jnp.exp(end_log)[..., None, None] * start_state + jnp.einsum(
        "brh,brhp,brn->bhpn", weights, feature_values, inflow
    )


def body(
    mamba_input,
    gate_input,
    in_b,
    in_c,
    step_size,
    decay_rate,
    skip_weight,
    norm_gain,
    ssm_state,
    out_weight,
    queries,
    draft_token_keys,
    draft_values,
    cached_key_rows,
    cache_values,
    cache_len,
    accepted,
):
    sequences, block_len, feature_width = mamba_input.shape
    head_count = decay_rate.shape[0]
    head_size = feature_width // head_count
    tok_count = lax.axis_size("tok")
    tok_index = lax.axis_index("tok")
    first_draft = tok_index * block_len
    feature_values = mamba_input.astype(jnp.float32).reshape(
        sequences, block_len, head_count, head_size
    )
    inflow_cols, readout_cols = in_one_piece((in_b, in_c), "tok", 2, 1, 0)
    all_inputs, all_steps = sent_together((mamba_input, step_size), "tok", 1, 2)
    draft_len = all_inputs.shape[1]
    all_features = all_inputs.astype(jnp.float32).reshape(
        sequences, draft_len, head_count, head_size
    )
    step_sizes = all_steps.astype(jnp.float32)
    inflow = inflow_cols.astype(jnp.float32)
    readout = readout_cols.astype(jnp.float32)
    log_decay = -step_sizes * decay_rate[None, None, :]
    running = jnp.cumsum(log_decay, axis=1)
    within = within_block(running, step_sizes, all_features, inflow, readout)
    start_state = ssm_state.astype(jnp.float32)
    carried = jnp.einsum("bsn,bhpn->bshp", readout, start_state) * jnp.exp(running)[..., None]
    partial_sum = (within + carried).reshape(sequences, draft_len, feature_width)
    mixed = summed_on_arrival(partial_sum.astype(jnp.bfloat16), "tok", 1).reshape(
        sequences, block_len, head_count, head_size
    )
    chosen = select_state(
        accepted, log_decay, running, step_sizes, all_features, inflow, start_state
    )
    committed_state = chosen.astype(jnp.bfloat16)
    mixed = mixed + skip_weight[None, None, :, None] * feature_values
    gated = mixed.reshape(sequences, block_len, feature_width) * jax.nn.silu(
        gate_input.astype(jnp.float32)
    )
    mean_sq = jnp.mean(gated * gated, axis=-1, keepdims=True)
    normed = (gated * lax.rsqrt(mean_sq + EPSILON) * norm_gain).astype(jnp.bfloat16)
    regrouped = lax.all_to_all(normed, "tok", split_axis=2, concat_axis=1, tiled=True)
    mamba_out = summed_on_arrival(
        jnp.einsum("sdf,fo->dso", regrouped, out_weight, preferred_element_type=jnp.float32).astype(
            jnp.bfloat16
        ),
        ("head", "tok"),
        0,
    ).astype(jnp.bfloat16)
    all_queries = gather_directly(queries, "tok", 1)
    att_size = draft_token_keys.shape[2]
    per_kv = queries.shape[2] // att_size
    draft_len = all_queries.shape[1]
    cache_block = cached_key_rows.shape[1]
    query_matrix = all_queries.reshape(sequences, draft_len * per_kv, att_size)
    score_scale = att_size ** (-0.5)
    cache_scores = (
        jnp.einsum(
            "cmq,czq->cmz", query_matrix, cached_key_rows, preferred_element_type=jnp.float32
        )
        * score_scale
    )
    draft_scores = (
        jnp.einsum(
            "cmq,czq->cmz", query_matrix, draft_token_keys, preferred_element_type=jnp.float32
        )
        * score_scale
    )
    cache_pos = tok_index * cache_block + jnp.arange(cache_block)
    cache_valid = cache_pos[None, None, :] < cache_len[:, None, None]
    query_pos = jnp.repeat(jnp.arange(draft_len), per_kv)
    draft_valid = ((first_draft + jnp.arange(block_len))[None, :] <= query_pos[:, None])[None, :, :]
    cache_scores = jnp.where(cache_valid, cache_scores, MASKED)
    draft_scores = jnp.where(draft_valid, draft_scores, MASKED)
    row_peak = jnp.maximum(jnp.max(cache_scores, axis=-1), jnp.max(draft_scores, axis=-1))
    cache_probs = jnp.where(cache_valid, jnp.exp(cache_scores - row_peak[..., None]), 0.0)
    draft_probs = jnp.where(draft_valid, jnp.exp(draft_scores - row_peak[..., None]), 0.0)
    row_total = jnp.sum(cache_probs, axis=-1) + jnp.sum(draft_probs, axis=-1)
    numer = jnp.einsum(
        "ces,csx->cex",
        cache_probs.astype(jnp.bfloat16),
        cache_values,
        preferred_element_type=jnp.float32,
    )
    numer = numer + jnp.einsum(
        "ces,csx->cex",
        draft_probs.astype(jnp.bfloat16),
        draft_values,
        preferred_element_type=jnp.float32,
    )
    peaks, totals, numers = tuple(
        (
            part.astype(jnp.float32)
            for part in in_one_piece(
                (
                    row_peak.reshape(1, sequences, draft_len, per_kv).astype(jnp.bfloat16),
                    row_total.reshape(1, sequences, draft_len, per_kv).astype(jnp.bfloat16),
                    numer.reshape(1, sequences, draft_len, per_kv * att_size).astype(jnp.bfloat16),
                ),
                "tok",
                2,
                0,
                3,
            )
        )
    )
    overall = jnp.max(peaks, axis=0)
    rescale = jnp.exp(peaks - overall[None])
    denominator = jnp.sum(rescale * totals, axis=0)
    numers = numers.reshape(tok_count, sequences, block_len, per_kv, att_size)
    context = jnp.sum(rescale[..., None] * numers, axis=0) / denominator[..., None]
    attn_context = context.reshape(sequences, block_len, per_kv * att_size).astype(jnp.bfloat16)
    return (mamba_out, attn_context, committed_state)


def solution(mesh):
    in_specs = (
        P("dp", "tok", "head"),
        P("dp", "tok", "head"),
        P("dp", "tok", "head"),
        P("dp", "tok", "head"),
        P("dp", "tok", "head"),
        P("head"),
        P("head"),
        P("head"),
        P("dp", "head", None, "tok"),
        P(("head", "tok"), None),
        P("dp", "tok", "head"),
        P("dp", "tok", "head"),
        P("dp", "tok", "head"),
        P("dp", "tok", "head"),
        P("dp", "tok", "head"),
        P("dp"),
        P("dp"),
    )
    out_specs = (
        P(("head", "tok"), "dp", None),
        P("dp", "tok", "head"),
        P("dp", "head", None, "tok"),
    )
    return jax.shard_map(body, mesh=mesh, in_specs=in_specs, out_specs=out_specs, check_vma=False)
```

profile of v0, /device:TPU:2, one launch (start us, length us, event | category | flops | bytes accessed | tf_op | source)
XLA Modules:
  0.0 98.2 jit_solution(13853714180560108559)
XLA Ops:
  0.7 0.9 pad_maximum_fusion.2
  1.5 0.1 copy.76
  1.7 0.8 reshape.233
  2.4 9.1 %all-to-all-start = ((bf16[4,2,1024]{2,1,0:T(2,128)(2,1)}), bf16[4,2,1024]{2,1,0:T(2,128)(2,1)S(1)}, u32[]{:S(2)}, u32[]{:S(2)}) async-start(bf16[4,2,1024]{2,1,0:T(2,128)(2,1)} %reshape.233), calls=%async_computation | async-start | bytes 32768 | tf_op jit(solution)/shard_map/all_to_all | solution.py:13
  11.6 0.1 le.20
  11.7 0.9 pad_maximum_fusion.1
  12.6 12.3 %all_gather.3 = bf16[2,64,1040]{2,1,0:T(8,128)(2,1)S(1)} all-gather(bf16[2,16,1040]{2,1,0:T(8,128)(2,1)S(1)} %pad_maximum_fusion.1), channel_id=1, replica_groups=mesh['dp'=16,'head'=8,'tok'=4] {'tok'}, dimensions={1}, use_global_device_ids=true | all-gather | bytes 332800 | tf_op jit(solution)/shard_map/all_gather | solution.py:20
  24.9 0.7 iota_compare_fusion.1
  25.6 0.7 broadcast_compare_fusion.1
  26.3 0.1 broadcast_compare_fusion
  26.4 0.8 select_reduce_fusion
  27.2 0.1 reduce_window_sum.11
  27.3 0.1 multiply_select_fusion.1
  27.5 0.3 copy.75
  27.9 0.1 mul.122
  28.0 0.1 mul.123
  28.1 0.7 broadcast_in_dim.109
  28.7 4.5 %all-to-all-start.4 = ((bf16[4,2,16,512]{3,2,1,0:T(8,128)(2,1)}), bf16[4,2,16,512]{3,2,1,0:T(8,128)(2,1)S(1)}, u32[]{:S(2)}, u32[]{:S(2)}) async-start(bf16[4,2,16,512]{3,2,1,0:T(8,128)(2,1)} %broadcast_in_dim.109), calls=%async_computation.4 | async-start | bytes 262144 | tf_op jit(solution)/shard_map/all_to_all | solution.py:37
  33.2 0.1 reshape.234
  33.4 0.1 copy.77
  33.5 0.1 fusion.50
  33.7 0.5 convolution_bitcast_fusion
  34.2 1.3 %fusion.6 = bf16[2,64,16,64]{1,3,2,0:T(8,128)(2,1)S(1)} fusion(f32[2,64,16,64]{1,3,2,0:T(8,128)S(1)} %convolution_bitcast_fusion, bf16[2,64,32,1]{2,1,3,0:T(8,128)(2,1)S(1)} %bitcast.67, bf16[2,16,64,32]{2,3,1,0:T(8,128)(2,1)} %param.25, f32[2,64,16]{1,2,0:T(8,128)S(1)} %copy.84), kind=kOutput, calls=%fused_computation.11 | convolution fusion | flops 8781824 | bytes 933888 | tf_op jit(solution)/shard_map/bsn,bhpn->bshp/dot_general | solution.py:115
  35.5 0.4 copy.86
  35.9 0.3 convert_element_type.101
  36.3 0.7 copy.87
  37.0 1.2 %all-to-all-done.4 = bf16[4,2,16,512]{3,2,1,0:T(8,128)(2,1)S(1)} async-done(((bf16[4,2,16,512]{3,2,1,0:T(8,128)(2,1)}), bf16[4,2,16,512]{3,2,1,0:T(8,128)(2,1)S(1)}, u32[]{:S(2)}, u32[]{:S(2)}) %all-to-all-start.4) | async-done | bytes 131104 | tf_op jit(solution)/shard_map/all_to_all | solution.py:37
  38.2 4.8 %all-to-all-start.1 = ((bf16[4,2,16,1024]{3,2,1,0:T(8,128)(2,1)}), bf16[4,2,16,1024]{3,2,1,0:T(8,128)(2,1)S(1)}, u32[]{:S(2)}, u32[]{:S(2)}) async-start(bf16[4,2,16,1024]{3,2,1,0:T(8,128)(2,1)} %copy.87), calls=%async_computation.1 | async-start | bytes 524288 | tf_op jit(solution)/shard_map/all_to_all | solution.py:31
  43.0 0.1 reshape_reshape.3
  43.1 1.6 %fusion.2 = (f32[2,256]{1,0:T(2,128)S(1)}, f32[2,256,1024]{2,1,0:T(8,128)S(1)}) fusion(pred[2,1024]{1,0:T(4,128)(4,1)S(1)} %broadcast_compare_fusion.1, bf16[2,256,128]{2,1,0:T(8,128)(2,1)S(1)} %reshape_reshape.3, bf16[2,1024,128]{2,1,0:T(8,128)(2,1)} %param.30), kind=kOutput, calls=%fused_computation.5 | convolution fusion | flops 135790080 | bytes 2756608 | tf_op jit(solution)/shard_map/cmq,czq->cmz/dot_general | solution.py:146
  44.8 0.2 fusion.49
  45.0 0.2 fusion.36
  45.3 0.6 fusion.4
  45.9 0.7 fusion.8
  46.6 0.1 convert_element_type.115
  46.7 0.1 copy.95
  46.9 0.1 convert_element_type.111
  47.0 0.1 convert_element_type.109
  47.2 1.4 %all-to-all-done.1 = bf16[4,2,16,1024]{3,2,1,0:T(8,128)(2,1)S(1)} async-done(((bf16[4,2,16,1024]{3,2,1,0:T(8,128)(2,1)}), bf16[4,2,16,1024]{3,2,1,0:T(8,128)(2,1)S(1)}, u32[]{:S(2)}, u32[]{:S(2)}) %all-to-all-start.1) | async-done | bytes 262176 | tf_op jit(solution)/shard_map/all_to_all | solution.py:31
  48.7 0.1 multiply_reduce_fusion.1
  48.8 0.1 multiply_convert_fusion
  48.9 0.4 copy.88
  49.3 1.2 %reshape.235 = bf16[4,2,4096]{2,1,0:T(2,128)(2,1)} reshape(bf16[1024,2,16]{2,1,0:T(2,128)(2,1)S(1)} %bitcast.55) | data formatting | bytes 131072
  50.5 4.7 %all-to-all-start.2 = ((bf16[4,2,4096]{2,1,0:T(2,128)(2,1)}), bf16[4,2,4096]{2,1,0:T(2,128)(2,1)S(1)}, u32[]{:S(2)}, u32[]{:S(2)}) async-start(bf16[4,2,4096]{2,1,0:T(2,128)(2,1)} %reshape.235), calls=%async_computation.2 | async-start | bytes 131072 | tf_op jit(solution)/shard_map/all_to_all | solution.py:130
  55.2 1.1 %pad_maximum_fusion = bf16[1,2,64,520]{3,1,0,2:T(2,128)(2,1)} fusion(bf16[1,2,64,512]{3,1,0,2:T(2,128)(2,1)S(1)} %copy.95, bf16[1,2,64,4]{3,1,0,2:T(2,128)(2,1)S(1)} %copy.94, bf16[1,2,64,4]{3,1,0,2:T(2,128)(2,1)S(1)} %copy.93), kind=kLoop, calls=%fused_computation.41 | loop fusion | flops 399360 | bytes 266240 | tf_op jit(solution)/shard_map/concatenate | solution.py:12
  56.2 3.1 %all-to-all-done.2 = bf16[4,2,4096]{2,1,0:T(2,128)(2,1)S(1)} async-done(((bf16[4,2,4096]{2,1,0:T(2,128)(2,1)}), bf16[4,2,4096]{2,1,0:T(2,128)(2,1)S(1)}, u32[]{:S(2)}, u32[]{:S(2)}) %all-to-all-start.2) | async-done | bytes 65568 | tf_op jit(solution)/shard_map/all_to_all | solution.py:130
  59.3 4.8 %all-to-all-start.5 = ((bf16[1,2,64,520]{3,1,0,2:T(2,128)(2,1)}), bf16[1,2,64,520]{3,1,0,2:T(2,128)(2,1)S(1)}, u32[]{:S(2)}, u32[]{:S(2)}) async-start(bf16[1,2,64,520]{3,1,0,2:T(2,128)(2,1)} %pad_maximum_fusion), calls=%async_computation.5 | async-start | bytes 327680 | tf_op jit(solution)/shard_map/all_to_all | solution.py:13
  64.1 0.4 reshape.236
  64.5 0.3 copy.89
  64.8 0.4 fusion
  65.3 1.5 %reshape.230 = bf16[32,2,2,4096]{3,1,0,2:T(2,128)(2,1)} reshape(bf16[64,2,4096]{2,0,1:T(8,128)(2,1)S(1)} %fusion) | data formatting | bytes 2097152 | tf_op jit(solution)/shard_map/reshape | solution.py:26
  66.8 3.4 %copy.90 = bf16[32,2,2,4096]{3,1,2,0:T(2,128)(2,1)} copy(bf16[32,2,2,4096]{3,1,0,2:T(2,128)(2,1)} %reshape.230) | data formatting | bytes 2097152 | tf_op jit(solution)/shard_map/reshape | solution.py:26
  70.2 5.5 %all-to-all-start.3 = ((bf16[32,2,2,4096]{3,1,2,0:T(2,128)(2,1)}), bf16[32,2,2,4096]{3,1,2,0:T(2,128)(2,1)S(1)}, u32[]{:S(2)}, u32[]{:S(2)}) async-start(bf16[32,2,2,4096]{3,1,2,0:T(2,128)(2,1)} %copy.90), calls=%async_computation.3 | async-start | bytes 2097152 | tf_op jit(solution)/shard_map/all_to_all | solution.py:31
  75.8 0.1 copy.96
  75.8 2.2 %fusion.7 = bf16[2,16,64,32]{2,3,1,0:T(8,128)(2,1)} fusion(bf16[2,64,16,64]{1,3,2,0:T(8,128)(2,1)} %bitcast.62, bf16[2,16,64,32]{2,3,1,0:T(8,128)(2,1)} %param.25, f32[2,64,16]{1,2,0:T(8,128)S(1)} %copy.97, f32[2,64,32]{1,2,0:T(8,128)S(1)} %copy.96, f32[2,16]{1,0:T(2,128)S(1)} %exp.39), kind=kOutput, calls=%fused_computation.13 | convolution fusion | flops 8716288 | bytes 548992 | tf_op jit(solution)/shard_map/brh,brhp,brn->bhpn/dot_general | solution.py:69
  78.1 0.1 multiply_reduce_fusion.2
  78.3 0.9 mul.139
  79.2 1.1 %mul.140 = f32[4,2,16,512]{3,1,2,0:T(2,128)S(1)} reshape(f32[4,2,16,4,128]{4,3,1,2,0:T(4,128)} %mul.139) | data formatting | bytes 524288 | tf_op jit(solution)/shard_map/mul | solution.py:199
  80.3 0.1 div.24
  80.5 1.2 %multiply_reduce_fusion = f32[2,16,512]{2,0,1:T(2,128)S(1)} fusion(f32[4,2,16,512]{3,1,2,0:T(2,128)S(1)} %mul.140, bf16[4,2,16,520]{3,1,2,0:T(2,128)(2,1)} %bitcast.60), kind=kLoop, calls=%fused_computation.38 | loop fusion | flops 180224 | bytes 458752 | tf_op jit(solution)/shard_map/reduce_sum | solution.py:199
  81.8 0.6 copy.100
  82.4 14.1 %all-to-all-done.3 = bf16[32,2,2,4096]{3,1,2,0:T(2,128)(2,1)S(1)} async-done(((bf16[32,2,2,4096]{3,1,2,0:T(2,128)(2,1)}), bf16[32,2,2,4096]{3,1,2,0:T(2,128)(2,1)S(1)}, u32[]{:S(2)}, u32[]{:S(2)}) %all-to-all-start.3) | async-done | bytes 1048608 | tf_op jit(solution)/shard_map/all_to_all | solution.py:31
  96.5 1.0 %reduce_sum.77 = bf16[2,2,4096]{2,0,1:T(2,128)(2,1)S(1)} reduce(bf16[32,2,2,4096]{3,1,2,0:T(2,128)(2,1)S(1)} %all-to-all-done.3, bf16[]{:T(256)} %constant.10.clone.1), dimensions={0}, to_apply=%region_3.4 | reduce | flops 507904 | bytes 1081346 | tf_op jit(solution)/shard_map/reduce_sum | solution.py:32
  97.5 0.7 copy.99
  (49 shorter events, 0.7 us)
Async XLA Ops:
  0.6 64.2 %copy-start = (bf16[256,4096]{1,0:T(8,128)(2,1)S(1)}, bf16[256,4096]{1,0:T(8,128)(2,1)}, u32[]{:S(2)}) copy-start(bf16[256,4096]{1,0:T(8,128)(2,1)} %param.26) | copy-start | bytes 6291460
  0.6 27.3 %copy-start.9 = (f32[16]{0:T(128)S(1)}, f32[16]{0:T(128)}, u32[]{:S(2)}) copy-start(f32[16]{0:T(128)} %param.23) | copy-start | bytes 196
  0.7 27.4 %copy-start.5 = (bf16[2,16,512]{2,1,0:T(8,128)(2,1)S(1)}, bf16[2,16,512]{2,1,0:T(8,128)(2,1)}, u32[]{:S(2)}) copy-start(bf16[2,16,512]{2,1,0:T(8,128)(2,1)} %param.27) | copy-start | bytes 98308
  2.4 25.6 %all-to-all-start = ((bf16[4,2,1024]{2,1,0:T(2,128)(2,1)}), bf16[4,2,1024]{2,1,0:T(2,128)(2,1)S(1)}, u32[]{:S(2)}, u32[]{:S(2)}) async-start(bf16[4,2,1024]{2,1,0:T(2,128)(2,1)} %reshape.233), calls=%async_computation | async-start | bytes 32768 | tf_op jit(solution)/shard_map/all_to_all | solution.py:13
  27.8 6.4 %copy-start.2 = (bf16[2,64,1024]{1,2,0:T(8,128)(2,1)}, bf16[2,64,1024]{1,2,0:T(8,128)(2,1)S(1)}, u32[]{:S(2)}) copy-start(bf16[2,64,1024]{1,2,0:T(8,128)(2,1)S(1)} %copy.75) | copy-start | bytes 786436
  28.7 9.5 %all-to-all-start.4 = ((bf16[4,2,16,512]{3,2,1,0:T(8,128)(2,1)}), bf16[4,2,16,512]{3,2,1,0:T(8,128)(2,1)S(1)}, u32[]{:S(2)}, u32[]{:S(2)}) async-start(bf16[4,2,16,512]{3,2,1,0:T(8,128)(2,1)} %broadcast_in_dim.109), calls=%async_computation.4 | async-start | bytes 262144 | tf_op jit(solution)/shard_map/all_to_all | solution.py:37
  36.3 8.5 %copy-start.6 = (bf16[2,16,128]{2,1,0:T(8,128)(2,1)S(1)}, bf16[2,16,128]{2,1,0:T(8,128)(2,1)}, u32[]{:S(2)}) copy-start(bf16[2,16,128]{2,1,0:T(8,128)(2,1)} %param.28) | copy-start | bytes 24580
  37.0 8.0 %copy-start.7 = (bf16[2,16,128]{2,1,0:T(8,128)(2,1)S(1)}, bf16[2,16,128]{2,1,0:T(8,128)(2,1)}, u32[]{:S(2)}) copy-start(bf16[2,16,128]{2,1,0:T(8,128)(2,1)} %param.29) | copy-start | bytes 24580
  38.2 10.4 %all-to-all-start.1 = ((bf16[4,2,16,1024]{3,2,1,0:T(8,128)(2,1)}), bf16[4,2,16,1024]{3,2,1,0:T(8,128)(2,1)S(1)}, u32[]{:S(2)}, u32[]{:S(2)}) async-start(bf16[4,2,16,1024]{3,2,1,0:T(8,128)(2,1)} %copy.87), calls=%async_computation.1 | async-start | bytes 524288 | tf_op jit(solution)/shard_map/all_to_all | solution.py:31
  43.1 2.8 %copy-start.10 = (bf16[2,1024,128]{2,1,0:T(8,128)(2,1)S(1)}, bf16[2,1024,128]{2,1,0:T(8,128)(2,1)}, u32[]{:S(2)}) copy-start(bf16[2,1024,128]{2,1,0:T(8,128)(2,1)} %param.31) | copy-start | bytes 1572868
  45.9 2.8 %copy-start.3 = (bf16[2,16,1024]{2,1,0:T(8,128)(2,1)S(1)}, bf16[2,16,1024]{2,1,0:T(8,128)(2,1)}, u32[]{:S(2)}) copy-start(bf16[2,16,1024]{2,1,0:T(8,128)(2,1)} %param.17) | copy-start | bytes 196612
  45.9 2.8 %copy-start.4 = (bf16[2,16,1024]{2,1,0:T(8,128)(2,1)S(1)}, bf16[2,16,1024]{2,1,0:T(8,128)(2,1)}, u32[]{:S(2)}) copy-start(bf16[2,16,1024]{2,1,0:T(8,128)(2,1)} %param.18) | copy-start | bytes 196612
  45.9 2.9 %copy-start.8 = (f32[1024]{0:T(1024)S(1)}, f32[1024]{0:T(1024)}, u32[]{:S(2)}) copy-start(f32[1024]{0:T(1024)} %param.24) | copy-start | bytes 12292
  50.5 8.9 %all-to-all-start.2 = ((bf16[4,2,4096]{2,1,0:T(2,128)(2,1)}), bf16[4,2,4096]{2,1,0:T(2,128)(2,1)S(1)}, u32[]{:S(2)}, u32[]{:S(2)}) async-start(bf16[4,2,4096]{2,1,0:T(2,128)(2,1)} %reshape.235), calls=%async_computation.2 | async-start | bytes 131072 | tf_op jit(solution)/shard_map/all_to_all | solution.py:130
  59.3 10.8 %all-to-all-start.5 = ((bf16[1,2,64,520]{3,1,0,2:T(2,128)(2,1)}), bf16[1,2,64,520]{3,1,0,2:T(2,128)(2,1)S(1)}, u32[]{:S(2)}, u32[]{:S(2)}) async-start(bf16[1,2,64,520]{3,1,0,2:T(2,128)(2,1)} %pad_maximum_fusion), calls=%async_computation.5 | async-start | bytes 327680 | tf_op jit(solution)/shard_map/all_to_all | solution.py:13
  70.2 8.1 %copy-start.1 = (bf16[1,2,64,520]{3,1,0,2:T(2,128)(2,1)}, bf16[1,2,64,520]{3,1,0,2:T(2,128)(2,1)S(1)}, u32[]{:S(2)}) copy-start(bf16[1,2,64,520]{3,1,0,2:T(2,128)(2,1)S(1)} %all-to-all-done.5) | copy-start | bytes 399364
  70.2 26.3 %all-to-all-start.3 = ((bf16[32,2,2,4096]{3,1,2,0:T(2,128)(2,1)}), bf16[32,2,2,4096]{3,1,2,0:T(2,128)(2,1)S(1)}, u32[]{:S(2)}, u32[]{:S(2)}) async-start(bf16[32,2,2,4096]{3,1,2,0:T(2,128)(2,1)} %copy.90), calls=%async_computation.3 | async-start | bytes 2097152 | tf_op jit(solution)/shard_map/all_to_all | solution.py:31
where the time goes:
time: 99.1 us; the launch traced here: 98.2 us
  starting transfers between devices  33.4 us (34%)
  waiting for transfers between devices  19.8 us (20%)
  local copies, waits for them, and re-layouts  15.6 us (16%)
  blocking collectives  12.3 us (12%)
  other arithmetic  8.71 us (9%)
  matrix products  7.29 us (7%)
  between operations  1.06 us (1%)
    all_to_all x2, waiting for transfers between devices, summed_on_arrival(): lax.all_to_all(parts, axis, split_axis=0, concat_axis=0, tiled=True)  15.5 us
    all_to_all x2, starting transfers between devices, in_one_piece(): lax.all_to_all(both, axis, split_axis=split_dim, concat_axis=concat_dim,...  13.9 us
    all_gather x1, blocking collectives, sent_together(): filled = lax.all_gather(both, axis, axis=dim, tiled=True)  12.3 us
    all_to_all x2, starting transfers between devices, summed_on_arrival(): lax.all_to_all(parts, axis, split_axis=0, concat_axis=0, tiled=True)  10.3 us
    reshape x2, local copies, waits for them, and re-layouts, in_blocks(): return jnp.moveaxis(array.reshape(*before, count, -1, *after), dim, 0)  4.9 us
    all_to_all x1, starting transfers between devices, body(): lax.all_to_all(normed, 'tok', split_axis=2, concat_axis=1, tiled=True)  4.71 us
    all_to_all x1, starting transfers between devices, from_everyone(): return lax.all_to_all(copies, axis, split_axis=0, concat_axis=0, tiled=True)  4.5 us
    unnamed x28, local copies, waits for them, and re-layouts  3.78 us
  transfers between devices with their start and end apart: 6, of which 4 were waited for; matrix products, arithmetic and copies ran while one was open for 26% of the time, Pallas kernels for 0%

commit v1 on v0

v1 whole, which is shorter than its diff:
```python
import functools

import jax
import jax.numpy as jnp
from jax import lax
from jax.experimental import pallas as pl
from jax.experimental.pallas import tpu as pltpu
from jax.sharding import PartitionSpec as P

EPSILON = 1e-05
MASKED = -1e30
FLOOR = -1e20
INTERPRET = False

F32 = jnp.float32
BF16 = jnp.bfloat16

X_ROW = 0
Z_ROW = 64
B_ROW = 128
C_ROW = 160
Q_ROW = 192
S_ROW = 320
T_ROW = 448
ROWS = 480

N_ROW = 0
M_ROW = 128
H_ROW = 256
BACK_ROWS = 384

HALF = 2048
WIDTH = HALF + 128


def dot(a, b):
    return jnp.dot(a, b, preferred_element_type=F32)


def dot_t(a, b):
    return lax.dot_general(a, b, (((1,), (1,)), ((), ())), preferred_element_type=F32)


def iota(shape, dim):
    return lax.broadcasted_iota(jnp.int32, shape, dim)


def pack_kernel(x_ref, z_ref, b_ref, c_ref, t_ref, s_ref, q_ref, out_ref):
    for seq in range(2):
        bs = b_ref[seq]
        cs = c_ref[seq]
        steps = t_ref[seq]
        for to in range(4):
            for block in range(2):
                lanes = pl.ds(to * 256 + block * 128, 128)
                row = (seq * 2 + block) * 16
                out_ref[to, pl.ds(X_ROW + row, 16), :] = x_ref[seq, :, lanes]
                out_ref[to, pl.ds(Z_ROW + row, 16), :] = z_ref[seq, :, lanes]
                head = to * 4 + block * 2
                pair = jnp.concatenate([s_ref[seq, head], s_ref[seq, head + 1]], axis=1)
                out_ref[to, pl.ds(S_ROW + (seq * 2 + block) * 32, 32), :] = pair
            out_ref[to, pl.ds(B_ROW + seq * 16, 16), :] = bs
            out_ref[to, pl.ds(C_ROW + seq * 16, 16), :] = cs
            for head in range(4):
                row = Q_ROW + (seq * 4 + head) * 16
                out_ref[to, pl.ds(row, 16), :] = q_ref[seq, :, pl.ds(head * 128, 128)]
            own = steps[:, to * 4 : to * 4 + 4].astype(F32)
            own = jnp.concatenate([own, jnp.zeros((16, 124), F32)], axis=1)
            out_ref[to, pl.ds(T_ROW + seq * 16, 16), :] = own.astype(BF16)


def both(in_ref, first, stride):
    return jnp.concatenate(
        [in_ref[src, pl.ds(first + seq * stride, 16), :] for seq in range(2) for src in range(4)],
        axis=0,
    )


def mixer_kernel(
    in_ref, w_ref, rate_ref, skip_ref, gain_ref, out_ref, run_ref, w_buf, sem
):
    fetch = pltpu.make_async_copy(w_ref, w_buf, sem)
    fetch.start()
    row = iota((128, 128), 0)
    col = iota((128, 128), 1)
    low = col < 64
    causal = (row >= col) & ((row >= 64) == (col >= 64))
    ones = jnp.where(causal, 1.0, 0.0).astype(BF16)
    steps = both(in_ref, T_ROW, 16)
    total = dot(ones, steps)
    rate = rate_ref[...]
    run = -total * rate
    run_ref[...] = run
    run_t = run.T
    steps_t = steps.astype(F32).T
    grow = jnp.exp(run)
    inflow = both(in_ref, B_ROW, 16)
    readout = both(in_ref, C_ROW, 16)
    affinity = dot_t(readout, inflow)
    squares = jnp.zeros((128, 1), F32)
    parts = []
    for block in range(2):
        x = both(in_ref, X_ROW + block * 16, 32)
        z = both(in_ref, Z_ROW + block * 16, 32).astype(F32)
        mixed = []
        for half in range(2):
            head = block * 2 + half
            gap = jnp.where(causal, run[:, head : head + 1] - run_t[head : head + 1, :], 0.0)
            mixing = jnp.where(
                causal, jnp.exp(gap) * steps_t[head : head + 1, :] * affinity, 0.0
            )
            mixed.append(dot(mixing.astype(BF16), x))
        y = jnp.where(low, mixed[0], mixed[1])
        carried = []
        for seq in range(2):
            state = jnp.concatenate(
                [
                    in_ref[src, pl.ds(S_ROW + (seq * 2 + block) * 32, 32), :]
                    for src in range(4)
                ],
                axis=0,
            )
            carried.append(dot(readout[seq * 64 : seq * 64 + 64], state))
        factor = jnp.where(
            low, grow[:, 2 * block : 2 * block + 1], grow[:, 2 * block + 1 : 2 * block + 2]
        )
        lanes = pl.ds(block * 128, 128)
        y = y + jnp.concatenate(carried, axis=0) * factor + skip_ref[:, lanes] * x.astype(F32)
        gated = y * (z / (1.0 + jnp.exp(-z)))
        squares = squares + jnp.sum(gated * gated, axis=1, keepdims=True)
        parts.append((gated * gain_ref[:, lanes]).astype(BF16))
    act = jnp.concatenate(parts, axis=1)
    first = jnp.where(col == (row % 2) * 64 + row // 2, 1.0, 0.0).astype(BF16)
    other = (row // 8) * 8 + (row + 4) % 8
    second = jnp.where(col == (other % 2) * 64 + other // 2, 1.0, 0.0).astype(BF16)
    lhs_a = dot(first, act).astype(BF16)
    lhs_b = dot(second, act).astype(BF16)
    squares = jnp.broadcast_to(squares, (128, 128)).astype(BF16)

    def store(a, b, lanes, width):
        a = a.reshape(16, 8, width)
        b = b.reshape(16, 8, width)
        upper = iota((16, 8, width), 1) < 4
        even = jnp.where(upper, a, b)
        odd = jnp.where(upper, b, a)
        out_ref[:, :, lanes] = jnp.stack([even, odd], axis=1).reshape(32, 8, width).astype(BF16)

    store(dot(first, squares), dot(second, squares), pl.ds(HALF, 128), 128)
    fetch.wait()
    for chunk in range(8):
        lanes = pl.ds(chunk * 256, 256)
        a = dot(lhs_a, w_buf[:, lanes])
        b = dot(lhs_b, w_buf[:, pl.ds(HALF + chunk * 256, 256)])
        store(a, b, lanes, 256)


def attend_kernel(
    where_ref, len_ref, acc_ref, in_ref, run_ref, rate_ref, k_ref, v_ref, dk_ref, dv_ref, out_ref
):
    tok = where_ref[0]
    scale = 128 ** (-0.5)
    cache = k_ref.shape[1]
    for seq in range(2):
        queries = jnp.concatenate(
            [in_ref[src, pl.ds(Q_ROW + seq * 64, 64), :] for src in range(4)], axis=0
        )
        old = dot_t(queries, k_ref[seq]) * scale
        new = dot_t(queries, dk_ref[seq]) * scale
        limit = len_ref[seq] - tok * cache
        old = jnp.where(iota(old.shape, 1) < limit, old, MASKED)
        line = iota(new.shape, 0)
        draft = (line // 64) * 16 + line % 16
        new = jnp.where(iota(new.shape, 1) + tok * 16 <= draft, new, MASKED)
        peak = jnp.maximum(
            jnp.max(old, axis=1, keepdims=True), jnp.max(new, axis=1, keepdims=True)
        )
        peak = jnp.maximum(peak, FLOOR).astype(BF16).astype(F32)
        old = jnp.exp(old - peak)
        new = jnp.exp(new - peak)
        total = jnp.sum(old, axis=1, keepdims=True) + jnp.sum(new, axis=1, keepdims=True)
        numer = dot(old.astype(BF16), v_ref[seq]) + dot(new.astype(BF16), dv_ref[seq])
        numer = numer.astype(BF16)
        stats = jnp.where(iota((256, 128), 1) < 64, peak, total).astype(BF16)
        for to in range(4):
            out_ref[to, pl.ds(N_ROW + seq * 64, 64), :] = numer[to * 64 : to * 64 + 64]
            out_ref[to, pl.ds(M_ROW + seq * 64, 64), :] = stats[to * 64 : to * 64 + 64]

    row = iota((128, 128), 0)
    low = iota((128, 128), 1) < 64
    low_row = iota((1, 128), 1) < 64
    steps = both(in_ref, T_ROW, 16).astype(F32)
    inflow_t = both(in_ref, B_ROW, 16).astype(F32).T.astype(BF16)
    run = run_ref[...]
    rate = rate_ref[...]
    for seq in range(2):
        alive = (row >= seq * 64) & (row < seq * 64 + acc_ref[seq])
        end = -jnp.sum(jnp.where(alive, steps, 0.0), axis=0, keepdims=True) * rate
        weights = jnp.where(alive, jnp.exp(jnp.where(alive, end - run, 0.0)) * steps, 0.0)
        keep = jnp.exp(end)
        for block in range(2):
            first, second = 2 * block, 2 * block + 1
            x = both(in_ref, X_ROW + block * 16, 32).astype(F32)
            factor = jnp.where(
                low, weights[:, first : first + 1], weights[:, second : second + 1]
            )
            added = dot(inflow_t, (x * factor).astype(BF16))
            decay = jnp.where(low_row, keep[:, first : first + 1], keep[:, second : second + 1])
            for src in range(4):
                at = (seq * 2 + block) * 32
                state = in_ref[src, pl.ds(S_ROW + at, 32), :].astype(F32)
                result = decay * state + added[src * 32 : src * 32 + 32]
                out_ref[src, pl.ds(H_ROW + at, 32), :] = result.astype(BF16)


def combine_kernel(in_ref, att_ref, state_ref):
    for seq in range(2):
        stats = [in_ref[src, pl.ds(M_ROW + seq * 64, 64), :].astype(F32) for src in range(4)]
        peaks = [s[:, 0:1] for s in stats]
        overall = functools.reduce(jnp.maximum, peaks)
        numer = jnp.zeros((64, 128), F32)
        denominator = jnp.zeros((64, 1), F32)
        for src in range(4):
            rescale = jnp.exp(peaks[src] - overall)
            denominator = denominator + rescale * stats[src][:, 64:65]
            part = in_ref[src, pl.ds(N_ROW + seq * 64, 64), :].astype(F32)
            numer = numer + rescale * part
        context = (numer / denominator).astype(BF16)
        for head in range(4):
            att_ref[seq, :, pl.ds(head * 128, 128)] = context[head * 16 : head * 16 + 16]
        for src in range(4):
            for block in range(2):
                pair = in_ref[src, pl.ds(H_ROW + (seq * 2 + block) * 32, 32), :]
                state_ref[seq, src * 4 + block * 2] = pair[:, :64]
                state_ref[seq, src * 4 + block * 2 + 1] = pair[:, 64:]


def sum_kernel(where_ref, in_ref, out_ref):
    squares = in_ref[:, :, pl.ds(HALF, 128)].astype(F32)
    squares = squares.reshape(8, 4, 8, 128).sum(axis=1)
    scale = lax.rsqrt(squares * (1.0 / 1024.0) + EPSILON)
    swapped = where_ref[0] % 2 == 1
    for chunk in range(HALF // 128):
        part = in_ref[:, :, pl.ds(chunk * 128, 128)].astype(F32)
        part = part.reshape(8, 4, 8, 128).sum(axis=1)
        total = (part * scale).sum(axis=0)
        flipped = jnp.concatenate([total[4:8], total[0:4]], axis=0)
        total = jnp.where(swapped, flipped, total).astype(BF16)
        for draft in range(2):
            for half in range(2):
                rows = total[half * 4 + draft * 2 : half * 4 + draft * 2 + 2]
                out_ref[draft, :, pl.ds(half * HALF + chunk * 128, 128)] = rows


def in_vmem(count):
    return [pl.BlockSpec(memory_space=pltpu.VMEM) for _ in range(count)]


def in_smem(count):
    return [pl.BlockSpec(memory_space=pltpu.SMEM) for _ in range(count)]


def call(kernel, ins, outs, cost, **kwargs):
    flops, moved = cost
    return pl.pallas_call(
        kernel,
        in_specs=ins,
        out_specs=tuple(in_vmem(len(outs))),
        out_shape=tuple(jax.ShapeDtypeStruct(s, d) for s, d in outs),
        cost_estimate=pl.CostEstimate(flops=flops, bytes_accessed=moved, transcendentals=0),
        interpret=INTERPRET,
        **kwargs,
    )


def body(
    mamba_input,
    gate_input,
    in_b,
    in_c,
    step_size,
    decay_rate,
    skip_weight,
    norm_gain,
    ssm_state,
    out_weight,
    queries,
    draft_token_keys,
    draft_values,
    cached_key_rows,
    cache_values,
    cache_len,
    accepted,
):
    tok = lax.axis_index("tok")
    where = tok.reshape(1).astype(jnp.int32)
    (packed,) = call(pack_kernel, in_vmem(7), [((4, ROWS, 128), BF16)], (0, 1500000))(
        mamba_input,
        gate_input,
        in_b,
        in_c,
        step_size,
        jnp.swapaxes(ssm_state, 2, 3),
        queries,
    )
    arrived = lax.all_to_all(packed, "tok", split_axis=0, concat_axis=0, tiled=True)
    rate = jnp.pad(lax.dynamic_slice(decay_rate, (tok * 4,), (4,)), (0, 124)).reshape(1, 128)
    skip = jnp.repeat(lax.dynamic_slice(skip_weight, (tok * 4,), (4,)), 64).reshape(1, 256)
    gain = lax.dynamic_slice(norm_gain, (tok * 256,), (256,)).reshape(1, 256)
    shares, run = call(
        mixer_kernel,
        in_vmem(1) + [pl.BlockSpec(memory_space=pl.ANY)] + in_vmem(3),
        [((32, 8, WIDTH), BF16), ((128, 128), F32)],
        (400000000, 4000000),
        scratch_shapes=[pltpu.VMEM((256, 4096), BF16), pltpu.SemaphoreType.DMA],
    )(arrived, out_weight, rate, skip, gain)
    landed = lax.all_to_all(shares, ("head", "tok"), split_axis=0, concat_axis=0, tiled=True)
    (back,) = call(
        attend_kernel, in_smem(3) + in_vmem(7), [((4, BACK_ROWS, 128), BF16)], (300000000, 3000000)
    )(
        where,
        cache_len,
        accepted,
        arrived,
        run,
        rate,
        cached_key_rows,
        cache_values,
        draft_token_keys,
        draft_values,
    )
    returned = lax.all_to_all(back, "tok", split_axis=0, concat_axis=0, tiled=True)
    attn_context, state_t = call(
        combine_kernel,
        in_vmem(1),
        [((2, 16, 512), BF16), ((2, 16, 32, 64), BF16)],
        (1000000, 1000000),
    )(returned)
    (mamba_out,) = call(
        sum_kernel, in_smem(1) + in_vmem(1), [((2, 2, 4096), BF16)], (1000000, 1500000)
    )(where, landed)
    return (mamba_out, attn_context, jnp.swapaxes(state_t, 2, 3))


def solution(mesh):
    in_specs = (
        P("dp", "tok", "head"),
        P("dp", "tok", "head"),
        P("dp", "tok", "head"),
        P("dp", "tok", "head"),
        P("dp", "tok", "head"),
        P("head"),
        P("head"),
        P("head"),
        P("dp", "head", None, "tok"),
        P(("head", "tok"), None),
        P("dp", "tok", "head"),
        P("dp", "tok", "head"),
        P("dp", "tok", "head"),
        P("dp", "tok", "head"),
        P("dp", "tok", "head"),
        P("dp"),
        P("dp"),
    )
    out_specs = (
        P(("head", "tok"), "dp", None),
        P("dp", "tok", "head"),
        P("dp", "head", None, "tok"),
    )
    return jax.shard_map(body, mesh=mesh, in_specs=in_specs, out_specs=out_specs, check_vma=False)
```

time: 99.1 us -> 75 us (0.76)
  the two profiles are of different devices: /device:TPU:2 before, /device:TPU:452 now
where the time goes in v1:
time: 75 us; the launch traced here: 74.4 us
  waiting for transfers between devices  28.3 us (38%)
  starting transfers between devices  15.4 us (21%)
  Pallas kernels  13.8 us (18%)
  blocking collectives  11.8 us (16%)
  local copies, waits for them, and re-layouts  4.52 us (6%)
    all_to_all x1, waiting for transfers between devices, body(): lax.all_to_all(shares, ('head', 'tok'), split_axis=0, concat_axis=0, tile...  24.8 us
    all_to_all x1, blocking collectives, body(): lax.all_to_all(back, 'tok', split_axis=0, concat_axis=0, tiled=True)  11.8 us
    all_to_all x1, starting transfers between devices, body(): lax.all_to_all(shares, ('head', 'tok'), split_axis=0, concat_axis=0, tile...  10.6 us
    all_to_all x1, starting transfers between devices, body(): lax.all_to_all(packed, 'tok', split_axis=0, concat_axis=0, tiled=True)  4.8 us
    pallas_call x1, Pallas kernels, body(): call(mixer_kernel, in_vmem(1) + [pl.BlockSpec(memory_space=pl.ANY)] + in_...  4.09 us
    pallas_call x1, Pallas kernels, body(): call(attend_kernel, in_smem(3) + in_vmem(7), [((4, BACK_ROWS, 128), BF16)...  3.69 us
    all_to_all x1, waiting for transfers between devices, body(): lax.all_to_all(packed, 'tok', split_axis=0, concat_axis=0, tiled=True)  3.44 us
    pallas_call x1, Pallas kernels, body(): call(combine_kernel, in_vmem(1), [((2, 16, 512), BF16), ((2, 16, 32, 64),...  2.06 us
  transfers between devices with their start and end apart: 2, of which 2 were waited for; matrix products, arithmetic and copies ran while one was open for 4% of the time, Pallas kernels for 3%

profile of v1, /device:TPU:452, one launch (start us, length us, event | category | flops | bytes accessed | tf_op | source)
XLA Modules:
  0.0 74.4 jit_solution(6794349277538001833)
XLA Ops:
  0.6 0.0 copy-start.2
  0.6 0.0 copy-start.3
  0.7 1.9 %shard_map.184 = bf16[4,480,128]{2,1,0:T(8,128)(2,1)} custom-call(bf16[2,16,1024]{2,1,0:T(8,128)(2,1)} %x_ref.1, bf16[2,16,1024]{2,1,0:T(8,128)(2,1)} %z_ref.1, bf16[2,16,128]{2,1,0:T(8,128)(2,1)} %b_ref.1, bf16[2,16,128]{2,1,0:T(8,128)(2,1)} %c_ref.1, bf16[2,16,16]{2,1,0:T(8,128)(2,1)} %t_ref.1, bf16[2,16,32,64]{3,2,1,0:T(8,128)(2,1)} %bitcast.6, ...), custom_call_target="tpu_custom_call" | custom-call | bytes 1500000 | tf_op jit(solution)/shard_map/pallas_call | solution.py:296
  2.6 4.8 %all-to-all-start = ((bf16[4,480,128]{2,1,0:T(8,128)(2,1)}), bf16[4,480,128]{2,1,0:T(8,128)(2,1)S(1)}, u32[]{:S(2)}, u32[]{:S(2)}) async-start(bf16[4,480,128]{2,1,0:T(8,128)(2,1)} %shard_map.184), calls=%async_computation | async-start | bytes 983040 | tf_op jit(solution)/shard_map/all_to_all | solution.py:305
  7.4 0.0 copy-done.2
  7.4 0.1 dynamic_slice.9
  7.4 0.0 copy-done.3
  7.4 0.1 dynamic_slice.10
  7.5 0.1 broadcast_in_dim.3
  7.6 0.6 reshape_reshape.3.skip_ref
  8.2 1.3 %dynamic_slice.11 = f32[256]{0:T(256)} dynamic-slice(f32[1024]{0:T(1024)} %param.24, s32[]{:T(128)S(6)} %select_n.8), dynamic_slice_sizes={256} | dynamic-slice | bytes 2052 | tf_op jit(solution)/shard_map/dynamic_slice | solution.py:308
  9.6 0.5 pad_bitcast_fusion.rate_ref
  10.1 3.4 %all-to-all-done.in_ref = bf16[4,480,128]{2,1,0:T(8,128)(2,1)S(1)} async-done(((bf16[4,480,128]{2,1,0:T(8,128)(2,1)}), bf16[4,480,128]{2,1,0:T(8,128)(2,1)S(1)}, u32[]{:S(2)}, u32[]{:S(2)}) %all-to-all-start) | async-done | bytes 491552 | tf_op jit(solution)/shard_map/all_to_all | solution.py:305
  13.5 0.0 copy-start.1
  13.5 0.8 %copy-done.1 = bf16[4,480,128]{2,1,0:T(8,128)(2,1)} copy-done((bf16[4,480,128]{2,1,0:T(8,128)(2,1)}, bf16[4,480,128]{2,1,0:T(8,128)(2,1)S(1)}, u32[]{:S(2)}) %copy-start.1) | copy-done | bytes 491544
  14.3 4.1 %shard_map.185 = (bf16[32,8,2176]{2,1,0:T(8,128)(2,1)}, f32[128,128]{1,0:T(8,128)}) custom-call(bf16[4,480,128]{2,1,0:T(8,128)(2,1)} %copy-done.1, bf16[256,4096]{1,0:T(8,128)(2,1)} %w_ref.1, f32[1,128]{1,0:T(1,128)} %pad_bitcast_fusion.rate_ref, f32[1,256]{1,0:T(1,128)} %reshape_reshape.3.skip_ref, f32[1,256]{1,0:T(1,128)} %bitcast.7), custom_call_target="tpu_custom_call" | custom-call | flops 400000000 | bytes 4000000 | tf_op jit(solution)/shard_map/pallas_call | solution.py:309
  18.4 3.7 %shard_map.187 = bf16[4,384,128]{2,1,0:T(8,128)(2,1)} custom-call(s32[1]{0:T(128)} %bitcast.where_ref, s32[2]{0:T(128)} %len_ref.1, s32[2]{0:T(128)} %acc_ref.1, bf16[4,480,128]{2,1,0:T(8,128)(2,1)} %copy-done.1, f32[128,128]{1,0:T(8,128)} %get-tuple-element.8.run_ref, f32[1,128]{1,0:T(1,128)} %pad_bitcast_fusion.rate_ref, bf16[2,1024,128]{2,1,0:T(8,128)(2,1)} %k_ref.1, ...), custom_call_target="tpu_custom_call" | custom-call | flops 300000000 | bytes 3000000 | tf_op jit(solution)/shard_map/pallas_call | solution.py:317
  22.1 11.8 %all_to_all.15.in_ref = bf16[4,384,128]{2,1,0:T(8,128)(2,1)} all-to-all(bf16[4,384,128]{2,1,0:T(8,128)(2,1)} %shard_map.187), channel_id=1, replica_groups=mesh['dp'=16,'head'=8,'tok'=4] {'tok'}, dimensions={0} | all-to-all | bytes 786432 | tf_op jit(solution)/shard_map/all_to_all | solution.py:331
  33.9 10.6 %all-to-all-start.1 = ((bf16[32,8,2176]{2,1,0:T(8,128)(2,1)}), bf16[32,8,2176]{2,1,0:T(8,128)(2,1)S(1)}, u32[]{:S(2)}, u32[]{:S(2)}) async-start(bf16[32,8,2176]{2,1,0:T(8,128)(2,1)} %get-tuple-element.7), calls=%async_computation.1 | async-start | bytes 2228224 | tf_op jit(solution)/shard_map/all_to_all | solution.py:316
  44.5 2.1 %shard_map.188 = (bf16[2,16,512]{2,1,0:T(8,128)(2,1)}, bf16[2,16,32,64]{3,2,1,0:T(8,128)(2,1)}) custom-call(bf16[4,384,128]{2,1,0:T(8,128)(2,1)} %all_to_all.15.in_ref), custom_call_target="tpu_custom_call" | custom-call | flops 1000000 | bytes 1000000 | tf_op jit(solution)/shard_map/pallas_call | solution.py:332
  46.5 24.8 %all-to-all-done.1.in_ref = bf16[32,8,2176]{2,1,0:T(8,128)(2,1)S(1)} async-done(((bf16[32,8,2176]{2,1,0:T(8,128)(2,1)}), bf16[32,8,2176]{2,1,0:T(8,128)(2,1)S(1)}, u32[]{:S(2)}, u32[]{:S(2)}) %all-to-all-start.1) | async-done | bytes 1114144 | tf_op jit(solution)/shard_map/all_to_all | solution.py:316
  71.4 0.0 copy-start
  71.4 1.0 %copy-done = bf16[32,8,2176]{2,1,0:T(8,128)(2,1)} copy-done((bf16[32,8,2176]{2,1,0:T(8,128)(2,1)}, bf16[32,8,2176]{2,1,0:T(8,128)(2,1)S(1)}, u32[]{:S(2)}) %copy-start) | copy-done | bytes 1114136
  72.4 2.1 %shard_map.186 = bf16[2,2,4096]{2,1,0:T(2,128)(2,1)} custom-call(s32[1]{0:T(128)} %bitcast.where_ref, bf16[32,8,2176]{2,1,0:T(8,128)(2,1)} %copy-done), custom_call_target="tpu_custom_call" | custom-call | flops 1000000 | bytes 1500000 | tf_op jit(solution)/shard_map/pallas_call | solution.py:338
Async XLA Ops:
  0.6 6.7 %copy-start.2 = (f32[16]{0:T(128)S(1)}, f32[16]{0:T(128)}, u32[]{:S(2)}) copy-start(f32[16]{0:T(128)} %param.22) | copy-start | bytes 196
  0.6 6.8 %copy-start.3 = (f32[16]{0:T(128)S(1)}, f32[16]{0:T(128)}, u32[]{:S(2)}) copy-start(f32[16]{0:T(128)} %param.23) | copy-start | bytes 196
  2.6 11.0 %all-to-all-start = ((bf16[4,480,128]{2,1,0:T(8,128)(2,1)}), bf16[4,480,128]{2,1,0:T(8,128)(2,1)S(1)}, u32[]{:S(2)}, u32[]{:S(2)}) async-start(bf16[4,480,128]{2,1,0:T(8,128)(2,1)} %shard_map.184), calls=%async_computation | async-start | bytes 983040 | tf_op jit(solution)/shard_map/all_to_all | solution.py:305
  13.5 0.8 %copy-start.1 = (bf16[4,480,128]{2,1,0:T(8,128)(2,1)}, bf16[4,480,128]{2,1,0:T(8,128)(2,1)S(1)}, u32[]{:S(2)}) copy-start(bf16[4,480,128]{2,1,0:T(8,128)(2,1)S(1)} %all-to-all-done.in_ref) | copy-start | bytes 1474564
  33.9 37.5 %all-to-all-start.1 = ((bf16[32,8,2176]{2,1,0:T(8,128)(2,1)}), bf16[32,8,2176]{2,1,0:T(8,128)(2,1)S(1)}, u32[]{:S(2)}, u32[]{:S(2)}) async-start(bf16[32,8,2176]{2,1,0:T(8,128)(2,1)} %get-tuple-element.7), calls=%async_computation.1 | async-start | bytes 2228224 | tf_op jit(solution)/shard_map/all_to_all | solution.py:316
  71.4 1.0 %copy-start = (bf16[32,8,2176]{2,1,0:T(8,128)(2,1)}, bf16[32,8,2176]{2,1,0:T(8,128)(2,1)S(1)}, u32[]{:S(2)}) copy-start(bf16[32,8,2176]{2,1,0:T(8,128)(2,1)S(1)} %all-to-all-done.1.in_ref) | copy-start | bytes 3342340

commit v2 on v1

--- a/solution.py
+++ b/solution.py
@@ -155,7 +155,21 @@
 
 
 def attend_kernel(
-    where_ref, len_ref, acc_ref, in_ref, run_ref, rate_ref, k_ref, v_ref, dk_ref, dv_ref, out_ref
+    where_ref,
+    len_ref,
+    acc_ref,
+    in_ref,
+    run_ref,
+    rate_ref,
+    k_ref,
+    v_ref,
+    dk_ref,
+    dv_ref,
+    near_ref,
+    next_ref,
+    across_ref,
+    last_ref,
+    out_ref,
 ):
     tok = where_ref[0]
     scale = 128 ** (-0.5)
@@ -210,26 +224,30 @@
                 state = in_ref[src, pl.ds(S_ROW + at, 32), :].astype(F32)
                 result = decay * state + added[src * 32 : src * 32 + 32]
                 out_ref[src, pl.ds(H_ROW + at, 32), :] = result.astype(BF16)
-
-
-def combine_kernel(in_ref, att_ref, state_ref):
+    for shift, ref in enumerate((near_ref, next_ref, across_ref, last_ref)):
+        ref[...] = out_ref[lax.rem(tok + shift, 4)]
+
+
+def combine_kernel(where_ref, near_ref, next_ref, across_ref, last_ref, att_ref, state_ref):
+    refs = (near_ref, next_ref, across_ref, last_ref)
     for seq in range(2):
-        stats = [in_ref[src, pl.ds(M_ROW + seq * 64, 64), :].astype(F32) for src in range(4)]
+        stats = [ref[pl.ds(M_ROW + seq * 64, 64), :].astype(F32) for ref in refs]
         peaks = [s[:, 0:1] for s in stats]
         overall = functools.reduce(jnp.maximum, peaks)
         numer = jnp.zeros((64, 128), F32)
         denominator = jnp.zeros((64, 1), F32)
-        for src in range(4):
-            rescale = jnp.exp(peaks[src] - overall)
-            denominator = denominator + rescale * stats[src][:, 64:65]
-            part = in_ref[src, pl.ds(N_ROW + seq * 64, 64), :].astype(F32)
+        for ref, peak, stat in zip(refs, peaks, stats):
+            rescale = jnp.exp(peak - overall)
+            denominator = denominator + rescale * stat[:, 64:65]
+            part = ref[pl.ds(N_ROW + seq * 64, 64), :].astype(F32)
             numer = numer + rescale * part
         context = (numer / denominator).astype(BF16)
         for head in range(4):
             att_ref[seq, :, pl.ds(head * 128, 128)] = context[head * 16 : head * 16 + 16]
-        for src in range(4):
+        for shift, ref in enumerate(refs):
+            src = lax.rem(where_ref[0] + 4 - shift, 4)
             for block in range(2):
-                pair = in_ref[src, pl.ds(H_ROW + (seq * 2 + block) * 32, 32), :]
+                pair = ref[pl.ds(H_ROW + (seq * 2 + block) * 32, 32), :]
                 state_ref[seq, src * 4 + block * 2] = pair[:, :64]
                 state_ref[seq, src * 4 + block * 2 + 1] = pair[:, 64:]
 
@@ -259,13 +277,21 @@
     return [pl.BlockSpec(memory_space=pltpu.SMEM) for _ in range(count)]
 
 
+def held(array):
+    if INTERPRET:
+        return array
+    return pltpu.with_memory_space_constraint(array, pltpu.VMEM)
+
+
 def call(kernel, ins, outs, cost, **kwargs):
     flops, moved = cost
     return pl.pallas_call(
         kernel,
         in_specs=ins,
         out_specs=tuple(in_vmem(len(outs))),
-        out_shape=tuple(jax.ShapeDtypeStruct(s, d) for s, d in outs),
+        out_shape=tuple(
+            (jax.ShapeDtypeStruct if plain else pltpu.VMEM)(s, d) for s, d, plain in outs
+        ),
         cost_estimate=pl.CostEstimate(flops=flops, bytes_accessed=moved, transcendentals=0),
         interpret=INTERPRET,
         **kwargs,
@@ -293,7 +319,7 @@
 ):
     tok = lax.axis_index("tok")
     where = tok.reshape(1).astype(jnp.int32)
-    (packed,) = call(pack_kernel, in_vmem(7), [((4, ROWS, 128), BF16)], (0, 1500000))(
+    (packed,) = call(pack_kernel, in_vmem(7), [((4, ROWS, 128), BF16, INTERPRET)], (0, 1500000))(
         mamba_input,
         gate_input,
         in_b,
@@ -303,41 +329,49 @@
         queries,
     )
     arrived = lax.all_to_all(packed, "tok", split_axis=0, concat_axis=0, tiled=True)
+    arrived = held(arrived)
     rate = jnp.pad(lax.dynamic_slice(decay_rate, (tok * 4,), (4,)), (0, 124)).reshape(1, 128)
     skip = jnp.repeat(lax.dynamic_slice(skip_weight, (tok * 4,), (4,)), 64).reshape(1, 256)
     gain = lax.dynamic_slice(norm_gain, (tok * 256,), (256,)).reshape(1, 256)
     shares, run = call(
         mixer_kernel,
         in_vmem(1) + [pl.BlockSpec(memory_space=pl.ANY)] + in_vmem(3),
-        [((32, 8, WIDTH), BF16), ((128, 128), F32)],
+        [((32, 8, WIDTH), BF16, INTERPRET), ((128, 128), F32, INTERPRET)],
         (400000000, 4000000),
         scratch_shapes=[pltpu.VMEM((256, 4096), BF16), pltpu.SemaphoreType.DMA],
     )(arrived, out_weight, rate, skip, gain)
     landed = lax.all_to_all(shares, ("head", "tok"), split_axis=0, concat_axis=0, tiled=True)
-    (back,) = call(
-        attend_kernel, in_smem(3) + in_vmem(7), [((4, BACK_ROWS, 128), BF16)], (300000000, 3000000)
+    back = call(
+        attend_kernel,
+        in_smem(3) + in_vmem(7),
+        [((BACK_ROWS, 128), BF16, INTERPRET)] * 4,
+        (0, 0),
+        scratch_shapes=[pltpu.VMEM((4, BACK_ROWS, 128), BF16)],
     )(
         where,
         cache_len,
         accepted,
         arrived,
-        run,
+        held(run),
         rate,
         cached_key_rows,
         cache_values,
         draft_token_keys,
         draft_values,
     )
-    returned = lax.all_to_all(back, "tok", split_axis=0, concat_axis=0, tiled=True)
+    returned = [held(back[0])] + [
+        held(lax.ppermute(back[k], "tok", [(i, (i + k) % 4) for i in range(4)]))
+        for k in (1, 2, 3)
+    ]
     attn_context, state_t = call(
         combine_kernel,
-        in_vmem(1),
-        [((2, 16, 512), BF16), ((2, 16, 32, 64), BF16)],
-        (1000000, 1000000),
-    )(returned)
+        in_smem(1) + in_vmem(4),
+        [((2, 16, 512), BF16, True), ((2, 16, 32, 64), BF16, True)],
+        (0, 0),
+    )(where, *returned)
     (mamba_out,) = call(
-        sum_kernel, in_smem(1) + in_vmem(1), [((2, 2, 4096), BF16)], (1000000, 1500000)
-    )(where, landed)
+        sum_kernel, in_smem(1) + in_vmem(1), [((2, 2, 4096), BF16, True)], (1000000, 1500000)
+    )(where, held(landed))
     return (mamba_out, attn_context, jnp.swapaxes(state_t, 2, 3))
 
 

time: 75 us -> 57.9 us (0.77)
  the two profiles are of different devices: /device:TPU:452 before, /device:TPU:386 now
where the time goes in v2:
time: 57.9 us; the launch traced here: 57.5 us
  starting transfers between devices  24.6 us (42%)
  waiting for transfers between devices  18.6 us (32%)
  Pallas kernels  10.8 us (19%)
  local copies, waits for them, and re-layouts  2.71 us (5%)
  between operations  0.71 us (1%)
    ppermute x3, starting transfers between devices, body(): lax.ppermute(back[k], 'tok', [(i, (i + k) % 4) for i in range(4)])  10.4 us
    all_to_all x1, starting transfers between devices, body(): lax.all_to_all(shares, ('head', 'tok'), split_axis=0, concat_axis=0, tile...  9.34 us
    all_to_all x1, waiting for transfers between devices, body(): lax.all_to_all(shares, ('head', 'tok'), split_axis=0, concat_axis=0, tile...  8.82 us
    all_to_all x1, waiting for transfers between devices, body(): lax.all_to_all(packed, 'tok', split_axis=0, concat_axis=0, tiled=True)  4.96 us
    all_to_all x1, starting transfers between devices, body(): lax.all_to_all(packed, 'tok', split_axis=0, concat_axis=0, tiled=True)  4.82 us
    ppermute x3, waiting for transfers between devices, body(): lax.ppermute(back[k], 'tok', [(i, (i + k) % 4) for i in range(4)])  4.82 us
    pallas_call x1, Pallas kernels, body(): call(mixer_kernel, in_vmem(1) + [pl.BlockSpec(memory_space=pl.ANY)] + in_...  4.25 us
    pallas_call x1, Pallas kernels, body(): call(attend_kernel, in_smem(3) + in_vmem(7), [((BACK_ROWS, 128), BF16, IN...  2.8 us
  transfers between devices with their start and end apart: 5, of which 4 were waited for; matrix products, arithmetic and copies ran while one was open for 5% of the time, Pallas kernels for 7%

profile of v2, /device:TPU:386, one launch (start us, length us, event | category | flops | bytes accessed | tf_op | source)
XLA Modules:
  0.0 57.5 jit_solution(13115609712052207819)
XLA Ops:
  0.6 0.0 copy-start
  0.6 0.0 copy-start.1
  0.7 1.9 %shard_map.184 = bf16[4,480,128]{2,1,0:T(8,128)(2,1)} custom-call(bf16[2,16,1024]{2,1,0:T(8,128)(2,1)} %x_ref.1, bf16[2,16,1024]{2,1,0:T(8,128)(2,1)} %z_ref.1, bf16[2,16,128]{2,1,0:T(8,128)(2,1)} %b_ref.1, bf16[2,16,128]{2,1,0:T(8,128)(2,1)} %c_ref.1, bf16[2,16,16]{2,1,0:T(8,128)(2,1)} %t_ref.1, bf16[2,16,32,64]{3,2,1,0:T(8,128)(2,1)} %bitcast.6, ...), custom_call_target="tpu_custom_call" | custom-call | bytes 1500000 | tf_op jit(solution)/shard_map/pallas_call | solution.py:322
  2.6 4.8 %all-to-all-start = ((bf16[4,480,128]{2,1,0:T(8,128)(2,1)}), bf16[4,480,128]{2,1,0:T(8,128)(2,1)S(1)}, u32[]{:S(2)}, u32[]{:S(2)}) async-start(bf16[4,480,128]{2,1,0:T(8,128)(2,1)} %shard_map.184), calls=%async_computation | async-start | bytes 983040 | tf_op jit(solution)/shard_map/all_to_all | solution.py:331
  7.4 0.0 copy-done
  7.4 0.1 dynamic_slice.9
  7.5 0.0 copy-done.1
  7.5 0.1 dynamic_slice.10
  7.5 0.1 broadcast_in_dim.3
  7.6 0.6 %reshape_reshape.3.skip_ref = f32[1,256]{1,0:T(1,128)} reshape(f32[4,64]{1,0:T(4,128)S(1)} %broadcast_in_dim.3) | data formatting | bytes 2048 | tf_op jit(solution)/shard_map/reshape;reshape | solution.py:334
  8.3 1.3 %dynamic_slice.11 = f32[256]{0:T(256)} dynamic-slice(f32[1024]{0:T(1024)} %param.24, s32[]{:T(128)S(6)} %select_n.8), dynamic_slice_sizes={256} | dynamic-slice | bytes 2052 | tf_op jit(solution)/shard_map/dynamic_slice | solution.py:335
  9.6 0.5 pad_bitcast_fusion.rate_ref
  10.1 5.0 %all-to-all-done.in_ref = bf16[4,480,128]{2,1,0:T(8,128)(2,1)S(1)} async-done(((bf16[4,480,128]{2,1,0:T(8,128)(2,1)}), bf16[4,480,128]{2,1,0:T(8,128)(2,1)S(1)}, u32[]{:S(2)}, u32[]{:S(2)}) %all-to-all-start) | async-done | bytes 491552 | tf_op jit(solution)/shard_map/all_to_all | solution.py:331
  15.1 4.2 %shard_map.185 = (bf16[32,8,2176]{2,1,0:T(8,128)(2,1)}, f32[128,128]{1,0:T(8,128)S(1)}) custom-call(bf16[4,480,128]{2,1,0:T(8,128)(2,1)S(1)} %all-to-all-done.in_ref, bf16[256,4096]{1,0:T(8,128)(2,1)} %w_ref.1, f32[1,128]{1,0:T(1,128)} %pad_bitcast_fusion.rate_ref, f32[1,256]{1,0:T(1,128)} %reshape_reshape.3.skip_ref, f32[1,256]{1,0:T(1,128)} %bitcast.7), custom_call_target="tpu_custom_call" | custom-call | flops 400000000 | bytes 4000000 | tf_op jit(solution)/shard_map/pallas_call | solution.py:336
  19.3 9.3 %all-to-all-start.1 = ((bf16[32,8,2176]{2,1,0:T(8,128)(2,1)}), bf16[32,8,2176]{2,1,0:T(8,128)(2,1)S(1)}, u32[]{:S(2)}, u32[]{:S(2)}) async-start(bf16[32,8,2176]{2,1,0:T(8,128)(2,1)} %get-tuple-element.11), calls=%async_computation.1 | async-start | bytes 2228224 | tf_op jit(solution)/shard_map/all_to_all | solution.py:343
  28.7 2.8 %shard_map.187 = (bf16[384,128]{1,0:T(8,128)(2,1)S(1)}, bf16[384,128]{1,0:T(8,128)(2,1)S(1)}, bf16[384,128]{1,0:T(8,128)(2,1)S(1)}, bf16[384,128]{1,0:T(8,128)(2,1)S(1)}) custom-call(s32[1]{0:T(128)} %bitcast.where_ref, s32[2]{0:T(128)} %len_ref.1, s32[2]{0:T(128)} %acc_ref.1, bf16[4,480,128]{2,1,0:T(8,128)(2,1)S(1)} %all-to-all-done.in_ref, ...), custom_call_target="tpu_custom_call" | custom-call | tf_op jit(solution)/shard_map/pallas_call | solution.py:344
  31.5 3.4 %collective-permute-start = (bf16[384,128]{1,0:T(8,128)(2,1)S(1)}, bf16[384,128]{1,0:T(8,128)(2,1)S(1)}, u32[]{:S(2)}, u32[]{:S(2)}) collective-permute-start(bf16[384,128]{1,0:T(8,128)(2,1)S(1)} %get-tuple-element.14), channel_id=1, source_target_pairs={{0,1},{1,2},{2,3},{3,0},{4,5},{5,6},{6,7},{7,4},{8,9},{9,10},{10,1... | collective-permute-start | bytes 294920 | tf_op jit(solution)/shard_map/ppermute | solution.py:363
  34.9 2.7 %collective-permute-start.1 = (bf16[384,128]{1,0:T(8,128)(2,1)S(1)}, bf16[384,128]{1,0:T(8,128)(2,1)S(1)}, u32[]{:S(2)}, u32[]{:S(2)}) collective-permute-start(bf16[384,128]{1,0:T(8,128)(2,1)S(1)} %get-tuple-element.15), channel_id=1, source_target_pairs={{0,2},{1,3},{2,0},{3,1},{4,6},{5,7},{6,4},{7,5},{8,10},{9,11},{10,... | collective-permute-start | bytes 294920 | tf_op jit(solution)/shard_map/ppermute | solution.py:363
  37.6 4.3 %collective-permute-start.2 = (bf16[384,128]{1,0:T(8,128)(2,1)S(1)}, bf16[384,128]{1,0:T(8,128)(2,1)S(1)}, u32[]{:S(2)}, u32[]{:S(2)}) collective-permute-start(bf16[384,128]{1,0:T(8,128)(2,1)S(1)} %get-tuple-element.16), channel_id=1, source_target_pairs={{0,3},{1,0},{2,1},{3,2},{4,7},{5,4},{6,5},{7,6},{8,11},{9,8},{10,9... | collective-permute-start | bytes 294920 | tf_op jit(solution)/shard_map/ppermute | solution.py:363
  41.9 0.0 collective-permute-done.next_ref
  41.9 3.1 %collective-permute-done.1.across_ref = bf16[384,128]{1,0:T(8,128)(2,1)S(1)} collective-permute-done((bf16[384,128]{1,0:T(8,128)(2,1)S(1)}, bf16[384,128]{1,0:T(8,128)(2,1)S(1)}, u32[]{:S(2)}, u32[]{:S(2)}) %collective-permute-start.1) | collective-permute-done | bytes 98336 | tf_op jit(solution)/shard_map/ppermute | solution.py:363
  45.1 1.7 %collective-permute-done.2.last_ref = bf16[384,128]{1,0:T(8,128)(2,1)S(1)} collective-permute-done((bf16[384,128]{1,0:T(8,128)(2,1)S(1)}, bf16[384,128]{1,0:T(8,128)(2,1)S(1)}, u32[]{:S(2)}, u32[]{:S(2)}) %collective-permute-start.2) | collective-permute-done | bytes 98336 | tf_op jit(solution)/shard_map/ppermute | solution.py:363
  46.8 1.1 %shard_map.188 = (bf16[2,16,512]{2,1,0:T(8,128)(2,1)}, bf16[2,16,32,64]{3,2,1,0:T(8,128)(2,1)}) custom-call(s32[1]{0:T(128)} %bitcast.where_ref, bf16[384,128]{1,0:T(8,128)(2,1)S(1)} %get-tuple-element.13.near_ref, bf16[384,128]{1,0:T(8,128)(2,1)S(1)} %collective-permute-done.next_ref, bf16[384,128]{1,0:T(8,128)(2,1)S(1)} %collective-permute-done.1.across_ref, ...), custom_call_target="tpu_custom_call" | custom-call | tf_op jit(solution)/shard_map/pallas_call | solution.py:366
  47.8 8.8 %all-to-all-done.1.in_ref = bf16[32,8,2176]{2,1,0:T(8,128)(2,1)S(1)} async-done(((bf16[32,8,2176]{2,1,0:T(8,128)(2,1)}), bf16[32,8,2176]{2,1,0:T(8,128)(2,1)S(1)}, u32[]{:S(2)}, u32[]{:S(2)}) %all-to-all-start.1) | async-done | bytes 1114144 | tf_op jit(solution)/shard_map/all_to_all | solution.py:343
  56.7 0.8 %shard_map.186 = bf16[2,2,4096]{2,1,0:T(2,128)(2,1)} custom-call(s32[1]{0:T(128)} %bitcast.where_ref, bf16[32,8,2176]{2,1,0:T(8,128)(2,1)S(1)} %all-to-all-done.1.in_ref), custom_call_target="tpu_custom_call" | custom-call | flops 1000000 | bytes 1500000 | tf_op jit(solution)/shard_map/pallas_call | solution.py:372
Async XLA Ops:
  0.6 6.8 %copy-start = (f32[16]{0:T(128)S(1)}, f32[16]{0:T(128)}, u32[]{:S(2)}) copy-start(f32[16]{0:T(128)} %param.22) | copy-start | bytes 196
  0.6 6.8 %copy-start.1 = (f32[16]{0:T(128)S(1)}, f32[16]{0:T(128)}, u32[]{:S(2)}) copy-start(f32[16]{0:T(128)} %param.23) | copy-start | bytes 196
  2.6 12.5 %all-to-all-start = ((bf16[4,480,128]{2,1,0:T(8,128)(2,1)}), bf16[4,480,128]{2,1,0:T(8,128)(2,1)S(1)}, u32[]{:S(2)}, u32[]{:S(2)}) async-start(bf16[4,480,128]{2,1,0:T(8,128)(2,1)} %shard_map.184), calls=%async_computation | async-start | bytes 983040 | tf_op jit(solution)/shard_map/all_to_all | solution.py:331
  19.3 37.3 %all-to-all-start.1 = ((bf16[32,8,2176]{2,1,0:T(8,128)(2,1)}), bf16[32,8,2176]{2,1,0:T(8,128)(2,1)S(1)}, u32[]{:S(2)}, u32[]{:S(2)}) async-start(bf16[32,8,2176]{2,1,0:T(8,128)(2,1)} %get-tuple-element.11), calls=%async_computation.1 | async-start | bytes 2228224 | tf_op jit(solution)/shard_map/all_to_all | solution.py:343
  31.5 10.5 %collective-permute-start = (bf16[384,128]{1,0:T(8,128)(2,1)S(1)}, bf16[384,128]{1,0:T(8,128)(2,1)S(1)}, u32[]{:S(2)}, u32[]{:S(2)}) collective-permute-start(bf16[384,128]{1,0:T(8,128)(2,1)S(1)} %get-tuple-element.14), channel_id=1, source_target_pairs={{0,1},{1,2},{2,3},{3,0},{4,5},{5,6},{6,7},{7,4},{8,9},{9,10},{10,1... | collective-permute-start | bytes 294920 | tf_op jit(solution)/shard_map/ppermute | solution.py:363
  34.9 10.2 %collective-permute-start.1 = (bf16[384,128]{1,0:T(8,128)(2,1)S(1)}, bf16[384,128]{1,0:T(8,128)(2,1)S(1)}, u32[]{:S(2)}, u32[]{:S(2)}) collective-permute-start(bf16[384,128]{1,0:T(8,128)(2,1)S(1)} %get-tuple-element.15), channel_id=1, source_target_pairs={{0,2},{1,3},{2,0},{3,1},{4,6},{5,7},{6,4},{7,5},{8,10},{9,11},{10,... | collective-permute-start | bytes 294920 | tf_op jit(solution)/shard_map/ppermute | solution.py:363
  37.6 9.2 %collective-permute-start.2 = (bf16[384,128]{1,0:T(8,128)(2,1)S(1)}, bf16[384,128]{1,0:T(8,128)(2,1)S(1)}, u32[]{:S(2)}, u32[]{:S(2)}) collective-permute-start(bf16[384,128]{1,0:T(8,128)(2,1)S(1)} %get-tuple-element.16), channel_id=1, source_target_pairs={{0,3},{1,0},{2,1},{3,2},{4,7},{5,4},{6,5},{7,6},{8,11},{9,8},{10,9... | collective-permute-start | bytes 294920 | tf_op jit(solution)/shard_map/ppermute | solution.py:363

commit v3 on v2

--- a/solution.py
+++ b/solution.py
@@ -15,22 +15,26 @@
 F32 = jnp.float32
 BF16 = jnp.bfloat16
 
+PAIR = 512
+
 X_ROW = 0
-Z_ROW = 64
-B_ROW = 128
-C_ROW = 160
-Q_ROW = 192
-S_ROW = 320
-T_ROW = 448
-ROWS = 480
+Z_ROW = 128
+B_ROW = 256
+C_ROW = 288
+Q_ROW = 320
+S_ROW = 448
+T_ROW = 704
+ROWS = 736
 
 N_ROW = 0
 M_ROW = 128
 H_ROW = 256
 BACK_ROWS = 384
 
-HALF = 2048
+COLUMNS = 2048
+HALF = 1024
 WIDTH = HALF + 128
+PIECE = 128
 
 
 def dot(a, b):
@@ -45,28 +49,41 @@
     return lax.broadcasted_iota(jnp.int32, shape, dim)
 
 
-def pack_kernel(x_ref, z_ref, b_ref, c_ref, t_ref, s_ref, q_ref, out_ref):
+def pack_kernel(
+    where_ref, x_ref, z_ref, b_ref, c_ref, t_ref, s_ref, q_ref, w_ref, out_ref, piece_ref, sem
+):
+    tok, core = where_ref[0], where_ref[1]
+    rows = pl.ds(pl.multiple_of(core * PIECE, PIECE), PIECE)
+    columns = pl.ds(pl.multiple_of((1 - tok % 2) * COLUMNS, COLUMNS), COLUMNS)
+    fetch = pltpu.make_async_copy(w_ref.at[rows, columns], piece_ref, sem)
+    fetch.start()
     for seq in range(2):
         bs = b_ref[seq]
         cs = c_ref[seq]
-        steps = t_ref[seq]
-        for to in range(4):
-            for block in range(2):
-                lanes = pl.ds(to * 256 + block * 128, 128)
-                row = (seq * 2 + block) * 16
-                out_ref[to, pl.ds(X_ROW + row, 16), :] = x_ref[seq, :, lanes]
-                out_ref[to, pl.ds(Z_ROW + row, 16), :] = z_ref[seq, :, lanes]
-                head = to * 4 + block * 2
-                pair = jnp.concatenate([s_ref[seq, head], s_ref[seq, head + 1]], axis=1)
-                out_ref[to, pl.ds(S_ROW + (seq * 2 + block) * 32, 32), :] = pair
-            out_ref[to, pl.ds(B_ROW + seq * 16, 16), :] = bs
-            out_ref[to, pl.ds(C_ROW + seq * 16, 16), :] = cs
-            for head in range(4):
-                row = Q_ROW + (seq * 4 + head) * 16
-                out_ref[to, pl.ds(row, 16), :] = q_ref[seq, :, pl.ds(head * 128, 128)]
-            own = steps[:, to * 4 : to * 4 + 4].astype(F32)
-            own = jnp.concatenate([own, jnp.zeros((16, 124), F32)], axis=1)
-            out_ref[to, pl.ds(T_ROW + seq * 16, 16), :] = own.astype(BF16)
+        steps = t_ref[seq].astype(F32)
+        heads = [q_ref[seq, :, pl.ds(head * 128, 128)] for head in range(4)]
+        for pair in range(2):
+            own = steps[:, pair * 8 : pair * 8 + 8]
+            own = jnp.concatenate([own, jnp.zeros((16, 120), F32)], axis=1).astype(BF16)
+            for block in range(4):
+                lanes = pl.ds(pair * PAIR + block * 128, 128)
+                row = (seq * 4 + block) * 16
+                x = x_ref[seq, :, lanes]
+                z = z_ref[seq, :, lanes]
+                head = pair * 8 + block * 2
+                state = jnp.concatenate([s_ref[seq, head], s_ref[seq, head + 1]], axis=1)
+                for to in (2 * pair, 2 * pair + 1):
+                    out_ref[to, pl.ds(X_ROW + row, 16), :] = x
+                    out_ref[to, pl.ds(Z_ROW + row, 16), :] = z
+                    out_ref[to, pl.ds(S_ROW + 2 * row, 32), :] = state
+            for to in (2 * pair, 2 * pair + 1):
+                out_ref[to, pl.ds(B_ROW + seq * 16, 16), :] = bs
+                out_ref[to, pl.ds(C_ROW + seq * 16, 16), :] = cs
+                out_ref[to, pl.ds(T_ROW + seq * 16, 16), :] = own
+                for head in range(4):
+                    row = Q_ROW + (seq * 4 + head) * 16
+                    out_ref[to, pl.ds(row, 16), :] = heads[head]
+    fetch.wait()
 
 
 def both(in_ref, first, stride):
@@ -77,10 +94,33 @@
 
 
 def mixer_kernel(
-    in_ref, w_ref, rate_ref, skip_ref, gain_ref, out_ref, run_ref, w_buf, sem
+    where_ref,
+    in_ref,
+    w_ref,
+    same_ref,
+    other_ref,
+    rate_ref,
+    skip_ref,
+    gain_ref,
+    out_ref,
+    run_ref,
+    w_buf,
+    sems,
 ):
-    fetch = pltpu.make_async_copy(w_ref, w_buf, sem)
-    fetch.start()
+    side, core = where_ref[0] % 2, where_ref[1]
+    columns = pl.ds(pl.multiple_of(side * COLUMNS, COLUMNS), COLUMNS)
+
+    def rows(first, count):
+        return w_buf.at[pl.ds(pl.multiple_of(first, PIECE), count), :]
+
+    near = (1 - side) * 256
+    fetches = [
+        pltpu.make_async_copy(w_ref.at[:, columns], rows(side * 256, 256), sems.at[0]),
+        pltpu.make_async_copy(same_ref, rows(near + core * PIECE, PIECE), sems.at[1]),
+        pltpu.make_async_copy(other_ref, rows(near + (1 - core) * PIECE, PIECE), sems.at[2]),
+    ]
+    for fetch in fetches:
+        fetch.start()
     row = iota((128, 128), 0)
     col = iota((128, 128), 1)
     low = col < 64
@@ -99,9 +139,9 @@
     affinity = dot_t(readout, inflow)
     squares = jnp.zeros((128, 1), F32)
     parts = []
-    for block in range(2):
-        x = both(in_ref, X_ROW + block * 16, 32)
-        z = both(in_ref, Z_ROW + block * 16, 32).astype(F32)
+    for block in range(4):
+        x = both(in_ref, X_ROW + block * 16, 64)
+        z = both(in_ref, Z_ROW + block * 16, 64).astype(F32)
         mixed = []
         for half in range(2):
             head = block * 2 + half
@@ -115,7 +155,7 @@
         for seq in range(2):
             state = jnp.concatenate(
                 [
-                    in_ref[src, pl.ds(S_ROW + (seq * 2 + block) * 32, 32), :]
+                    in_ref[src, pl.ds(S_ROW + (seq * 4 + block) * 32, 32), :]
                     for src in range(4)
                 ],
                 axis=0,
@@ -146,8 +186,9 @@
         out_ref[:, :, lanes] = jnp.stack([even, odd], axis=1).reshape(32, 8, width).astype(BF16)
 
     store(dot(first, squares), dot(second, squares), pl.ds(HALF, 128), 128)
-    fetch.wait()
-    for chunk in range(8):
+    for fetch in fetches:
+        fetch.wait()
+    for chunk in range(HALF // 256):
         lanes = pl.ds(chunk * 256, 256)
         a = dot(lhs_a, w_buf[:, lanes])
         b = dot(lhs_b, w_buf[:, pl.ds(HALF + chunk * 256, 256)])
@@ -202,6 +243,15 @@
     row = iota((128, 128), 0)
     low = iota((128, 128), 1) < 64
     low_row = iota((1, 128), 1) < 64
+    side = tok % 2
+
+    def pick(values, block):
+        cols = [
+            jnp.where(side == 0, values[:, k : k + 1], values[:, k + 4 : k + 5])
+            for k in (2 * block, 2 * block + 1)
+        ]
+        return jnp.where(low if values.shape[0] > 1 else low_row, cols[0], cols[1])
+
     steps = both(in_ref, T_ROW, 16).astype(F32)
     inflow_t = both(in_ref, B_ROW, 16).astype(F32).T.astype(BF16)
     run = run_ref[...]
@@ -212,18 +262,16 @@
         weights = jnp.where(alive, jnp.exp(jnp.where(alive, end - run, 0.0)) * steps, 0.0)
         keep = jnp.exp(end)
         for block in range(2):
-            first, second = 2 * block, 2 * block + 1
-            x = both(in_ref, X_ROW + block * 16, 32).astype(F32)
-            factor = jnp.where(
-                low, weights[:, first : first + 1], weights[:, second : second + 1]
-            )
-            added = dot(inflow_t, (x * factor).astype(BF16))
-            decay = jnp.where(low_row, keep[:, first : first + 1], keep[:, second : second + 1])
+            start = pl.multiple_of((2 * side + block) * 16, 16)
+            x = both(in_ref, X_ROW + start, 64).astype(F32)
+            added = dot(inflow_t, (x * pick(weights, block)).astype(BF16))
+            decay = pick(keep, block)
             for src in range(4):
-                at = (seq * 2 + block) * 32
-                state = in_ref[src, pl.ds(S_ROW + at, 32), :].astype(F32)
+                first = pl.multiple_of(S_ROW + seq * 128 + 2 * start, 32)
+                state = in_ref[src, pl.ds(first, 32), :].astype(F32)
                 result = decay * state + added[src * 32 : src * 32 + 32]
-                out_ref[src, pl.ds(H_ROW + at, 32), :] = result.astype(BF16)
+                at = H_ROW + (seq * 2 + block) * 32
+                out_ref[src, pl.ds(at, 32), :] = result.astype(BF16)
     for shift, ref in enumerate((near_ref, next_ref, across_ref, last_ref)):
         ref[...] = out_ref[lax.rem(tok + shift, 4)]
 
@@ -255,18 +303,21 @@
 def sum_kernel(where_ref, in_ref, out_ref):
     squares = in_ref[:, :, pl.ds(HALF, 128)].astype(F32)
     squares = squares.reshape(8, 4, 8, 128).sum(axis=1)
-    scale = lax.rsqrt(squares * (1.0 / 1024.0) + EPSILON)
+    scale = lax.rsqrt(squares * (0.5 / 1024.0) + EPSILON)
     swapped = where_ref[0] % 2 == 1
     for chunk in range(HALF // 128):
         part = in_ref[:, :, pl.ds(chunk * 128, 128)].astype(F32)
-        part = part.reshape(8, 4, 8, 128).sum(axis=1)
-        total = (part * scale).sum(axis=0)
-        flipped = jnp.concatenate([total[4:8], total[0:4]], axis=0)
-        total = jnp.where(swapped, flipped, total).astype(BF16)
-        for draft in range(2):
-            for half in range(2):
-                rows = total[half * 4 + draft * 2 : half * 4 + draft * 2 + 2]
-                out_ref[draft, :, pl.ds(half * HALF + chunk * 128, 128)] = rows
+        part = part.reshape(8, 2, 2, 8, 128).sum(axis=1)
+        both_sides = (part * scale[:, None]).sum(axis=0)
+        for side in range(2):
+            total = both_sides[side]
+            flipped = jnp.concatenate([total[4:8], total[0:4]], axis=0)
+            total = jnp.where(swapped, flipped, total).astype(BF16)
+            for draft in range(2):
+                for half in range(2):
+                    rows = total[half * 4 + draft * 2 : half * 4 + draft * 2 + 2]
+                    first = side * COLUMNS + half * HALF + chunk * 128
+                    out_ref[draft, :, pl.ds(first, 128)] = rows
 
 
 def in_vmem(count):
@@ -318,8 +369,16 @@
     accepted,
 ):
     tok = lax.axis_index("tok")
-    where = tok.reshape(1).astype(jnp.int32)
-    (packed,) = call(pack_kernel, in_vmem(7), [((4, ROWS, 128), BF16, INTERPRET)], (0, 1500000))(
+    where = jnp.stack([tok, lax.axis_index("dp") % 2]).astype(jnp.int32)
+    whole = pl.BlockSpec(memory_space=pl.ANY)
+    packed, piece = call(
+        pack_kernel,
+        in_smem(1) + in_vmem(7) + [whole],
+        [((4, ROWS, 128), BF16, True), ((PIECE, COLUMNS), BF16, INTERPRET)],
+        (0, 2500000),
+        scratch_shapes=[pltpu.SemaphoreType.DMA],
+    )(
+        where,
         mamba_input,
         gate_input,
         in_b,
@@ -327,19 +386,23 @@
         step_size,
         jnp.swapaxes(ssm_state, 2, 3),
         queries,
-    )
+        out_weight,
+    )
+    same = lax.ppermute(piece, "tok", [(i, i ^ 1) for i in range(4)])
+    other = lax.ppermute(same, "dp", [(i, i ^ 1) for i in range(lax.axis_size("dp"))])
     arrived = lax.all_to_all(packed, "tok", split_axis=0, concat_axis=0, tiled=True)
     arrived = held(arrived)
-    rate = jnp.pad(lax.dynamic_slice(decay_rate, (tok * 4,), (4,)), (0, 124)).reshape(1, 128)
-    skip = jnp.repeat(lax.dynamic_slice(skip_weight, (tok * 4,), (4,)), 64).reshape(1, 256)
-    gain = lax.dynamic_slice(norm_gain, (tok * 256,), (256,)).reshape(1, 256)
+    pair = tok // 2
+    rate = jnp.pad(lax.dynamic_slice(decay_rate, (pair * 8,), (8,)), (0, 120)).reshape(1, 128)
+    skip = jnp.repeat(lax.dynamic_slice(skip_weight, (pair * 8,), (8,)), 64).reshape(1, PAIR)
+    gain = lax.dynamic_slice(norm_gain, (pair * PAIR,), (PAIR,)).reshape(1, PAIR)
     shares, run = call(
         mixer_kernel,
-        in_vmem(1) + [pl.BlockSpec(memory_space=pl.ANY)] + in_vmem(3),
-        [((32, 8, WIDTH), BF16, INTERPRET), ((128, 128), F32, INTERPRET)],
+        in_smem(1) + in_vmem(1) + [whole] + in_vmem(5),
+        [((32, 8, WIDTH), BF16, True), ((128, 128), F32, INTERPRET)],
         (400000000, 4000000),
-        scratch_shapes=[pltpu.VMEM((256, 4096), BF16), pltpu.SemaphoreType.DMA],
-    )(arrived, out_weight, rate, skip, gain)
+        scratch_shapes=[pltpu.VMEM((PAIR, COLUMNS), BF16), pltpu.SemaphoreType.DMA((3,))],
+    )(where, arrived, out_weight, held(same), held(other), rate, skip, gain)
     landed = lax.all_to_all(shares, ("head", "tok"), split_axis=0, concat_axis=0, tiled=True)
     back = call(
         attend_kernel,

time: 57.9 us -> 62.6 us (1.081)
  the two profiles are of different devices: /device:TPU:386 before, /device:TPU:320 now
where the time goes in v3:
time: 62.6 us; the launch traced here: 62.1 us
  starting transfers between devices  28.7 us (46%)
  waiting for transfers between devices  17.5 us (28%)
  Pallas kernels  12.4 us (20%)
  local copies, waits for them, and re-layouts  2.05 us (3%)
  between operations  0.78 us (1%)
    ppermute x3, starting transfers between devices, body(): lax.ppermute(back[k], 'tok', [(i, (i + k) % 4) for i in range(4)])  11.7 us
    ppermute x1, waiting for transfers between devices, body(): same = lax.ppermute(piece, 'tok', [(i, i ^ 1) for i in range(4)])  9.28 us
    all_to_all x1, starting transfers between devices, body(): lax.all_to_all(shares, ('head', 'tok'), split_axis=0, concat_axis=0, tile...  7.73 us
    all_to_all x1, waiting for transfers between devices, body(): lax.all_to_all(packed, 'tok', split_axis=0, concat_axis=0, tiled=True)  5.13 us
    all_to_all x1, starting transfers between devices, body(): lax.all_to_all(packed, 'tok', split_axis=0, concat_axis=0, tiled=True)  4.01 us
    ppermute x1, starting transfers between devices, body(): same = lax.ppermute(piece, 'tok', [(i, i ^ 1) for i in range(4)])  3.4 us
    pallas_call x1, Pallas kernels, body(): call(mixer_kernel, in_smem(1) + in_vmem(1) + [whole] + in_vmem(5), [((32,...  3.36 us
    ppermute x3, waiting for transfers between devices, body(): lax.ppermute(back[k], 'tok', [(i, (i + k) % 4) for i in range(4)])  3.12 us
  transfers between devices with their start and end apart: 7, of which 4 were waited for; matrix products, arithmetic and copies ran while one was open for 3% of the time, Pallas kernels for 7%

profile of v3, /device:TPU:320, one launch (start us, length us, event | category | flops | bytes accessed | tf_op | source)
XLA Modules:
  0.0 62.1 jit_solution(7145005863638738979)
XLA Ops:
  0.6 0.0 copy-start.1
  0.6 0.0 copy-start.2
  0.7 0.0 copy-start
  0.7 0.6 pad_add_fusion.where_ref
  1.3 3.0 %shard_map.184 = (bf16[4,736,128]{2,1,0:T(8,128)(2,1)}, bf16[128,2048]{1,0:T(8,128)(2,1)S(1)}) custom-call(s32[2]{0:T(128)} %pad_add_fusion.where_ref, bf16[2,16,1024]{2,1,0:T(8,128)(2,1)} %x_ref.1, bf16[2,16,1024]{2,1,0:T(8,128)(2,1)} %z_ref.1, bf16[2,16,128]{2,1,0:T(8,128)(2,1)} %b_ref.1, bf16[2,16,128]{2,1,0:T(8,128)(2,1)} %c_ref.1, ...), custom_call_target="tpu_custom_call" | custom-call | bytes 2500000 | tf_op jit(solution)/shard_map/pallas_call | solution.py:374
  4.2 3.4 %collective-permute-start = (bf16[128,2048]{1,0:T(8,128)(2,1)S(1)}, bf16[128,2048]{1,0:T(8,128)(2,1)S(1)}, u32[]{:S(2)}, u32[]{:S(2)}) collective-permute-start(bf16[128,2048]{1,0:T(8,128)(2,1)S(1)} %get-tuple-element.14), channel_id=1, source_target_pairs={{0,1},{1,0},{2,3},{3,2},{4,5},{5,4},{6,7},{7,6},{8,9},{9,8},{10,11... | collective-permute-start | bytes 1572872 | tf_op jit(solution)/shard_map/ppermute | solution.py:391
  7.7 4.0 %all-to-all-start = ((bf16[4,736,128]{2,1,0:T(8,128)(2,1)}), bf16[4,736,128]{2,1,0:T(8,128)(2,1)S(1)}, u32[]{:S(2)}, u32[]{:S(2)}) async-start(bf16[4,736,128]{2,1,0:T(8,128)(2,1)} %get-tuple-element.13), calls=%async_computation | async-start | bytes 1507328 | tf_op jit(solution)/shard_map/all_to_all | solution.py:393
  11.7 9.3 %collective-permute-done.same_ref = bf16[128,2048]{1,0:T(8,128)(2,1)S(1)} collective-permute-done((bf16[128,2048]{1,0:T(8,128)(2,1)S(1)}, bf16[128,2048]{1,0:T(8,128)(2,1)S(1)}, u32[]{:S(2)}, u32[]{:S(2)}) %collective-permute-start) | collective-permute-done | bytes 524320 | tf_op jit(solution)/shard_map/ppermute | solution.py:391
  21.0 1.9 %collective-permute-start.1 = (bf16[128,2048]{1,0:T(8,128)(2,1)S(1)}, bf16[128,2048]{1,0:T(8,128)(2,1)S(1)}, u32[]{:S(2)}, u32[]{:S(2)}) collective-permute-start(bf16[128,2048]{1,0:T(8,128)(2,1)S(1)} %collective-permute-done.same_ref), channel_id=1, source_target_pairs={{0,32},{32,0},{64,96},{96,64},{128,160},{160,128},{192,224},{224,1... | collective-permute-start | bytes 1572872 | tf_op jit(solution)/shard_map/ppermute | solution.py:392
  22.9 0.0 copy-done.1
  22.9 0.1 dynamic_slice.9
  23.0 0.0 copy-done.2
  23.0 0.1 dynamic_slice.10
  23.1 0.1 broadcast_in_dim.3
  23.1 0.7 %reshape_reshape.3.skip_ref = f32[1,512]{1,0:T(1,128)} reshape(f32[8,64]{1,0:T(8,128)S(1)} %broadcast_in_dim.3) | data formatting | bytes 4096 | tf_op jit(solution)/shard_map/reshape;reshape | solution.py:397
  23.8 0.0 copy-done
  23.8 0.7 %dynamic_slice.11 = f32[512]{0:T(512)} dynamic-slice(f32[1024]{0:T(1024)S(1)} %copy-done, s32[]{:T(128)S(6)} %select_n.21), dynamic_slice_sizes={512} | dynamic-slice | bytes 4100 | tf_op jit(solution)/shard_map/dynamic_slice | solution.py:398
  24.4 0.5 pad_bitcast_fusion.rate_ref
  25.0 5.1 %all-to-all-done.in_ref = bf16[4,736,128]{2,1,0:T(8,128)(2,1)S(1)} async-done(((bf16[4,736,128]{2,1,0:T(8,128)(2,1)}), bf16[4,736,128]{2,1,0:T(8,128)(2,1)S(1)}, u32[]{:S(2)}, u32[]{:S(2)}) %all-to-all-start) | async-done | bytes 753696 | tf_op jit(solution)/shard_map/all_to_all | solution.py:393
  30.1 0.0 collective-permute-done.1.other_ref
  30.1 3.4 %shard_map.185 = (bf16[32,8,1152]{2,1,0:T(8,128)(2,1)}, f32[128,128]{1,0:T(8,128)S(1)}) custom-call(s32[2]{0:T(128)} %pad_add_fusion.where_ref, bf16[4,736,128]{2,1,0:T(8,128)(2,1)S(1)} %all-to-all-done.in_ref, bf16[256,4096]{1,0:T(8,128)(2,1)} %w_ref.3, bf16[128,2048]{1,0:T(8,128)(2,1)S(1)} %collective-permute-done.same_ref, ...), custom_call_target="tpu_custom_call" | custom-call | flops 400000000 | bytes 4000000 | tf_op jit(solution)/shard_map/pallas_call | solution.py:399
  33.4 7.7 %all-to-all-start.1 = ((bf16[32,8,1152]{2,1,0:T(8,128)(2,1)}), bf16[32,8,1152]{2,1,0:T(8,128)(2,1)S(1)}, u32[]{:S(2)}, u32[]{:S(2)}) async-start(bf16[32,8,1152]{2,1,0:T(8,128)(2,1)} %get-tuple-element.15), calls=%async_computation.1 | async-start | bytes 1179648 | tf_op jit(solution)/shard_map/all_to_all | solution.py:406
  41.2 2.9 %shard_map.187 = (bf16[384,128]{1,0:T(8,128)(2,1)S(1)}, bf16[384,128]{1,0:T(8,128)(2,1)S(1)}, bf16[384,128]{1,0:T(8,128)(2,1)S(1)}, bf16[384,128]{1,0:T(8,128)(2,1)S(1)}) custom-call(s32[2]{0:T(128)} %pad_add_fusion.where_ref, s32[2]{0:T(128)} %len_ref.1, s32[2]{0:T(128)} %acc_ref.1, bf16[4,736,128]{2,1,0:T(8,128)(2,1)S(1)} %all-to-all-done.in_ref, ...), custom_call_target="tpu_custom_call" | custom-call | tf_op jit(solution)/shard_map/pallas_call | solution.py:407
  44.1 3.7 %collective-permute-start.2 = (bf16[384,128]{1,0:T(8,128)(2,1)S(1)}, bf16[384,128]{1,0:T(8,128)(2,1)S(1)}, u32[]{:S(2)}, u32[]{:S(2)}) collective-permute-start(bf16[384,128]{1,0:T(8,128)(2,1)S(1)} %get-tuple-element.18), channel_id=1, source_target_pairs={{0,1},{1,2},{2,3},{3,0},{4,5},{5,6},{6,7},{7,4},{8,9},{9,10},{10,1... | collective-permute-start | bytes 294920 | tf_op jit(solution)/shard_map/ppermute | solution.py:426
  47.8 4.6 %collective-permute-start.3 = (bf16[384,128]{1,0:T(8,128)(2,1)S(1)}, bf16[384,128]{1,0:T(8,128)(2,1)S(1)}, u32[]{:S(2)}, u32[]{:S(2)}) collective-permute-start(bf16[384,128]{1,0:T(8,128)(2,1)S(1)} %get-tuple-element.19), channel_id=1, source_target_pairs={{0,2},{1,3},{2,0},{3,1},{4,6},{5,7},{6,4},{7,5},{8,10},{9,11},{10,... | collective-permute-start | bytes 294920 | tf_op jit(solution)/shard_map/ppermute | solution.py:426
  52.4 3.4 %collective-permute-start.4 = (bf16[384,128]{1,0:T(8,128)(2,1)S(1)}, bf16[384,128]{1,0:T(8,128)(2,1)S(1)}, u32[]{:S(2)}, u32[]{:S(2)}) collective-permute-start(bf16[384,128]{1,0:T(8,128)(2,1)S(1)} %get-tuple-element.20), channel_id=1, source_target_pairs={{0,3},{1,0},{2,1},{3,2},{4,7},{5,4},{6,5},{7,6},{8,11},{9,8},{10,9... | collective-permute-start | bytes 294920 | tf_op jit(solution)/shard_map/ppermute | solution.py:426
  55.8 0.0 collective-permute-done.2.next_ref
  55.8 2.2 %collective-permute-done.3.across_ref = bf16[384,128]{1,0:T(8,128)(2,1)S(1)} collective-permute-done((bf16[384,128]{1,0:T(8,128)(2,1)S(1)}, bf16[384,128]{1,0:T(8,128)(2,1)S(1)}, u32[]{:S(2)}, u32[]{:S(2)}) %collective-permute-start.3) | collective-permute-done | bytes 98336 | tf_op jit(solution)/shard_map/ppermute | solution.py:426
  58.0 0.9 %collective-permute-done.4.last_ref = bf16[384,128]{1,0:T(8,128)(2,1)S(1)} collective-permute-done((bf16[384,128]{1,0:T(8,128)(2,1)S(1)}, bf16[384,128]{1,0:T(8,128)(2,1)S(1)}, u32[]{:S(2)}, u32[]{:S(2)}) %collective-permute-start.4) | collective-permute-done | bytes 98336 | tf_op jit(solution)/shard_map/ppermute | solution.py:426
  58.9 1.7 %shard_map.188 = (bf16[2,16,512]{2,1,0:T(8,128)(2,1)}, bf16[2,16,32,64]{3,2,1,0:T(8,128)(2,1)}) custom-call(s32[2]{0:T(128)} %pad_add_fusion.where_ref, bf16[384,128]{1,0:T(8,128)(2,1)S(1)} %get-tuple-element.17.near_ref, bf16[384,128]{1,0:T(8,128)(2,1)S(1)} %collective-permute-done.2.next_ref, bf16[384,128]{1,0:T(8,128)(2,1)S(1)} %collective-permute-done.3.across_ref, ...), custom_call_target="tpu_custom_call" | custom-call | tf_op jit(solution)/shard_map/pallas_call | solution.py:429
  60.7 0.0 all-to-all-done.1.in_ref
  60.7 1.4 %shard_map.186 = bf16[2,2,4096]{2,1,0:T(2,128)(2,1)} custom-call(s32[2]{0:T(128)} %pad_add_fusion.where_ref, bf16[32,8,1152]{2,1,0:T(8,128)(2,1)S(1)} %all-to-all-done.1.in_ref), custom_call_target="tpu_custom_call" | custom-call | flops 1000000 | bytes 1500000 | tf_op jit(solution)/shard_map/pallas_call | solution.py:435
Async XLA Ops:
  0.6 22.3 %copy-start.1 = (f32[16]{0:T(128)S(1)}, f32[16]{0:T(128)}, u32[]{:S(2)}) copy-start(f32[16]{0:T(128)} %param.22) | copy-start | bytes 196
  0.6 22.3 %copy-start.2 = (f32[16]{0:T(128)S(1)}, f32[16]{0:T(128)}, u32[]{:S(2)}) copy-start(f32[16]{0:T(128)} %param.23) | copy-start | bytes 196
  0.7 23.1 %copy-start = (f32[1024]{0:T(1024)S(1)}, f32[1024]{0:T(1024)}, u32[]{:S(2)}) copy-start(f32[1024]{0:T(1024)} %param.24) | copy-start | bytes 12292
  4.2 16.7 %collective-permute-start = (bf16[128,2048]{1,0:T(8,128)(2,1)S(1)}, bf16[128,2048]{1,0:T(8,128)(2,1)S(1)}, u32[]{:S(2)}, u32[]{:S(2)}) collective-permute-start(bf16[128,2048]{1,0:T(8,128)(2,1)S(1)} %get-tuple-element.14), channel_id=1, source_target_pairs={{0,1},{1,0},{2,3},{3,2},{4,5},{5,4},{6,7},{7,6},{8,9},{9,8},{10,11... | collective-permute-start | bytes 1572872 | tf_op jit(solution)/shard_map/ppermute | solution.py:391
  7.7 22.4 %all-to-all-start = ((bf16[4,736,128]{2,1,0:T(8,128)(2,1)}), bf16[4,736,128]{2,1,0:T(8,128)(2,1)S(1)}, u32[]{:S(2)}, u32[]{:S(2)}) async-start(bf16[4,736,128]{2,1,0:T(8,128)(2,1)} %get-tuple-element.13), calls=%async_computation | async-start | bytes 1507328 | tf_op jit(solution)/shard_map/all_to_all | solution.py:393
  21.0 9.1 %collective-permute-start.1 = (bf16[128,2048]{1,0:T(8,128)(2,1)S(1)}, bf16[128,2048]{1,0:T(8,128)(2,1)S(1)}, u32[]{:S(2)}, u32[]{:S(2)}) collective-permute-start(bf16[128,2048]{1,0:T(8,128)(2,1)S(1)} %collective-permute-done.same_ref), channel_id=1, source_target_pairs={{0,32},{32,0},{64,96},{96,64},{128,160},{160,128},{192,224},{224,1... | collective-permute-start | bytes 1572872 | tf_op jit(solution)/shard_map/ppermute | solution.py:392
  33.4 27.2 %all-to-all-start.1 = ((bf16[32,8,1152]{2,1,0:T(8,128)(2,1)}), bf16[32,8,1152]{2,1,0:T(8,128)(2,1)S(1)}, u32[]{:S(2)}, u32[]{:S(2)}) async-start(bf16[32,8,1152]{2,1,0:T(8,128)(2,1)} %get-tuple-element.15), calls=%async_computation.1 | async-start | bytes 1179648 | tf_op jit(solution)/shard_map/all_to_all | solution.py:406
  44.1 11.7 %collective-permute-start.2 = (bf16[384,128]{1,0:T(8,128)(2,1)S(1)}, bf16[384,128]{1,0:T(8,128)(2,1)S(1)}, u32[]{:S(2)}, u32[]{:S(2)}) collective-permute-start(bf16[384,128]{1,0:T(8,128)(2,1)S(1)} %get-tuple-element.18), channel_id=1, source_target_pairs={{0,1},{1,2},{2,3},{3,0},{4,5},{5,6},{6,7},{7,4},{8,9},{9,10},{10,1... | collective-permute-start | bytes 294920 | tf_op jit(solution)/shard_map/ppermute | solution.py:426
  47.8 10.2 %collective-permute-start.3 = (bf16[384,128]{1,0:T(8,128)(2,1)S(1)}, bf16[384,128]{1,0:T(8,128)(2,1)S(1)}, u32[]{:S(2)}, u32[]{:S(2)}) collective-permute-start(bf16[384,128]{1,0:T(8,128)(2,1)S(1)} %get-tuple-element.19), channel_id=1, source_target_pairs={{0,2},{1,3},{2,0},{3,1},{4,6},{5,7},{6,4},{7,5},{8,10},{9,11},{10,... | collective-permute-start | bytes 294920 | tf_op jit(solution)/shard_map/ppermute | solution.py:426
  52.4 6.5 %collective-permute-start.4 = (bf16[384,128]{1,0:T(8,128)(2,1)S(1)}, bf16[384,128]{1,0:T(8,128)(2,1)S(1)}, u32[]{:S(2)}, u32[]{:S(2)}) collective-permute-start(bf16[384,128]{1,0:T(8,128)(2,1)S(1)} %get-tuple-element.20), channel_id=1, source_target_pairs={{0,3},{1,0},{2,1},{3,2},{4,7},{5,4},{6,5},{7,6},{8,11},{9,8},{10,9... | collective-permute-start | bytes 294920 | tf_op jit(solution)/shard_map/ppermute | solution.py:426

commit v4 on v2

--- a/solution.py
+++ b/solution.py
@@ -143,7 +143,9 @@
         upper = iota((16, 8, width), 1) < 4
         even = jnp.where(upper, a, b)
         odd = jnp.where(upper, b, a)
-        out_ref[:, :, lanes] = jnp.stack([even, odd], axis=1).reshape(32, 8, width).astype(BF16)
+        rows = jnp.stack([even, odd], axis=1).reshape(8, 4, 8, width).astype(BF16)
+        for to in range(4):
+            out_ref[to, :, :, lanes] = rows[:, to]
 
     store(dot(first, squares), dot(second, squares), pl.ds(HALF, 128), 128)
     fetch.wait()
@@ -252,15 +254,19 @@
                 state_ref[seq, src * 4 + block * 2 + 1] = pair[:, 64:]
 
 
+def stage_kernel(in_ref, after_ref, out_ref):
+    squares = in_ref[:, :, :, pl.ds(HALF, 128)].astype(F32).sum(axis=0)
+    scale = lax.rsqrt(squares * (1.0 / 1024.0) + EPSILON)
+    for chunk in range(HALF // 128):
+        lanes = pl.ds(chunk * 128, 128)
+        total = in_ref[:, :, :, lanes].astype(F32).sum(axis=0)
+        out_ref[:, :, lanes] = (total * scale).astype(BF16)
+
+
 def sum_kernel(where_ref, in_ref, out_ref):
-    squares = in_ref[:, :, pl.ds(HALF, 128)].astype(F32)
-    squares = squares.reshape(8, 4, 8, 128).sum(axis=1)
-    scale = lax.rsqrt(squares * (1.0 / 1024.0) + EPSILON)
     swapped = where_ref[0] % 2 == 1
     for chunk in range(HALF // 128):
-        part = in_ref[:, :, pl.ds(chunk * 128, 128)].astype(F32)
-        part = part.reshape(8, 4, 8, 128).sum(axis=1)
-        total = (part * scale).sum(axis=0)
+        total = in_ref[:, :, pl.ds(chunk * 128, 128)].astype(F32).sum(axis=0)
         flipped = jnp.concatenate([total[4:8], total[0:4]], axis=0)
         total = jnp.where(swapped, flipped, total).astype(BF16)
         for draft in range(2):
@@ -336,11 +342,11 @@
     shares, run = call(
         mixer_kernel,
         in_vmem(1) + [pl.BlockSpec(memory_space=pl.ANY)] + in_vmem(3),
-        [((32, 8, WIDTH), BF16, INTERPRET), ((128, 128), F32, INTERPRET)],
+        [((4, 8, 8, WIDTH), BF16, INTERPRET), ((128, 128), F32, INTERPRET)],
         (400000000, 4000000),
         scratch_shapes=[pltpu.VMEM((256, 4096), BF16), pltpu.SemaphoreType.DMA],
     )(arrived, out_weight, rate, skip, gain)
-    landed = lax.all_to_all(shares, ("head", "tok"), split_axis=0, concat_axis=0, tiled=True)
+    nearer = lax.all_to_all(shares, "tok", split_axis=0, concat_axis=0, tiled=True)
     back = call(
         attend_kernel,
         in_smem(3) + in_vmem(7),
@@ -359,6 +365,10 @@
         draft_token_keys,
         draft_values,
     )
+    (staged,) = call(
+        stage_kernel, in_vmem(2), [((8, 8, HALF), BF16, INTERPRET)], (2000000, 1500000)
+    )(held(nearer), held(back[0]))
+    landed = lax.all_to_all(staged, "head", split_axis=0, concat_axis=0, tiled=True)
     returned = [held(back[0])] + [
         held(lax.ppermute(back[k], "tok", [(i, (i + k) % 4) for i in range(4)]))
         for k in (1, 2, 3)

time: 57.9 us -> 62 us (1.071)
  starting transfers between devices: 24.6 us -> 26.7 us
  Pallas kernels: 10.8 us -> 11.6 us
  waiting for transfers between devices: 18.6 us -> 19.3 us
    all_to_all x1 -> x2, starting transfers between devices: 9.34 us -> 12.1 us  [the longest x1 7.11 us: body(): lax.all_to_all(staged, 'head', split_axis=0, concat_axis=0, tiled=True)]
    all_to_all x1 -> x2, waiting for transfers between devices: 8.82 us -> 10.3 us  [the longest x1 10.3 us: body(): lax.all_to_all(shares, 'tok', split_axis=0, concat_axis=0, tiled=True)]
    pallas_call x0 -> x1, Pallas kernels: none -> 0.86 us  [body(): call(stage_kernel, in_vmem(2), [((8, 8, HALF), BF16, INTERPRET)], (200000...]
    ppermute x3, waiting for transfers between devices: 4.82 us -> 4.02 us  [body(): lax.ppermute(back[k], 'tok', [(i, (i + k) % 4) for i in range(4)])]
    ppermute x3, starting transfers between devices: 10.4 us -> 9.8 us  [body(): lax.ppermute(back[k], 'tok', [(i, (i + k) % 4) for i in range(4)])]
  transfers between devices with their start and end apart: 5 -> 6, of which waited for: 4 -> 4; matrix products, arithmetic and copies ran while one was open for 5% -> 4% of each run, Pallas kernels for 7% -> 6%
where the time goes in v4:
time: 62 us; the launch traced here: 61 us
  starting transfers between devices  26.7 us (43%)
  waiting for transfers between devices  19.3 us (31%)
  Pallas kernels  11.6 us (19%)
  local copies, waits for them, and re-layouts  2.71 us (4%)
  between operations  0.7 us (1%)
    all_to_all x1, waiting for transfers between devices, body(): lax.all_to_all(shares, 'tok', split_axis=0, concat_axis=0, tiled=True)  10.3 us
    ppermute x3, starting transfers between devices, body(): lax.ppermute(back[k], 'tok', [(i, (i + k) % 4) for i in range(4)])  9.8 us
    all_to_all x1, starting transfers between devices, body(): lax.all_to_all(staged, 'head', split_axis=0, concat_axis=0, tiled=True)  7.11 us
    all_to_all x1, starting transfers between devices, body(): lax.all_to_all(shares, 'tok', split_axis=0, concat_axis=0, tiled=True)  4.96 us
    all_to_all x1, waiting for transfers between devices, body(): lax.all_to_all(packed, 'tok', split_axis=0, concat_axis=0, tiled=True)  4.96 us
    all_to_all x1, starting transfers between devices, body(): lax.all_to_all(packed, 'tok', split_axis=0, concat_axis=0, tiled=True)  4.82 us
    pallas_call x1, Pallas kernels, body(): call(mixer_kernel, in_vmem(1) + [pl.BlockSpec(memory_space=pl.ANY)] + in_...  4.26 us
    ppermute x3, waiting for transfers between devices, body(): lax.ppermute(back[k], 'tok', [(i, (i + k) % 4) for i in range(4)])  4.02 us
  transfers between devices with their start and end apart: 6, of which 4 were waited for; matrix products, arithmetic and copies ran while one was open for 4% of the time, Pallas kernels for 6%

profile of v4, /device:TPU:386, one launch (start us, length us, event | category | flops | bytes accessed | tf_op | source)
XLA Modules:
  0.0 61.0 jit_solution(15946371206951703365)
XLA Ops:
  0.6 0.0 copy-start
  0.6 0.0 copy-start.1
  0.7 1.9 %shard_map.184 = bf16[4,480,128]{2,1,0:T(8,128)(2,1)} custom-call(bf16[2,16,1024]{2,1,0:T(8,128)(2,1)} %x_ref.1, bf16[2,16,1024]{2,1,0:T(8,128)(2,1)} %z_ref.1, bf16[2,16,128]{2,1,0:T(8,128)(2,1)} %b_ref.1, bf16[2,16,128]{2,1,0:T(8,128)(2,1)} %c_ref.1, bf16[2,16,16]{2,1,0:T(8,128)(2,1)} %t_ref.1, bf16[2,16,32,64]{3,2,1,0:T(8,128)(2,1)} %bitcast.6, ...), custom_call_target="tpu_custom_call" | custom-call | bytes 1500000 | tf_op jit(solution)/shard_map/pallas_call | solution.py:328
  2.6 4.8 %all-to-all-start = ((bf16[4,480,128]{2,1,0:T(8,128)(2,1)}), bf16[4,480,128]{2,1,0:T(8,128)(2,1)S(1)}, u32[]{:S(2)}, u32[]{:S(2)}) async-start(bf16[4,480,128]{2,1,0:T(8,128)(2,1)} %shard_map.184), calls=%async_computation | async-start | bytes 983040 | tf_op jit(solution)/shard_map/all_to_all | solution.py:337
  7.4 0.0 copy-done
  7.4 0.1 dynamic_slice.9
  7.5 0.0 copy-done.1
  7.5 0.1 dynamic_slice.10
  7.5 0.1 broadcast_in_dim.3
  7.6 0.6 %reshape_reshape.3.skip_ref = f32[1,256]{1,0:T(1,128)} reshape(f32[4,64]{1,0:T(4,128)S(1)} %broadcast_in_dim.3) | data formatting | bytes 2048 | tf_op jit(solution)/shard_map/reshape;reshape | solution.py:340
  8.3 1.3 %dynamic_slice.11 = f32[256]{0:T(256)} dynamic-slice(f32[1024]{0:T(1024)} %param.24, s32[]{:T(128)S(6)} %select_n.8), dynamic_slice_sizes={256} | dynamic-slice | bytes 2052 | tf_op jit(solution)/shard_map/dynamic_slice | solution.py:341
  9.6 0.5 pad_bitcast_fusion.rate_ref
  10.1 5.0 %all-to-all-done.in_ref = bf16[4,480,128]{2,1,0:T(8,128)(2,1)S(1)} async-done(((bf16[4,480,128]{2,1,0:T(8,128)(2,1)}), bf16[4,480,128]{2,1,0:T(8,128)(2,1)S(1)}, u32[]{:S(2)}, u32[]{:S(2)}) %all-to-all-start) | async-done | bytes 491552 | tf_op jit(solution)/shard_map/all_to_all | solution.py:337
  15.1 4.3 %shard_map.185 = (bf16[4,8,8,2176]{3,2,1,0:T(8,128)(2,1)}, f32[128,128]{1,0:T(8,128)S(1)}) custom-call(bf16[4,480,128]{2,1,0:T(8,128)(2,1)S(1)} %all-to-all-done.in_ref, bf16[256,4096]{1,0:T(8,128)(2,1)} %w_ref.1, f32[1,128]{1,0:T(1,128)} %pad_bitcast_fusion.rate_ref, f32[1,256]{1,0:T(1,128)} %reshape_reshape.3.skip_ref, f32[1,256]{1,0:T(1,128)} %bitcast.7), custom_call_target="tpu_custom_call" | custom-call | flops 400000000 | bytes 4000000 | tf_op jit(solution)/shard_map/pallas_call | solution.py:342
  19.3 5.0 %all-to-all-start.1 = ((bf16[4,8,8,2176]{3,2,1,0:T(8,128)(2,1)}), bf16[4,8,8,2176]{3,2,1,0:T(8,128)(2,1)S(1)}, u32[]{:S(2)}, u32[]{:S(2)}) async-start(bf16[4,8,8,2176]{3,2,1,0:T(8,128)(2,1)} %get-tuple-element.11), calls=%async_computation.1 | async-start | bytes 2228224 | tf_op jit(solution)/shard_map/all_to_all | solution.py:349
  24.3 2.8 %shard_map.186 = (bf16[384,128]{1,0:T(8,128)(2,1)S(1)}, bf16[384,128]{1,0:T(8,128)(2,1)S(1)}, bf16[384,128]{1,0:T(8,128)(2,1)S(1)}, bf16[384,128]{1,0:T(8,128)(2,1)S(1)}) custom-call(s32[1]{0:T(128)} %bitcast.where_ref, s32[2]{0:T(128)} %len_ref.1, s32[2]{0:T(128)} %acc_ref.1, bf16[4,480,128]{2,1,0:T(8,128)(2,1)S(1)} %all-to-all-done.in_ref, ...), custom_call_target="tpu_custom_call" | custom-call | tf_op jit(solution)/shard_map/pallas_call | solution.py:350
  27.1 10.3 %all-to-all-done.1.in_ref = bf16[4,8,8,2176]{3,2,1,0:T(8,128)(2,1)S(1)} async-done(((bf16[4,8,8,2176]{3,2,1,0:T(8,128)(2,1)}), bf16[4,8,8,2176]{3,2,1,0:T(8,128)(2,1)S(1)}, u32[]{:S(2)}, u32[]{:S(2)}) %all-to-all-start.1) | async-done | bytes 1114144 | tf_op jit(solution)/shard_map/all_to_all | solution.py:349
  37.4 0.9 %shard_map.187 = bf16[8,8,2048]{2,1,0:T(8,128)(2,1)} custom-call(bf16[4,8,8,2176]{3,2,1,0:T(8,128)(2,1)S(1)} %all-to-all-done.1.in_ref, bf16[384,128]{1,0:T(8,128)(2,1)S(1)} %get-tuple-element.13.after_ref.near_ref), custom_call_target="tpu_custom_call" | custom-call | flops 2000000 | bytes 1500000 | tf_op jit(solution)/shard_map/pallas_call | solution.py:368
  38.3 7.1 %all-to-all-start.2 = ((bf16[8,8,2048]{2,1,0:T(8,128)(2,1)}), bf16[8,8,2048]{2,1,0:T(8,128)(2,1)S(1)}, u32[]{:S(2)}, u32[]{:S(2)}) async-start(bf16[8,8,2048]{2,1,0:T(8,128)(2,1)} %shard_map.187), calls=%async_computation.2 | async-start | bytes 524288 | tf_op jit(solution)/shard_map/all_to_all | solution.py:371
  45.4 1.9 %collective-permute-start = (bf16[384,128]{1,0:T(8,128)(2,1)S(1)}, bf16[384,128]{1,0:T(8,128)(2,1)S(1)}, u32[]{:S(2)}, u32[]{:S(2)}) collective-permute-start(bf16[384,128]{1,0:T(8,128)(2,1)S(1)} %get-tuple-element.14), channel_id=1, source_target_pairs={{0,1},{1,2},{2,3},{3,0},{4,5},{5,6},{6,7},{7,4},{8,9},{9,10},{10,1... | collective-permute-start | bytes 294920 | tf_op jit(solution)/shard_map/ppermute | solution.py:373
  47.3 5.4 %collective-permute-start.1 = (bf16[384,128]{1,0:T(8,128)(2,1)S(1)}, bf16[384,128]{1,0:T(8,128)(2,1)S(1)}, u32[]{:S(2)}, u32[]{:S(2)}) collective-permute-start(bf16[384,128]{1,0:T(8,128)(2,1)S(1)} %get-tuple-element.15), channel_id=1, source_target_pairs={{0,2},{1,3},{2,0},{3,1},{4,6},{5,7},{6,4},{7,5},{8,10},{9,11},{10,... | collective-permute-start | bytes 294920 | tf_op jit(solution)/shard_map/ppermute | solution.py:373
  52.7 2.5 %collective-permute-start.2 = (bf16[384,128]{1,0:T(8,128)(2,1)S(1)}, bf16[384,128]{1,0:T(8,128)(2,1)S(1)}, u32[]{:S(2)}, u32[]{:S(2)}) collective-permute-start(bf16[384,128]{1,0:T(8,128)(2,1)S(1)} %get-tuple-element.16), channel_id=1, source_target_pairs={{0,3},{1,0},{2,1},{3,2},{4,7},{5,4},{6,5},{7,6},{8,11},{9,8},{10,9... | collective-permute-start | bytes 294920 | tf_op jit(solution)/shard_map/ppermute | solution.py:373
  55.2 0.0 collective-permute-done.next_ref
  55.2 0.2 collective-permute-done.1.across_ref
  55.4 3.8 %collective-permute-done.2.last_ref = bf16[384,128]{1,0:T(8,128)(2,1)S(1)} collective-permute-done((bf16[384,128]{1,0:T(8,128)(2,1)S(1)}, bf16[384,128]{1,0:T(8,128)(2,1)S(1)}, u32[]{:S(2)}, u32[]{:S(2)}) %collective-permute-start.2) | collective-permute-done | bytes 98336 | tf_op jit(solution)/shard_map/ppermute | solution.py:373
  59.2 1.1 %shard_map.189 = (bf16[2,16,512]{2,1,0:T(8,128)(2,1)}, bf16[2,16,32,64]{3,2,1,0:T(8,128)(2,1)}) custom-call(s32[1]{0:T(128)} %bitcast.where_ref, bf16[384,128]{1,0:T(8,128)(2,1)S(1)} %get-tuple-element.13.after_ref.near_ref, bf16[384,128]{1,0:T(8,128)(2,1)S(1)} %collective-permute-done.next_ref, bf16[384,128]{1,0:T(8,128)(2,1)S(1)} %collective-permute-done.1.across_ref, ...), custom_call_target="tpu_custom_call" | custom-call | tf_op jit(solution)/shard_map/pallas_call | solution.py:376
  60.3 0.0 all-to-all-done.2.in_ref
  60.3 0.7 %shard_map.188 = bf16[2,2,4096]{2,1,0:T(2,128)(2,1)} custom-call(s32[1]{0:T(128)} %bitcast.where_ref, bf16[8,8,2048]{2,1,0:T(8,128)(2,1)S(1)} %all-to-all-done.2.in_ref), custom_call_target="tpu_custom_call" | custom-call | flops 1000000 | bytes 1500000 | tf_op jit(solution)/shard_map/pallas_call | solution.py:382
Async XLA Ops:
  0.6 6.8 %copy-start = (f32[16]{0:T(128)S(1)}, f32[16]{0:T(128)}, u32[]{:S(2)}) copy-start(f32[16]{0:T(128)} %param.22) | copy-start | bytes 196
  0.6 6.8 %copy-start.1 = (f32[16]{0:T(128)S(1)}, f32[16]{0:T(128)}, u32[]{:S(2)}) copy-start(f32[16]{0:T(128)} %param.23) | copy-start | bytes 196
  2.6 12.5 %all-to-all-start = ((bf16[4,480,128]{2,1,0:T(8,128)(2,1)}), bf16[4,480,128]{2,1,0:T(8,128)(2,1)S(1)}, u32[]{:S(2)}, u32[]{:S(2)}) async-start(bf16[4,480,128]{2,1,0:T(8,128)(2,1)} %shard_map.184), calls=%async_computation | async-start | bytes 983040 | tf_op jit(solution)/shard_map/all_to_all | solution.py:337
  19.3 18.1 %all-to-all-start.1 = ((bf16[4,8,8,2176]{3,2,1,0:T(8,128)(2,1)}), bf16[4,8,8,2176]{3,2,1,0:T(8,128)(2,1)S(1)}, u32[]{:S(2)}, u32[]{:S(2)}) async-start(bf16[4,8,8,2176]{3,2,1,0:T(8,128)(2,1)} %get-tuple-element.11), calls=%async_computation.1 | async-start | bytes 2228224 | tf_op jit(solution)/shard_map/all_to_all | solution.py:349
  38.3 22.0 %all-to-all-start.2 = ((bf16[8,8,2048]{2,1,0:T(8,128)(2,1)}), bf16[8,8,2048]{2,1,0:T(8,128)(2,1)S(1)}, u32[]{:S(2)}, u32[]{:S(2)}) async-start(bf16[8,8,2048]{2,1,0:T(8,128)(2,1)} %shard_map.187), calls=%async_computation.2 | async-start | bytes 524288 | tf_op jit(solution)/shard_map/all_to_all | solution.py:371
  45.4 9.8 %collective-permute-start = (bf16[384,128]{1,0:T(8,128)(2,1)S(1)}, bf16[384,128]{1,0:T(8,128)(2,1)S(1)}, u32[]{:S(2)}, u32[]{:S(2)}) collective-permute-start(bf16[384,128]{1,0:T(8,128)(2,1)S(1)} %get-tuple-element.14), channel_id=1, source_target_pairs={{0,1},{1,2},{2,3},{3,0},{4,5},{5,6},{6,7},{7,4},{8,9},{9,10},{10,1... | collective-permute-start | bytes 294920 | tf_op jit(solution)/shard_map/ppermute | solution.py:373
  47.3 8.1 %collective-permute-start.1 = (bf16[384,128]{1,0:T(8,128)(2,1)S(1)}, bf16[384,128]{1,0:T(8,128)(2,1)S(1)}, u32[]{:S(2)}, u32[]{:S(2)}) collective-permute-start(bf16[384,128]{1,0:T(8,128)(2,1)S(1)} %get-tuple-element.15), channel_id=1, source_target_pairs={{0,2},{1,3},{2,0},{3,1},{4,6},{5,7},{6,4},{7,5},{8,10},{9,11},{10,... | collective-permute-start | bytes 294920 | tf_op jit(solution)/shard_map/ppermute | solution.py:373
  52.7 6.5 %collective-permute-start.2 = (bf16[384,128]{1,0:T(8,128)(2,1)S(1)}, bf16[384,128]{1,0:T(8,128)(2,1)S(1)}, u32[]{:S(2)}, u32[]{:S(2)}) collective-permute-start(bf16[384,128]{1,0:T(8,128)(2,1)S(1)} %get-tuple-element.16), channel_id=1, source_target_pairs={{0,3},{1,0},{2,1},{3,2},{4,7},{5,4},{6,5},{7,6},{8,11},{9,8},{10,9... | collective-permute-start | bytes 294920 | tf_op jit(solution)/shard_map/ppermute | solution.py:373

commit v5 on v2

--- a/solution.py
+++ b/solution.py
@@ -22,7 +22,7 @@
 Q_ROW = 192
 S_ROW = 320
 T_ROW = 448
-ROWS = 480
+ROWS = 464
 
 N_ROW = 0
 M_ROW = 128
@@ -45,28 +45,40 @@
     return lax.broadcasted_iota(jnp.int32, shape, dim)
 
 
-def pack_kernel(x_ref, z_ref, b_ref, c_ref, t_ref, s_ref, q_ref, out_ref):
-    for seq in range(2):
-        bs = b_ref[seq]
-        cs = c_ref[seq]
-        steps = t_ref[seq]
-        for to in range(4):
+def pack_kernel(x_ref, z_ref, b_ref, c_ref, t_ref, s_ref, q_ref, out_ref, buf, sems):
+    pad = jnp.zeros((16, 60), F32)
+    copies = []
+    for to in range(4):
+        for seq in range(2):
             for block in range(2):
                 lanes = pl.ds(to * 256 + block * 128, 128)
                 row = (seq * 2 + block) * 16
-                out_ref[to, pl.ds(X_ROW + row, 16), :] = x_ref[seq, :, lanes]
-                out_ref[to, pl.ds(Z_ROW + row, 16), :] = z_ref[seq, :, lanes]
+                buf[to, pl.ds(X_ROW + row, 16), :] = x_ref[seq, :, lanes]
+                buf[to, pl.ds(Z_ROW + row, 16), :] = z_ref[seq, :, lanes]
                 head = to * 4 + block * 2
                 pair = jnp.concatenate([s_ref[seq, head], s_ref[seq, head + 1]], axis=1)
-                out_ref[to, pl.ds(S_ROW + (seq * 2 + block) * 32, 32), :] = pair
-            out_ref[to, pl.ds(B_ROW + seq * 16, 16), :] = bs
-            out_ref[to, pl.ds(C_ROW + seq * 16, 16), :] = cs
+                buf[to, pl.ds(S_ROW + (seq * 2 + block) * 32, 32), :] = pair
+            buf[to, pl.ds(B_ROW + seq * 16, 16), :] = b_ref[seq]
+            buf[to, pl.ds(C_ROW + seq * 16, 16), :] = c_ref[seq]
             for head in range(4):
                 row = Q_ROW + (seq * 4 + head) * 16
-                out_ref[to, pl.ds(row, 16), :] = q_ref[seq, :, pl.ds(head * 128, 128)]
-            own = steps[:, to * 4 : to * 4 + 4].astype(F32)
-            own = jnp.concatenate([own, jnp.zeros((16, 124), F32)], axis=1)
-            out_ref[to, pl.ds(T_ROW + seq * 16, 16), :] = own.astype(BF16)
+                buf[to, pl.ds(row, 16), :] = q_ref[seq, :, pl.ds(head * 128, 128)]
+        own = [t_ref[seq].astype(F32)[:, to * 4 : to * 4 + 4] for seq in range(2)]
+        lanes = jnp.concatenate([own[0], pad, own[1], pad], axis=1)
+        buf[to, pl.ds(T_ROW, 16), :] = lanes.astype(BF16)
+        copy = pltpu.make_async_copy(buf.at[to], out_ref.at[to], sems.at[to])
+        copy.start()
+        copies.append(copy)
+    for copy in copies:
+        copy.wait()
+
+
+def all_steps(in_ref):
+    both_lanes = jnp.concatenate(
+        [in_ref[src, pl.ds(T_ROW, 16), :].astype(F32) for src in range(4)], axis=0
+    )
+    swapped = jnp.concatenate([both_lanes[:, 64:], both_lanes[:, :64]], axis=1)
+    return jnp.concatenate([both_lanes, swapped], axis=0)
 
 
 def both(in_ref, first, stride):
@@ -77,7 +89,7 @@
 
 
 def mixer_kernel(
-    in_ref, w_ref, rate_ref, skip_ref, gain_ref, out_ref, run_ref, w_buf, sem
+    in_ref, w_ref, rate_ref, skip_ref, gain_ref, out_ref, run_ref, w_buf, o_buf, sem, out_sems
 ):
     fetch = pltpu.make_async_copy(w_ref, w_buf, sem)
     fetch.start()
@@ -86,13 +98,13 @@
     low = col < 64
     causal = (row >= col) & ((row >= 64) == (col >= 64))
     ones = jnp.where(causal, 1.0, 0.0).astype(BF16)
-    steps = both(in_ref, T_ROW, 16)
-    total = dot(ones, steps)
+    steps = all_steps(in_ref)
+    total = dot(ones, steps.astype(BF16))
     rate = rate_ref[...]
     run = -total * rate
     run_ref[...] = run
     run_t = run.T
-    steps_t = steps.astype(F32).T
+    steps_t = steps.T
     grow = jnp.exp(run)
     inflow = both(in_ref, B_ROW, 16)
     readout = both(in_ref, C_ROW, 16)
@@ -137,21 +149,35 @@
     lhs_b = dot(second, act).astype(BF16)
     squares = jnp.broadcast_to(squares, (128, 128)).astype(BF16)
 
-    def store(a, b, lanes, width):
+    def store(a, b, first, width):
+        lanes = pl.ds(first, width)
         a = a.reshape(16, 8, width)
         b = b.reshape(16, 8, width)
         upper = iota((16, 8, width), 1) < 4
         even = jnp.where(upper, a, b)
         odd = jnp.where(upper, b, a)
-        out_ref[:, :, lanes] = jnp.stack([even, odd], axis=1).reshape(32, 8, width).astype(BF16)
-
-    store(dot(first, squares), dot(second, squares), pl.ds(HALF, 128), 128)
+        o_buf[:, :, lanes] = jnp.stack([even, odd], axis=1).reshape(32, 8, width).astype(BF16)
+
+    def leave(first, width, slot):
+        lanes = pl.ds(first, width)
+        copy = pltpu.make_async_copy(
+            o_buf.at[:, :, lanes], out_ref.at[:, :, lanes], out_sems.at[slot]
+        )
+        copy.start()
+        return copy
+
+    store(dot(first, squares), dot(second, squares), HALF, 128)
+    leaving = [leave(HALF, 128, 4)]
     fetch.wait()
     for chunk in range(8):
         lanes = pl.ds(chunk * 256, 256)
         a = dot(lhs_a, w_buf[:, lanes])
         b = dot(lhs_b, w_buf[:, pl.ds(HALF + chunk * 256, 256)])
-        store(a, b, lanes, 256)
+        store(a, b, chunk * 256, 256)
+        if chunk % 2:
+            leaving.append(leave((chunk - 1) * 256, 512, chunk // 2))
+    for copy in leaving:
+        copy.wait()
 
 
 def attend_kernel(
@@ -202,7 +228,7 @@
     row = iota((128, 128), 0)
     low = iota((128, 128), 1) < 64
     low_row = iota((1, 128), 1) < 64
-    steps = both(in_ref, T_ROW, 16).astype(F32)
+    steps = all_steps(in_ref)
     inflow_t = both(in_ref, B_ROW, 16).astype(F32).T.astype(BF16)
     run = run_ref[...]
     rate = rate_ref[...]
@@ -252,11 +278,11 @@
                 state_ref[seq, src * 4 + block * 2 + 1] = pair[:, 64:]
 
 
-def sum_kernel(where_ref, in_ref, out_ref):
+def sum_kernel(in_ref, out_ref):
     squares = in_ref[:, :, pl.ds(HALF, 128)].astype(F32)
     squares = squares.reshape(8, 4, 8, 128).sum(axis=1)
     scale = lax.rsqrt(squares * (1.0 / 1024.0) + EPSILON)
-    swapped = where_ref[0] % 2 == 1
+    swapped = lax.axis_index("tok") % 2 == 1
     for chunk in range(HALF // 128):
         part = in_ref[:, :, pl.ds(chunk * 128, 128)].astype(F32)
         part = part.reshape(8, 4, 8, 128).sum(axis=1)
@@ -283,12 +309,12 @@
     return pltpu.with_memory_space_constraint(array, pltpu.VMEM)
 
 
-def call(kernel, ins, outs, cost, **kwargs):
+def call(kernel, ins, outs, cost, out_specs=None, **kwargs):
     flops, moved = cost
     return pl.pallas_call(
         kernel,
         in_specs=ins,
-        out_specs=tuple(in_vmem(len(outs))),
+        out_specs=tuple(in_vmem(len(outs))) if out_specs is None else out_specs,
         out_shape=tuple(
             (jax.ShapeDtypeStruct if plain else pltpu.VMEM)(s, d) for s, d, plain in outs
         ),
@@ -319,7 +345,14 @@
 ):
     tok = lax.axis_index("tok")
     where = tok.reshape(1).astype(jnp.int32)
-    (packed,) = call(pack_kernel, in_vmem(7), [((4, ROWS, 128), BF16, INTERPRET)], (0, 1500000))(
+    (packed,) = call(
+        pack_kernel,
+        in_vmem(7),
+        [((4, ROWS, 128), BF16, True)],
+        (0, 1500000),
+        out_specs=(pl.BlockSpec(memory_space=pl.ANY),),
+        scratch_shapes=[pltpu.VMEM((4, ROWS, 128), BF16), pltpu.SemaphoreType.DMA((4,))],
+    )(
         mamba_input,
         gate_input,
         in_b,
@@ -336,10 +369,16 @@
     shares, run = call(
         mixer_kernel,
         in_vmem(1) + [pl.BlockSpec(memory_space=pl.ANY)] + in_vmem(3),
-        [((32, 8, WIDTH), BF16, INTERPRET), ((128, 128), F32, INTERPRET)],
+        [((32, 8, WIDTH), BF16, True), ((128, 128), F32, INTERPRET)],
         (400000000, 4000000),
-        scratch_shapes=[pltpu.VMEM((256, 4096), BF16), pltpu.SemaphoreType.DMA],
-    )(arrived, out_weight, rate, skip, gain)
+        out_specs=(pl.BlockSpec(memory_space=pl.ANY), *in_vmem(1)),
+        scratch_shapes=[
+            pltpu.VMEM((256, 4096), BF16),
+            pltpu.VMEM((32, 8, WIDTH), BF16),
+            pltpu.SemaphoreType.DMA,
+            pltpu.SemaphoreType.DMA((5,)),
+        ],
+    )(arrived, out_weight, held(rate), held(skip), held(gain))
     landed = lax.all_to_all(shares, ("head", "tok"), split_axis=0, concat_axis=0, tiled=True)
     back = call(
         attend_kernel,
@@ -353,7 +392,7 @@
         accepted,
         arrived,
         held(run),
-        rate,
+        held(rate),
         cached_key_rows,
         cache_values,
         draft_token_keys,
@@ -370,8 +409,8 @@
         (0, 0),
     )(where, *returned)
     (mamba_out,) = call(
-        sum_kernel, in_smem(1) + in_vmem(1), [((2, 2, 4096), BF16, True)], (1000000, 1500000)
-    )(where, held(landed))
+        sum_kernel, in_vmem(1), [((2, 2, 4096), BF16, True)], (1000000, 1500000)
+    )(held(landed))
     return (mamba_out, attn_context, jnp.swapaxes(state_t, 2, 3))
 
 

time: 57.9 us -> 57 us (0.984)
  local copies, waits for them, and re-layouts: 2.71 us -> 1.08 us
  waiting for transfers between devices: 18.6 us -> 20 us
  Pallas kernels: 10.8 us -> 10.1 us
    all_to_all x1, waiting for transfers between devices: 4.96 us -> 6.42 us  [body(): lax.all_to_all(packed, 'tok', split_axis=0, concat_axis=0, tiled=True)]
    pallas_call x1, Pallas kernels: 4.25 us -> 3.46 us  [body(): call(mixer_kernel, in_vmem(1) + [pl.BlockSpec(memory_space=pl.ANY)] + in_...]
  transfers between devices with their start and end apart: 5 -> 5, of which waited for: 4 -> 4; matrix products, arithmetic and copies ran while one was open for 5% -> 2% of each run, Pallas kernels for 7% -> 7%
where the time goes in v5:
time: 57 us; the launch traced here: 56.5 us
  starting transfers between devices  24.6 us (43%)
  waiting for transfers between devices  20 us (35%)
  Pallas kernels  10.1 us (18%)
  local copies, waits for them, and re-layouts  1.08 us (2%)
  between operations  0.72 us (1%)
    ppermute x3, starting transfers between devices, body(): lax.ppermute(back[k], 'tok', [(i, (i + k) % 4) for i in range(4)])  10.4 us
    all_to_all x1, starting transfers between devices, body(): lax.all_to_all(shares, ('head', 'tok'), split_axis=0, concat_axis=0, tile...  9.33 us
    all_to_all x1, waiting for transfers between devices, body(): lax.all_to_all(shares, ('head', 'tok'), split_axis=0, concat_axis=0, tile...  8.77 us
    all_to_all x1, waiting for transfers between devices, body(): lax.all_to_all(packed, 'tok', split_axis=0, concat_axis=0, tiled=True)  6.42 us
    all_to_all x1, starting transfers between devices, body(): lax.all_to_all(packed, 'tok', split_axis=0, concat_axis=0, tiled=True)  4.84 us
    ppermute x3, waiting for transfers between devices, body(): lax.ppermute(back[k], 'tok', [(i, (i + k) % 4) for i in range(4)])  4.83 us
    pallas_call x1, Pallas kernels, body(): call(mixer_kernel, in_vmem(1) + [pl.BlockSpec(memory_space=pl.ANY)] + in_...  3.46 us
    pallas_call x1, Pallas kernels, body(): call(attend_kernel, in_smem(3) + in_vmem(7), [((BACK_ROWS, 128), BF16, IN...  2.84 us
  transfers between devices with their start and end apart: 5, of which 4 were waited for; matrix products, arithmetic and copies ran while one was open for 2% of the time, Pallas kernels for 7%

profile of v5, /device:TPU:386, one launch (start us, length us, event | category | flops | bytes accessed | tf_op | source)
XLA Modules:
  0.0 56.5 jit_solution(15818570341438194847)
XLA Ops:
  0.6 0.0 copy-start
  0.6 0.0 copy-start.1
  0.7 1.9 %shard_map.184 = bf16[4,464,128]{2,1,0:T(8,128)(2,1)} custom-call(bf16[2,16,1024]{2,1,0:T(8,128)(2,1)} %x_ref.1, bf16[2,16,1024]{2,1,0:T(8,128)(2,1)} %z_ref.1, bf16[2,16,128]{2,1,0:T(8,128)(2,1)} %b_ref.1, bf16[2,16,128]{2,1,0:T(8,128)(2,1)} %c_ref.1, bf16[2,16,16]{2,1,0:T(8,128)(2,1)} %t_ref.1, bf16[2,16,32,64]{3,2,1,0:T(8,128)(2,1)} %bitcast.7, ...), custom_call_target="tpu_custom_call" | custom-call | bytes 1500000 | tf_op jit(solution)/shard_map/pallas_call | solution.py:348
  2.6 4.8 %all-to-all-start = ((bf16[4,464,128]{2,1,0:T(8,128)(2,1)}), bf16[4,464,128]{2,1,0:T(8,128)(2,1)S(1)}, u32[]{:S(2)}, u32[]{:S(2)}) async-start(bf16[4,464,128]{2,1,0:T(8,128)(2,1)} %shard_map.184), calls=%async_computation | async-start | bytes 950272 | tf_op jit(solution)/shard_map/all_to_all | solution.py:364
  7.4 0.0 copy-done
  7.4 0.1 dynamic_slice.9
  7.5 0.0 copy-done.1
  7.5 0.1 dynamic_slice.10
  7.6 0.1 broadcast_in_dim.3
  7.6 0.1 reshape_reshape.3.skip_ref
  7.7 0.8 %dynamic_slice.11 = f32[256]{0:T(256)S(1)} dynamic-slice(f32[1024]{0:T(1024)} %param.24, s32[]{:T(128)S(6)} %select_n.8), dynamic_slice_sizes={256} | dynamic-slice | bytes 2052 | tf_op jit(solution)/shard_map/dynamic_slice | solution.py:368
  8.5 6.4 %all-to-all-done.in_ref = bf16[4,464,128]{2,1,0:T(8,128)(2,1)S(1)} async-done(((bf16[4,464,128]{2,1,0:T(8,128)(2,1)}), bf16[4,464,128]{2,1,0:T(8,128)(2,1)S(1)}, u32[]{:S(2)}, u32[]{:S(2)}) %all-to-all-start) | async-done | bytes 475168 | tf_op jit(solution)/shard_map/all_to_all | solution.py:364
  14.9 3.5 %shard_map.185 = (bf16[32,8,2176]{2,1,0:T(8,128)(2,1)}, f32[128,128]{1,0:T(8,128)S(1)}) custom-call(bf16[4,464,128]{2,1,0:T(8,128)(2,1)S(1)} %all-to-all-done.in_ref, bf16[256,4096]{1,0:T(8,128)(2,1)} %w_ref.1, f32[1,128]{1,0:T(1,128)S(1)} %pad_bitcast_fusion.rate_ref, f32[1,256]{1,0:T(1,128)S(1)} %reshape_reshape.3.skip_ref, f32[1,256]{1,0:T(1,128)S(1)} %bitcast.6), custom_call_target="tpu_custom_call" | custom-call | flops 400000000 | bytes 4000000 | tf_op jit(solution)/shard_map/pallas_call | solution.py:369
  18.4 9.3 %all-to-all-start.1 = ((bf16[32,8,2176]{2,1,0:T(8,128)(2,1)}), bf16[32,8,2176]{2,1,0:T(8,128)(2,1)S(1)}, u32[]{:S(2)}, u32[]{:S(2)}) async-start(bf16[32,8,2176]{2,1,0:T(8,128)(2,1)} %get-tuple-element.11), calls=%async_computation.1 | async-start | bytes 2228224 | tf_op jit(solution)/shard_map/all_to_all | solution.py:382
  27.7 2.8 %shard_map.187 = (bf16[384,128]{1,0:T(8,128)(2,1)S(1)}, bf16[384,128]{1,0:T(8,128)(2,1)S(1)}, bf16[384,128]{1,0:T(8,128)(2,1)S(1)}, bf16[384,128]{1,0:T(8,128)(2,1)S(1)}) custom-call(s32[1]{0:T(128)} %bitcast.3.where_ref, s32[2]{0:T(128)} %len_ref.1, s32[2]{0:T(128)} %acc_ref.1, bf16[4,464,128]{2,1,0:T(8,128)(2,1)S(1)} %all-to-all-done.in_ref, ...), custom_call_target="tpu_custom_call" | custom-call | tf_op jit(solution)/shard_map/pallas_call | solution.py:383
  30.6 3.4 %collective-permute-start = (bf16[384,128]{1,0:T(8,128)(2,1)S(1)}, bf16[384,128]{1,0:T(8,128)(2,1)S(1)}, u32[]{:S(2)}, u32[]{:S(2)}) collective-permute-start(bf16[384,128]{1,0:T(8,128)(2,1)S(1)} %get-tuple-element.14), channel_id=1, source_target_pairs={{0,1},{1,2},{2,3},{3,0},{4,5},{5,6},{6,7},{7,4},{8,9},{9,10},{10,1... | collective-permute-start | bytes 294920 | tf_op jit(solution)/shard_map/ppermute | solution.py:402
  33.9 2.7 %collective-permute-start.1 = (bf16[384,128]{1,0:T(8,128)(2,1)S(1)}, bf16[384,128]{1,0:T(8,128)(2,1)S(1)}, u32[]{:S(2)}, u32[]{:S(2)}) collective-permute-start(bf16[384,128]{1,0:T(8,128)(2,1)S(1)} %get-tuple-element.15), channel_id=1, source_target_pairs={{0,2},{1,3},{2,0},{3,1},{4,6},{5,7},{6,4},{7,5},{8,10},{9,11},{10,... | collective-permute-start | bytes 294920 | tf_op jit(solution)/shard_map/ppermute | solution.py:402
  36.7 4.3 %collective-permute-start.2 = (bf16[384,128]{1,0:T(8,128)(2,1)S(1)}, bf16[384,128]{1,0:T(8,128)(2,1)S(1)}, u32[]{:S(2)}, u32[]{:S(2)}) collective-permute-start(bf16[384,128]{1,0:T(8,128)(2,1)S(1)} %get-tuple-element.16), channel_id=1, source_target_pairs={{0,3},{1,0},{2,1},{3,2},{4,7},{5,4},{6,5},{7,6},{8,11},{9,8},{10,9... | collective-permute-start | bytes 294920 | tf_op jit(solution)/shard_map/ppermute | solution.py:402
  41.0 0.0 collective-permute-done.next_ref
  41.0 3.1 %collective-permute-done.1.across_ref = bf16[384,128]{1,0:T(8,128)(2,1)S(1)} collective-permute-done((bf16[384,128]{1,0:T(8,128)(2,1)S(1)}, bf16[384,128]{1,0:T(8,128)(2,1)S(1)}, u32[]{:S(2)}, u32[]{:S(2)}) %collective-permute-start.1) | collective-permute-done | bytes 98336 | tf_op jit(solution)/shard_map/ppermute | solution.py:402
  44.2 1.7 %collective-permute-done.2.last_ref = bf16[384,128]{1,0:T(8,128)(2,1)S(1)} collective-permute-done((bf16[384,128]{1,0:T(8,128)(2,1)S(1)}, bf16[384,128]{1,0:T(8,128)(2,1)S(1)}, u32[]{:S(2)}, u32[]{:S(2)}) %collective-permute-start.2) | collective-permute-done | bytes 98336 | tf_op jit(solution)/shard_map/ppermute | solution.py:402
  45.9 1.1 %shard_map.188 = (bf16[2,16,512]{2,1,0:T(8,128)(2,1)}, bf16[2,16,32,64]{3,2,1,0:T(8,128)(2,1)}) custom-call(s32[1]{0:T(128)} %bitcast.3.where_ref, bf16[384,128]{1,0:T(8,128)(2,1)S(1)} %get-tuple-element.13.near_ref, bf16[384,128]{1,0:T(8,128)(2,1)S(1)} %collective-permute-done.next_ref, bf16[384,128]{1,0:T(8,128)(2,1)S(1)} %collective-permute-done.1.across_ref, ...), custom_call_target="tpu_custom_call" | custom-call | tf_op jit(solution)/shard_map/pallas_call | solution.py:405
  46.9 8.8 %all-to-all-done.1.in_ref = bf16[32,8,2176]{2,1,0:T(8,128)(2,1)S(1)} async-done(((bf16[32,8,2176]{2,1,0:T(8,128)(2,1)}), bf16[32,8,2176]{2,1,0:T(8,128)(2,1)S(1)}, u32[]{:S(2)}, u32[]{:S(2)}) %all-to-all-start.1) | async-done | bytes 1114144 | tf_op jit(solution)/shard_map/all_to_all | solution.py:382
  55.7 0.8 %shard_map.186 = bf16[2,2,4096]{2,1,0:T(2,128)(2,1)} custom-call(bf16[32,8,2176]{2,1,0:T(8,128)(2,1)S(1)} %all-to-all-done.1.in_ref), custom_call_target="tpu_custom_call" | custom-call | flops 1000000 | bytes 1500000 | tf_op jit(solution)/shard_map/pallas_call | solution.py:411
  (1 shorter events, 0.0 us)
Async XLA Ops:
  0.6 6.8 %copy-start = (f32[16]{0:T(128)S(1)}, f32[16]{0:T(128)}, u32[]{:S(2)}) copy-start(f32[16]{0:T(128)} %param.22) | copy-start | bytes 196
  0.6 6.9 %copy-start.1 = (f32[16]{0:T(128)S(1)}, f32[16]{0:T(128)}, u32[]{:S(2)}) copy-start(f32[16]{0:T(128)} %param.23) | copy-start | bytes 196
  2.6 12.3 %all-to-all-start = ((bf16[4,464,128]{2,1,0:T(8,128)(2,1)}), bf16[4,464,128]{2,1,0:T(8,128)(2,1)S(1)}, u32[]{:S(2)}, u32[]{:S(2)}) async-start(bf16[4,464,128]{2,1,0:T(8,128)(2,1)} %shard_map.184), calls=%async_computation | async-start | bytes 950272 | tf_op jit(solution)/shard_map/all_to_all | solution.py:364
  18.4 37.3 %all-to-all-start.1 = ((bf16[32,8,2176]{2,1,0:T(8,128)(2,1)}), bf16[32,8,2176]{2,1,0:T(8,128)(2,1)S(1)}, u32[]{:S(2)}, u32[]{:S(2)}) async-start(bf16[32,8,2176]{2,1,0:T(8,128)(2,1)} %get-tuple-element.11), calls=%async_computation.1 | async-start | bytes 2228224 | tf_op jit(solution)/shard_map/all_to_all | solution.py:382
  30.6 10.5 %collective-permute-start = (bf16[384,128]{1,0:T(8,128)(2,1)S(1)}, bf16[384,128]{1,0:T(8,128)(2,1)S(1)}, u32[]{:S(2)}, u32[]{:S(2)}) collective-permute-start(bf16[384,128]{1,0:T(8,128)(2,1)S(1)} %get-tuple-element.14), channel_id=1, source_target_pairs={{0,1},{1,2},{2,3},{3,0},{4,5},{5,6},{6,7},{7,4},{8,9},{9,10},{10,1... | collective-permute-start | bytes 294920 | tf_op jit(solution)/shard_map/ppermute | solution.py:402
  33.9 10.2 %collective-permute-start.1 = (bf16[384,128]{1,0:T(8,128)(2,1)S(1)}, bf16[384,128]{1,0:T(8,128)(2,1)S(1)}, u32[]{:S(2)}, u32[]{:S(2)}) collective-permute-start(bf16[384,128]{1,0:T(8,128)(2,1)S(1)} %get-tuple-element.15), channel_id=1, source_target_pairs={{0,2},{1,3},{2,0},{3,1},{4,6},{5,7},{6,4},{7,5},{8,10},{9,11},{10,... | collective-permute-start | bytes 294920 | tf_op jit(solution)/shard_map/ppermute | solution.py:402
  36.7 9.2 %collective-permute-start.2 = (bf16[384,128]{1,0:T(8,128)(2,1)S(1)}, bf16[384,128]{1,0:T(8,128)(2,1)S(1)}, u32[]{:S(2)}, u32[]{:S(2)}) collective-permute-start(bf16[384,128]{1,0:T(8,128)(2,1)S(1)} %get-tuple-element.16), channel_id=1, source_target_pairs={{0,3},{1,0},{2,1},{3,2},{4,7},{5,4},{6,5},{7,6},{8,11},{9,8},{10,9... | collective-permute-start | bytes 294920 | tf_op jit(solution)/shard_map/ppermute | solution.py:402

commit v6 on v5

--- a/solution.py
+++ b/solution.py
@@ -19,10 +19,9 @@
 Z_ROW = 64
 B_ROW = 128
 C_ROW = 160
-Q_ROW = 192
-S_ROW = 320
-T_ROW = 448
-ROWS = 464
+S_ROW = 192
+T_ROW = 320
+ROWS = 336
 
 N_ROW = 0
 M_ROW = 128
@@ -45,7 +44,7 @@
     return lax.broadcasted_iota(jnp.int32, shape, dim)
 
 
-def pack_kernel(x_ref, z_ref, b_ref, c_ref, t_ref, s_ref, q_ref, out_ref, buf, sems):
+def pack_kernel(x_ref, z_ref, b_ref, c_ref, t_ref, s_ref, q_ref, out_ref, mine_ref, buf, sems):
     pad = jnp.zeros((16, 60), F32)
     copies = []
     for to in range(4):
@@ -60,15 +59,16 @@
                 buf[to, pl.ds(S_ROW + (seq * 2 + block) * 32, 32), :] = pair
             buf[to, pl.ds(B_ROW + seq * 16, 16), :] = b_ref[seq]
             buf[to, pl.ds(C_ROW + seq * 16, 16), :] = c_ref[seq]
-            for head in range(4):
-                row = Q_ROW + (seq * 4 + head) * 16
-                buf[to, pl.ds(row, 16), :] = q_ref[seq, :, pl.ds(head * 128, 128)]
         own = [t_ref[seq].astype(F32)[:, to * 4 : to * 4 + 4] for seq in range(2)]
         lanes = jnp.concatenate([own[0], pad, own[1], pad], axis=1)
         buf[to, pl.ds(T_ROW, 16), :] = lanes.astype(BF16)
         copy = pltpu.make_async_copy(buf.at[to], out_ref.at[to], sems.at[to])
         copy.start()
         copies.append(copy)
+    for seq in range(2):
+        for head in range(4):
+            row = (seq * 4 + head) * 16
+            mine_ref[pl.ds(row, 16), :] = q_ref[seq, :, pl.ds(head * 128, 128)]
     for copy in copies:
         copy.wait()
 
@@ -89,8 +89,23 @@
 
 
 def mixer_kernel(
-    in_ref, w_ref, rate_ref, skip_ref, gain_ref, out_ref, run_ref, w_buf, o_buf, sem, out_sems
+    in_ref,
+    w_ref,
+    rate_ref,
+    skip_ref,
+    gain_ref,
+    mine_ref,
+    before_ref,
+    out_ref,
+    run_ref,
+    pair_ref,
+    w_buf,
+    o_buf,
+    sem,
+    out_sems,
 ):
+    pair_ref[0] = mine_ref[...]
+    pair_ref[1] = before_ref[...]
     fetch = pltpu.make_async_copy(w_ref, w_buf, sem)
     fetch.start()
     row = iota((128, 128), 0)
@@ -180,11 +195,33 @@
         copy.wait()
 
 
-def attend_kernel(
+def attend(tok, seq, queries, backs, limit, k_ref, v_ref, dk_ref, dv_ref, refs):
+    scale = 128 ** (-0.5)
+    old = dot_t(queries, k_ref[seq]) * scale
+    new = dot_t(queries, dk_ref[seq]) * scale
+    old = jnp.where(iota(old.shape, 1) < limit, old, MASKED)
+    line = iota(new.shape, 0)
+    draft = ((tok + 4 - backs[0] - line // 64) % 4) * 16 + line % 16
+    new = jnp.where(iota(new.shape, 1) + tok * 16 <= draft, new, MASKED)
+    peak = jnp.maximum(jnp.max(old, axis=1, keepdims=True), jnp.max(new, axis=1, keepdims=True))
+    peak = jnp.maximum(peak, FLOOR).astype(BF16).astype(F32)
+    old = jnp.exp(old - peak)
+    new = jnp.exp(new - peak)
+    total = jnp.sum(old, axis=1, keepdims=True) + jnp.sum(new, axis=1, keepdims=True)
+    numer = dot(old.astype(BF16), v_ref[seq]) + dot(new.astype(BF16), dv_ref[seq])
+    numer = numer.astype(BF16)
+    stats = jnp.where(iota((128, 128), 1) < 64, peak, total).astype(BF16)
+    for part, ref in enumerate(refs):
+        ref[pl.ds(N_ROW + seq * 64, 64), :] = numer[part * 64 : part * 64 + 64]
+        ref[pl.ds(M_ROW + seq * 64, 64), :] = stats[part * 64 : part * 64 + 64]
+
+
+def near_kernel(
     where_ref,
     len_ref,
     acc_ref,
     in_ref,
+    pair_ref,
     run_ref,
     rate_ref,
     k_ref,
@@ -192,39 +229,11 @@
     dk_ref,
     dv_ref,
     near_ref,
-    next_ref,
-    across_ref,
     last_ref,
+    state_ref,
     out_ref,
 ):
     tok = where_ref[0]
-    scale = 128 ** (-0.5)
-    cache = k_ref.shape[1]
-    for seq in range(2):
-        queries = jnp.concatenate(
-            [in_ref[src, pl.ds(Q_ROW + seq * 64, 64), :] for src in range(4)], axis=0
-        )
-        old = dot_t(queries, k_ref[seq]) * scale
-        new = dot_t(queries, dk_ref[seq]) * scale
-        limit = len_ref[seq] - tok * cache
-        old = jnp.where(iota(old.shape, 1) < limit, old, MASKED)
-        line = iota(new.shape, 0)
-        draft = (line // 64) * 16 + line % 16
-        new = jnp.where(iota(new.shape, 1) + tok * 16 <= draft, new, MASKED)
-        peak = jnp.maximum(
-            jnp.max(old, axis=1, keepdims=True), jnp.max(new, axis=1, keepdims=True)
-        )
-        peak = jnp.maximum(peak, FLOOR).astype(BF16).astype(F32)
-        old = jnp.exp(old - peak)
-        new = jnp.exp(new - peak)
-        total = jnp.sum(old, axis=1, keepdims=True) + jnp.sum(new, axis=1, keepdims=True)
-        numer = dot(old.astype(BF16), v_ref[seq]) + dot(new.astype(BF16), dv_ref[seq])
-        numer = numer.astype(BF16)
-        stats = jnp.where(iota((256, 128), 1) < 64, peak, total).astype(BF16)
-        for to in range(4):
-            out_ref[to, pl.ds(N_ROW + seq * 64, 64), :] = numer[to * 64 : to * 64 + 64]
-            out_ref[to, pl.ds(M_ROW + seq * 64, 64), :] = stats[to * 64 : to * 64 + 64]
-
     row = iota((128, 128), 0)
     low = iota((128, 128), 1) < 64
     low_row = iota((1, 128), 1) < 64
@@ -233,6 +242,12 @@
     run = run_ref[...]
     rate = rate_ref[...]
     for seq in range(2):
+        rows = pl.ds(seq * 64, 64)
+        queries = jnp.concatenate([pair_ref[0, rows], pair_ref[1, rows]], axis=0)
+        limit = len_ref[seq] - tok * k_ref.shape[1]
+        attend(
+            tok, seq, queries, (0, 1), limit, k_ref, v_ref, dk_ref, dv_ref, (near_ref, last_ref)
+        )
         alive = (row >= seq * 64) & (row < seq * 64 + acc_ref[seq])
         end = -jnp.sum(jnp.where(alive, steps, 0.0), axis=0, keepdims=True) * rate
         weights = jnp.where(alive, jnp.exp(jnp.where(alive, end - run, 0.0)) * steps, 0.0)
@@ -249,9 +264,35 @@
                 at = (seq * 2 + block) * 32
                 state = in_ref[src, pl.ds(S_ROW + at, 32), :].astype(F32)
                 result = decay * state + added[src * 32 : src * 32 + 32]
-                out_ref[src, pl.ds(H_ROW + at, 32), :] = result.astype(BF16)
-    for shift, ref in enumerate((near_ref, next_ref, across_ref, last_ref)):
-        ref[...] = out_ref[lax.rem(tok + shift, 4)]
+                out_ref[src, pl.ds(at, 32), :] = result.astype(BF16)
+    near_ref[pl.ds(H_ROW, 128), :] = out_ref[tok]
+    last_ref[pl.ds(H_ROW, 128), :] = out_ref[lax.rem(tok + 3, 4)]
+    for shift in (1, 2):
+        state_ref[shift - 1] = out_ref[lax.rem(tok + shift, 4)]
+
+
+def far_kernel(
+    where_ref,
+    len_ref,
+    farther_ref,
+    state_ref,
+    k_ref,
+    v_ref,
+    dk_ref,
+    dv_ref,
+    next_ref,
+    across_ref,
+):
+    tok = where_ref[0]
+    for seq in range(2):
+        rows = pl.ds(seq * 64, 64)
+        queries = jnp.concatenate([farther_ref[0, rows], farther_ref[1, rows]], axis=0)
+        limit = len_ref[seq] - tok * k_ref.shape[1]
+        attend(
+            tok, seq, queries, (2, 3), limit, k_ref, v_ref, dk_ref, dv_ref, (across_ref, next_ref)
+        )
+    next_ref[pl.ds(H_ROW, 128), :] = state_ref[0]
+    across_ref[pl.ds(H_ROW, 128), :] = state_ref[1]
 
 
 def combine_kernel(where_ref, near_ref, next_ref, across_ref, last_ref, att_ref, state_ref):
@@ -345,12 +386,12 @@
 ):
     tok = lax.axis_index("tok")
     where = tok.reshape(1).astype(jnp.int32)
-    (packed,) = call(
+    packed, mine = call(
         pack_kernel,
         in_vmem(7),
-        [((4, ROWS, 128), BF16, True)],
+        [((4, ROWS, 128), BF16, True), ((128, 128), BF16, INTERPRET)],
         (0, 1500000),
-        out_specs=(pl.BlockSpec(memory_space=pl.ANY),),
+        out_specs=(pl.BlockSpec(memory_space=pl.ANY), *in_vmem(1)),
         scratch_shapes=[pltpu.VMEM((4, ROWS, 128), BF16), pltpu.SemaphoreType.DMA((4,))],
     )(
         mamba_input,
@@ -363,44 +404,44 @@
     )
     arrived = lax.all_to_all(packed, "tok", split_axis=0, concat_axis=0, tiled=True)
     arrived = held(arrived)
+    before = lax.ppermute(mine, "tok", [(i, (i + 1) % 4) for i in range(4)])
     rate = jnp.pad(lax.dynamic_slice(decay_rate, (tok * 4,), (4,)), (0, 124)).reshape(1, 128)
     skip = jnp.repeat(lax.dynamic_slice(skip_weight, (tok * 4,), (4,)), 64).reshape(1, 256)
     gain = lax.dynamic_slice(norm_gain, (tok * 256,), (256,)).reshape(1, 256)
-    shares, run = call(
+    shares, run, pair = call(
         mixer_kernel,
-        in_vmem(1) + [pl.BlockSpec(memory_space=pl.ANY)] + in_vmem(3),
-        [((32, 8, WIDTH), BF16, True), ((128, 128), F32, INTERPRET)],
+        in_vmem(1) + [pl.BlockSpec(memory_space=pl.ANY)] + in_vmem(5),
+        [
+            ((32, 8, WIDTH), BF16, True),
+            ((128, 128), F32, INTERPRET),
+            ((2, 128, 128), BF16, INTERPRET),
+        ],
         (400000000, 4000000),
-        out_specs=(pl.BlockSpec(memory_space=pl.ANY), *in_vmem(1)),
+        out_specs=(pl.BlockSpec(memory_space=pl.ANY), *in_vmem(2)),
         scratch_shapes=[
             pltpu.VMEM((256, 4096), BF16),
             pltpu.VMEM((32, 8, WIDTH), BF16),
             pltpu.SemaphoreType.DMA,
             pltpu.SemaphoreType.DMA((5,)),
         ],
-    )(arrived, out_weight, held(rate), held(skip), held(gain))
+    )(arrived, out_weight, held(rate), held(skip), held(gain), held(mine), held(before))
+    farther = lax.ppermute(pair, "tok", [(i, (i + 2) % 4) for i in range(4)])
     landed = lax.all_to_all(shares, ("head", "tok"), split_axis=0, concat_axis=0, tiled=True)
-    back = call(
-        attend_kernel,
-        in_smem(3) + in_vmem(7),
-        [((BACK_ROWS, 128), BF16, INTERPRET)] * 4,
+    cached = (cached_key_rows, cache_values, draft_token_keys, draft_values)
+    back = ((BACK_ROWS, 128), BF16, INTERPRET)
+    near, last, states = call(
+        near_kernel,
+        in_smem(3) + in_vmem(8),
+        [back, back, ((2, 128, 128), BF16, INTERPRET)],
         (0, 0),
-        scratch_shapes=[pltpu.VMEM((4, BACK_ROWS, 128), BF16)],
-    )(
-        where,
-        cache_len,
-        accepted,
-        arrived,
-        held(run),
-        held(rate),
-        cached_key_rows,
-        cache_values,
-        draft_token_keys,
-        draft_values,
-    )
-    returned = [held(back[0])] + [
-        held(lax.ppermute(back[k], "tok", [(i, (i + k) % 4) for i in range(4)]))
-        for k in (1, 2, 3)
+        scratch_shapes=[pltpu.VMEM((4, 128, 128), BF16)],
+    )(where, cache_len, accepted, arrived, held(pair), held(run), held(rate), *cached)
+    after, across = call(far_kernel, in_smem(2) + in_vmem(6), [back, back], (0, 0))(
+        where, cache_len, held(farther), held(states), *cached
+    )
+    returned = [held(near)] + [
+        held(lax.ppermute(part, "tok", [(i, (i + shift) % 4) for i in range(4)]))
+        for shift, part in ((1, after), (2, across), (3, last))
     ]
     attn_context, state_t = call(
         combine_kernel,

time: 57 us -> 56.4 us (0.989)
  waiting for transfers between devices: 20 us -> 10.4 us
  starting transfers between devices: 24.6 us -> 32.5 us
  Pallas kernels: 10.1 us -> 11.1 us
    ppermute x3 -> x5, starting transfers between devices: 10.4 us -> 17.8 us  [the longest x3 10.4 us: body(): lax.ppermute(part, 'tok', [(i, (i + shift) % 4) for i in range(4)])]
    all_to_all x1, waiting for transfers between devices: 6.42 us -> 0.29 us  [body(): lax.all_to_all(packed, 'tok', split_axis=0, concat_axis=0, tiled=True)]
    all_to_all x1, waiting for transfers between devices: 8.77 us -> 4.62 us  [body(): lax.all_to_all(shares, ('head', 'tok'), split_axis=0, concat_axis=0, tile...]
    pallas_call x2 -> x3, Pallas kernels: 4.76 us -> 6.32 us  [the longest x1 2.26 us: body(): call(near_kernel, in_smem(3) + in_vmem(8), [back, back, ((2, 128, 128), B...]
    all_to_all x1, starting transfers between devices: 9.33 us -> 9.94 us  [body(): lax.all_to_all(shares, ('head', 'tok'), split_axis=0, concat_axis=0, tile...]
    ppermute x3 -> x5, waiting for transfers between devices: 4.83 us -> 5.44 us  [the longest x3 4.11 us: body(): lax.ppermute(part, 'tok', [(i, (i + shift) % 4) for i in range(4)])]
  transfers between devices with their start and end apart: 5 -> 7, of which waited for: 4 -> 5; matrix products, arithmetic and copies ran while one was open for 2% -> 2% of each run, Pallas kernels for 7% -> 10%
where the time goes in v6:
time: 56.4 us; the launch traced here: 55.9 us
  starting transfers between devices  32.5 us (58%)
  Pallas kernels  11.1 us (20%)
  waiting for transfers between devices  10.4 us (18%)
  local copies, waits for them, and re-layouts  1.09 us (2%)
  between operations  0.76 us (1%)
    ppermute x3, starting transfers between devices, body(): lax.ppermute(part, 'tok', [(i, (i + shift) % 4) for i in range(4)])  10.4 us
    all_to_all x1, starting transfers between devices, body(): lax.all_to_all(shares, ('head', 'tok'), split_axis=0, concat_axis=0, tile...  9.94 us
    all_to_all x1, starting transfers between devices, body(): lax.all_to_all(packed, 'tok', split_axis=0, concat_axis=0, tiled=True)  4.84 us
    all_to_all x1, waiting for transfers between devices, body(): lax.all_to_all(shares, ('head', 'tok'), split_axis=0, concat_axis=0, tile...  4.62 us
    ppermute x3, waiting for transfers between devices, body(): lax.ppermute(part, 'tok', [(i, (i + shift) % 4) for i in range(4)])  4.11 us
    ppermute x1, starting transfers between devices, body(): farther = lax.ppermute(pair, 'tok', [(i, (i + 2) % 4) for i in range(4)])  3.98 us
    ppermute x1, starting transfers between devices, body(): before = lax.ppermute(mine, 'tok', [(i, (i + 1) % 4) for i in range(4)])  3.36 us
    pallas_call x1, Pallas kernels, body(): call(mixer_kernel, in_vmem(1) + [pl.BlockSpec(memory_space=pl.ANY)] + in_...  2.92 us
  transfers between devices with their start and end apart: 7, of which 5 were waited for; matrix products, arithmetic and copies ran while one was open for 2% of the time, Pallas kernels for 10%

profile of v6, /device:TPU:386, one launch (start us, length us, event | category | flops | bytes accessed | tf_op | source)
XLA Modules:
  0.0 55.9 jit_solution(4251646552627723248)
XLA Ops:
  0.6 0.0 copy-start
  0.6 0.0 copy-start.1
  0.7 1.9 %shard_map.184 = (bf16[4,336,128]{2,1,0:T(8,128)(2,1)}, bf16[128,128]{1,0:T(8,128)(2,1)S(1)}) custom-call(bf16[2,16,1024]{2,1,0:T(8,128)(2,1)} %x_ref.1, bf16[2,16,1024]{2,1,0:T(8,128)(2,1)} %z_ref.1, bf16[2,16,128]{2,1,0:T(8,128)(2,1)} %b_ref.1, bf16[2,16,128]{2,1,0:T(8,128)(2,1)} %c_ref.1, bf16[2,16,16]{2,1,0:T(8,128)(2,1)} %t_ref.1, ...), custom_call_target="tpu_custom_call" | custom-call | bytes 1500000 | tf_op jit(solution)/shard_map/pallas_call | solution.py:389
  2.5 4.8 %all-to-all-start = ((bf16[4,336,128]{2,1,0:T(8,128)(2,1)}), bf16[4,336,128]{2,1,0:T(8,128)(2,1)S(1)}, u32[]{:S(2)}, u32[]{:S(2)}) async-start(bf16[4,336,128]{2,1,0:T(8,128)(2,1)} %get-tuple-element.15), calls=%async_computation | async-start | bytes 688128 | tf_op jit(solution)/shard_map/all_to_all | solution.py:405
  7.4 3.4 %collective-permute-start = (bf16[128,128]{1,0:T(8,128)(2,1)S(1)}, bf16[128,128]{1,0:T(8,128)(2,1)S(1)}, u32[]{:S(2)}, u32[]{:S(2)}) collective-permute-start(bf16[128,128]{1,0:T(8,128)(2,1)S(1)} %get-tuple-element.16.mine_ref), channel_id=1, source_target_pairs={{0,1},{1,2},{2,3},{3,0},{4,5},{5,6},{6,7},{7,4},{8,9},{9,10},{10,1... | collective-permute-start | bytes 98312 | tf_op jit(solution)/shard_map/ppermute | solution.py:407
  10.7 0.0 copy-done
  10.7 0.1 dynamic_slice.9
  10.8 0.0 copy-done.1
  10.8 0.1 dynamic_slice.10
  10.9 0.1 broadcast_in_dim.3
  11.0 0.1 reshape_reshape.3.skip_ref
  11.1 0.8 %dynamic_slice.11 = f32[256]{0:T(256)S(1)} dynamic-slice(f32[1024]{0:T(1024)} %param.24, s32[]{:T(128)S(6)} %select_n.8), dynamic_slice_sizes={256} | dynamic-slice | bytes 2052 | tf_op jit(solution)/shard_map/dynamic_slice | solution.py:410
  11.8 1.3 %collective-permute-done.before_ref = bf16[128,128]{1,0:T(8,128)(2,1)S(1)} collective-permute-done((bf16[128,128]{1,0:T(8,128)(2,1)S(1)}, bf16[128,128]{1,0:T(8,128)(2,1)S(1)}, u32[]{:S(2)}, u32[]{:S(2)}) %collective-permute-start) | collective-permute-done | bytes 32800 | tf_op jit(solution)/shard_map/ppermute | solution.py:407
  13.2 0.3 all-to-all-done.in_ref
  13.4 2.9 %shard_map.185 = (bf16[32,8,2176]{2,1,0:T(8,128)(2,1)}, f32[128,128]{1,0:T(8,128)S(1)}, bf16[2,128,128]{2,1,0:T(8,128)(2,1)S(1)}) custom-call(bf16[4,336,128]{2,1,0:T(8,128)(2,1)S(1)} %all-to-all-done.in_ref, bf16[256,4096]{1,0:T(8,128)(2,1)} %w_ref.1, f32[1,128]{1,0:T(1,128)S(1)} %pad_bitcast_fusion.rate_ref, f32[1,256]{1,0:T(1,128)S(1)} %reshape_reshape.3.skip_ref, ...), custom_call_target="tpu_custom_call" | custom-call | flops 400000000 | bytes 4000000 | tf_op jit(solution)/shard_map/pallas_call | solution.py:411
  16.4 9.9 %all-to-all-start.1 = ((bf16[32,8,2176]{2,1,0:T(8,128)(2,1)}), bf16[32,8,2176]{2,1,0:T(8,128)(2,1)S(1)}, u32[]{:S(2)}, u32[]{:S(2)}) async-start(bf16[32,8,2176]{2,1,0:T(8,128)(2,1)} %get-tuple-element.17), calls=%async_computation.1 | async-start | bytes 2228224 | tf_op jit(solution)/shard_map/all_to_all | solution.py:429
  26.3 4.0 %collective-permute-start.1 = (bf16[2,128,128]{2,1,0:T(8,128)(2,1)S(1)}, bf16[2,128,128]{2,1,0:T(8,128)(2,1)S(1)}, u32[]{:S(2)}, u32[]{:S(2)}) collective-permute-start(bf16[2,128,128]{2,1,0:T(8,128)(2,1)S(1)} %get-tuple-element.18.pair_ref), channel_id=1, source_target_pairs={{0,2},{1,3},{2,0},{3,1},{4,6},{5,7},{6,4},{7,5},{8,10},{9,11},{10,... | collective-permute-start | bytes 196616 | tf_op jit(solution)/shard_map/ppermute | solution.py:428
  30.3 2.3 %shard_map.187 = (bf16[384,128]{1,0:T(8,128)(2,1)S(1)}, bf16[384,128]{1,0:T(8,128)(2,1)S(1)}, bf16[2,128,128]{2,1,0:T(8,128)(2,1)S(1)}) custom-call(s32[1]{0:T(128)} %bitcast.3.where_ref, s32[2]{0:T(128)} %len_ref.3, s32[2]{0:T(128)} %acc_ref.1, bf16[4,336,128]{2,1,0:T(8,128)(2,1)S(1)} %all-to-all-done.in_ref, ...), custom_call_target="tpu_custom_call" | custom-call | tf_op jit(solution)/shard_map/pallas_call | solution.py:432
  32.6 3.4 %collective-permute-start.4 = (bf16[384,128]{1,0:T(8,128)(2,1)S(1)}, bf16[384,128]{1,0:T(8,128)(2,1)S(1)}, u32[]{:S(2)}, u32[]{:S(2)}) collective-permute-start(bf16[384,128]{1,0:T(8,128)(2,1)S(1)} %get-tuple-element.24), channel_id=1, source_target_pairs={{0,3},{1,0},{2,1},{3,2},{4,7},{5,4},{6,5},{7,6},{8,11},{9,8},{10,9... | collective-permute-start | bytes 294920 | tf_op jit(solution)/shard_map/ppermute | solution.py:443
  35.9 0.0 collective-permute-done.1.farther_ref
  36.0 2.2 %shard_map.188 = (bf16[384,128]{1,0:T(8,128)(2,1)S(1)}, bf16[384,128]{1,0:T(8,128)(2,1)S(1)}) custom-call(s32[1]{0:T(128)} %bitcast.3.where_ref, s32[2]{0:T(128)} %len_ref.3, bf16[2,128,128]{2,1,0:T(8,128)(2,1)S(1)} %collective-permute-done.1.farther_ref, bf16[2,128,128]{2,1,0:T(8,128)(2,1)S(1)} %get-tuple-element.21.state_ref, bf16[2,1024,128]{2,1,0:T(8,128)(2,1)} %k_ref.3, ...), custom_call_target="tpu_custom_call" | custom-call | tf_op jit(solution)/shard_map/pallas_call | solution.py:439
  38.2 2.5 %collective-permute-start.2 = (bf16[384,128]{1,0:T(8,128)(2,1)S(1)}, bf16[384,128]{1,0:T(8,128)(2,1)S(1)}, u32[]{:S(2)}, u32[]{:S(2)}) collective-permute-start(bf16[384,128]{1,0:T(8,128)(2,1)S(1)} %get-tuple-element.22), channel_id=1, source_target_pairs={{0,1},{1,2},{2,3},{3,0},{4,5},{5,6},{6,7},{7,4},{8,9},{9,10},{10,1... | collective-permute-start | bytes 294920 | tf_op jit(solution)/shard_map/ppermute | solution.py:443
  40.7 4.6 %collective-permute-start.3 = (bf16[384,128]{1,0:T(8,128)(2,1)S(1)}, bf16[384,128]{1,0:T(8,128)(2,1)S(1)}, u32[]{:S(2)}, u32[]{:S(2)}) collective-permute-start(bf16[384,128]{1,0:T(8,128)(2,1)S(1)} %get-tuple-element.23), channel_id=1, source_target_pairs={{0,2},{1,3},{2,0},{3,1},{4,6},{5,7},{6,4},{7,5},{8,10},{9,11},{10,... | collective-permute-start | bytes 294920 | tf_op jit(solution)/shard_map/ppermute | solution.py:443
  45.2 0.0 collective-permute-done.4.last_ref
  45.3 1.1 %collective-permute-done.2.next_ref = bf16[384,128]{1,0:T(8,128)(2,1)S(1)} collective-permute-done((bf16[384,128]{1,0:T(8,128)(2,1)S(1)}, bf16[384,128]{1,0:T(8,128)(2,1)S(1)}, u32[]{:S(2)}, u32[]{:S(2)}) %collective-permute-start.2) | collective-permute-done | bytes 98336 | tf_op jit(solution)/shard_map/ppermute | solution.py:443
  46.3 3.0 %collective-permute-done.3.across_ref = bf16[384,128]{1,0:T(8,128)(2,1)S(1)} collective-permute-done((bf16[384,128]{1,0:T(8,128)(2,1)S(1)}, bf16[384,128]{1,0:T(8,128)(2,1)S(1)}, u32[]{:S(2)}, u32[]{:S(2)}) %collective-permute-start.3) | collective-permute-done | bytes 98336 | tf_op jit(solution)/shard_map/ppermute | solution.py:443
  49.4 1.1 %shard_map.189 = (bf16[2,16,512]{2,1,0:T(8,128)(2,1)}, bf16[2,16,32,64]{3,2,1,0:T(8,128)(2,1)}) custom-call(s32[1]{0:T(128)} %bitcast.3.where_ref, bf16[384,128]{1,0:T(8,128)(2,1)S(1)} %get-tuple-element.20.near_ref, bf16[384,128]{1,0:T(8,128)(2,1)S(1)} %collective-permute-done.2.next_ref, bf16[384,128]{1,0:T(8,128)(2,1)S(1)} %collective-permute-done.3.across_ref, ...), custom_call_target="tpu_custom_call" | custom-call | tf_op jit(solution)/shard_map/pallas_call | solution.py:446
  50.4 4.6 %all-to-all-done.1.in_ref = bf16[32,8,2176]{2,1,0:T(8,128)(2,1)S(1)} async-done(((bf16[32,8,2176]{2,1,0:T(8,128)(2,1)}), bf16[32,8,2176]{2,1,0:T(8,128)(2,1)S(1)}, u32[]{:S(2)}, u32[]{:S(2)}) %all-to-all-start.1) | async-done | bytes 1114144 | tf_op jit(solution)/shard_map/all_to_all | solution.py:429
  55.0 0.8 %shard_map.186 = bf16[2,2,4096]{2,1,0:T(2,128)(2,1)} custom-call(bf16[32,8,2176]{2,1,0:T(8,128)(2,1)S(1)} %all-to-all-done.1.in_ref), custom_call_target="tpu_custom_call" | custom-call | flops 1000000 | bytes 1500000 | tf_op jit(solution)/shard_map/pallas_call | solution.py:452
  (1 shorter events, 0.0 us)
Async XLA Ops:
  0.6 10.1 %copy-start = (f32[16]{0:T(128)S(1)}, f32[16]{0:T(128)}, u32[]{:S(2)}) copy-start(f32[16]{0:T(128)} %param.22) | copy-start | bytes 196
  0.6 10.2 %copy-start.1 = (f32[16]{0:T(128)S(1)}, f32[16]{0:T(128)}, u32[]{:S(2)}) copy-start(f32[16]{0:T(128)} %param.23) | copy-start | bytes 196
  2.5 10.9 %all-to-all-start = ((bf16[4,336,128]{2,1,0:T(8,128)(2,1)}), bf16[4,336,128]{2,1,0:T(8,128)(2,1)S(1)}, u32[]{:S(2)}, u32[]{:S(2)}) async-start(bf16[4,336,128]{2,1,0:T(8,128)(2,1)} %get-tuple-element.15), calls=%async_computation | async-start | bytes 688128 | tf_op jit(solution)/shard_map/all_to_all | solution.py:405
  7.4 5.8 %collective-permute-start = (bf16[128,128]{1,0:T(8,128)(2,1)S(1)}, bf16[128,128]{1,0:T(8,128)(2,1)S(1)}, u32[]{:S(2)}, u32[]{:S(2)}) collective-permute-start(bf16[128,128]{1,0:T(8,128)(2,1)S(1)} %get-tuple-element.16.mine_ref), channel_id=1, source_target_pairs={{0,1},{1,2},{2,3},{3,0},{4,5},{5,6},{6,7},{7,4},{8,9},{9,10},{10,1... | collective-permute-start | bytes 98312 | tf_op jit(solution)/shard_map/ppermute | solution.py:407
  16.4 38.7 %all-to-all-start.1 = ((bf16[32,8,2176]{2,1,0:T(8,128)(2,1)}), bf16[32,8,2176]{2,1,0:T(8,128)(2,1)S(1)}, u32[]{:S(2)}, u32[]{:S(2)}) async-start(bf16[32,8,2176]{2,1,0:T(8,128)(2,1)} %get-tuple-element.17), calls=%async_computation.1 | async-start | bytes 2228224 | tf_op jit(solution)/shard_map/all_to_all | solution.py:429
  26.3 9.6 %collective-permute-start.1 = (bf16[2,128,128]{2,1,0:T(8,128)(2,1)S(1)}, bf16[2,128,128]{2,1,0:T(8,128)(2,1)S(1)}, u32[]{:S(2)}, u32[]{:S(2)}) collective-permute-start(bf16[2,128,128]{2,1,0:T(8,128)(2,1)S(1)} %get-tuple-element.18.pair_ref), channel_id=1, source_target_pairs={{0,2},{1,3},{2,0},{3,1},{4,6},{5,7},{6,4},{7,5},{8,10},{9,11},{10,... | collective-permute-start | bytes 196616 | tf_op jit(solution)/shard_map/ppermute | solution.py:428
  32.6 12.7 %collective-permute-start.4 = (bf16[384,128]{1,0:T(8,128)(2,1)S(1)}, bf16[384,128]{1,0:T(8,128)(2,1)S(1)}, u32[]{:S(2)}, u32[]{:S(2)}) collective-permute-start(bf16[384,128]{1,0:T(8,128)(2,1)S(1)} %get-tuple-element.24), channel_id=1, source_target_pairs={{0,3},{1,0},{2,1},{3,2},{4,7},{5,4},{6,5},{7,6},{8,11},{9,8},{10,9... | collective-permute-start | bytes 294920 | tf_op jit(solution)/shard_map/ppermute | solution.py:443
  38.2 8.2 %collective-permute-start.2 = (bf16[384,128]{1,0:T(8,128)(2,1)S(1)}, bf16[384,128]{1,0:T(8,128)(2,1)S(1)}, u32[]{:S(2)}, u32[]{:S(2)}) collective-permute-start(bf16[384,128]{1,0:T(8,128)(2,1)S(1)} %get-tuple-element.22), channel_id=1, source_target_pairs={{0,1},{1,2},{2,3},{3,0},{4,5},{5,6},{6,7},{7,4},{8,9},{9,10},{10,1... | collective-permute-start | bytes 294920 | tf_op jit(solution)/shard_map/ppermute | solution.py:443
  40.7 8.7 %collective-permute-start.3 = (bf16[384,128]{1,0:T(8,128)(2,1)S(1)}, bf16[384,128]{1,0:T(8,128)(2,1)S(1)}, u32[]{:S(2)}, u32[]{:S(2)}) collective-permute-start(bf16[384,128]{1,0:T(8,128)(2,1)S(1)} %get-tuple-element.23), channel_id=1, source_target_pairs={{0,2},{1,3},{2,0},{3,1},{4,6},{5,7},{6,4},{7,5},{8,10},{9,11},{10,... | collective-permute-start | bytes 294920 | tf_op jit(solution)/shard_map/ppermute | solution.py:443

commit v7 on v6

--- a/solution.py
+++ b/solution.py
@@ -25,8 +25,8 @@
 
 N_ROW = 0
 M_ROW = 128
-H_ROW = 256
-BACK_ROWS = 384
+H_ROW = 144
+BACK_ROWS = 272
 
 HALF = 2048
 WIDTH = HALF + 128
@@ -210,10 +210,12 @@
     total = jnp.sum(old, axis=1, keepdims=True) + jnp.sum(new, axis=1, keepdims=True)
     numer = dot(old.astype(BF16), v_ref[seq]) + dot(new.astype(BF16), dv_ref[seq])
     numer = numer.astype(BF16)
-    stats = jnp.where(iota((128, 128), 1) < 64, peak, total).astype(BF16)
+    lanes = iota((128, 128), 1)
+    stats = jnp.where(lanes == 0, peak, total).T
     for part, ref in enumerate(refs):
         ref[pl.ds(N_ROW + seq * 64, 64), :] = numer[part * 64 : part * 64 + 64]
-        ref[pl.ds(M_ROW + seq * 64, 64), :] = stats[part * 64 : part * 64 + 64]
+        own = stats[:8] if part == 0 else jnp.concatenate([stats[:8, 64:], stats[:8, :64]], axis=1)
+        ref[pl.ds(M_ROW + seq * 8, 8), :] = own.astype(BF16)
 
 
 def near_kernel(
@@ -298,14 +300,18 @@
 def combine_kernel(where_ref, near_ref, next_ref, across_ref, last_ref, att_ref, state_ref):
     refs = (near_ref, next_ref, across_ref, last_ref)
     for seq in range(2):
-        stats = [ref[pl.ds(M_ROW + seq * 64, 64), :].astype(F32) for ref in refs]
-        peaks = [s[:, 0:1] for s in stats]
+        stats = []
+        for ref in refs:
+            lines = ref[pl.ds(M_ROW + seq * 8, 8), :].astype(F32)
+            stats.append(jnp.broadcast_to(lines[0:1], (128, 128)).T[:64])
+            stats.append(jnp.broadcast_to(lines[1:2], (128, 128)).T[:64])
+        peaks = stats[0::2]
         overall = functools.reduce(jnp.maximum, peaks)
         numer = jnp.zeros((64, 128), F32)
-        denominator = jnp.zeros((64, 1), F32)
-        for ref, peak, stat in zip(refs, peaks, stats):
+        denominator = jnp.zeros((64, 128), F32)
+        for ref, peak, stat in zip(refs, peaks, stats[1::2]):
             rescale = jnp.exp(peak - overall)
-            denominator = denominator + rescale * stat[:, 64:65]
+            denominator = denominator + rescale * stat
             part = ref[pl.ds(N_ROW + seq * 64, 64), :].astype(F32)
             numer = numer + rescale * part
         context = (numer / denominator).astype(BF16)

time: 56.4 us -> 56.4 us (level)
    ppermute x3, waiting for transfers between devices: 4.11 us -> 3.47 us  [body(): lax.ppermute(part, 'tok', [(i, (i + shift) % 4) for i in range(4)])]
where the time goes in v7:
time: 56.4 us; the launch traced here: 55.9 us
  starting transfers between devices  32.5 us (58%)
  Pallas kernels  11.4 us (20%)
  waiting for transfers between devices  10.1 us (18%)
  local copies, waits for them, and re-layouts  1.09 us (2%)
  between operations  0.75 us (1%)
    ppermute x3, starting transfers between devices, body(): lax.ppermute(part, 'tok', [(i, (i + shift) % 4) for i in range(4)])  10.4 us
    all_to_all x1, starting transfers between devices, body(): lax.all_to_all(shares, ('head', 'tok'), split_axis=0, concat_axis=0, tile...  9.94 us
    all_to_all x1, waiting for transfers between devices, body(): lax.all_to_all(shares, ('head', 'tok'), split_axis=0, concat_axis=0, tile...  5.03 us
    all_to_all x1, starting transfers between devices, body(): lax.all_to_all(packed, 'tok', split_axis=0, concat_axis=0, tiled=True)  4.84 us
    ppermute x1, starting transfers between devices, body(): farther = lax.ppermute(pair, 'tok', [(i, (i + 2) % 4) for i in range(4)])  3.98 us
    ppermute x3, waiting for transfers between devices, body(): lax.ppermute(part, 'tok', [(i, (i + shift) % 4) for i in range(4)])  3.47 us
    ppermute x1, starting transfers between devices, body(): before = lax.ppermute(mine, 'tok', [(i, (i + 1) % 4) for i in range(4)])  3.36 us
    pallas_call x1, Pallas kernels, body(): call(mixer_kernel, in_vmem(1) + [pl.BlockSpec(memory_space=pl.ANY)] + in_...  2.92 us
  transfers between devices with their start and end apart: 7, of which 5 were waited for; matrix products, arithmetic and copies ran while one was open for 2% of the time, Pallas kernels for 10%

profile of v7, /device:TPU:386, one launch (start us, length us, event | category | flops | bytes accessed | tf_op | source)
XLA Modules:
  0.0 55.9 jit_solution(7320473836662377812)
XLA Ops:
  0.6 0.0 copy-start
  0.6 0.0 copy-start.1
  0.7 1.9 %shard_map.184 = (bf16[4,336,128]{2,1,0:T(8,128)(2,1)}, bf16[128,128]{1,0:T(8,128)(2,1)S(1)}) custom-call(bf16[2,16,1024]{2,1,0:T(8,128)(2,1)} %x_ref.1, bf16[2,16,1024]{2,1,0:T(8,128)(2,1)} %z_ref.1, bf16[2,16,128]{2,1,0:T(8,128)(2,1)} %b_ref.1, bf16[2,16,128]{2,1,0:T(8,128)(2,1)} %c_ref.1, bf16[2,16,16]{2,1,0:T(8,128)(2,1)} %t_ref.1, ...), custom_call_target="tpu_custom_call" | custom-call | bytes 1500000 | tf_op jit(solution)/shard_map/pallas_call | solution.py:395
  2.5 4.8 %all-to-all-start = ((bf16[4,336,128]{2,1,0:T(8,128)(2,1)}), bf16[4,336,128]{2,1,0:T(8,128)(2,1)S(1)}, u32[]{:S(2)}, u32[]{:S(2)}) async-start(bf16[4,336,128]{2,1,0:T(8,128)(2,1)} %get-tuple-element.15), calls=%async_computation | async-start | bytes 688128 | tf_op jit(solution)/shard_map/all_to_all | solution.py:411
  7.4 3.4 %collective-permute-start = (bf16[128,128]{1,0:T(8,128)(2,1)S(1)}, bf16[128,128]{1,0:T(8,128)(2,1)S(1)}, u32[]{:S(2)}, u32[]{:S(2)}) collective-permute-start(bf16[128,128]{1,0:T(8,128)(2,1)S(1)} %get-tuple-element.16.mine_ref), channel_id=1, source_target_pairs={{0,1},{1,2},{2,3},{3,0},{4,5},{5,6},{6,7},{7,4},{8,9},{9,10},{10,1... | collective-permute-start | bytes 98312 | tf_op jit(solution)/shard_map/ppermute | solution.py:413
  10.7 0.0 copy-done
  10.7 0.1 dynamic_slice.9
  10.8 0.0 copy-done.1
  10.8 0.1 dynamic_slice.10
  10.9 0.1 broadcast_in_dim.3
  11.0 0.1 reshape_reshape.3.skip_ref
  11.1 0.8 %dynamic_slice.11 = f32[256]{0:T(256)S(1)} dynamic-slice(f32[1024]{0:T(1024)} %param.24, s32[]{:T(128)S(6)} %select_n.8), dynamic_slice_sizes={256} | dynamic-slice | bytes 2052 | tf_op jit(solution)/shard_map/dynamic_slice | solution.py:416
  11.8 1.3 %collective-permute-done.before_ref = bf16[128,128]{1,0:T(8,128)(2,1)S(1)} collective-permute-done((bf16[128,128]{1,0:T(8,128)(2,1)S(1)}, bf16[128,128]{1,0:T(8,128)(2,1)S(1)}, u32[]{:S(2)}, u32[]{:S(2)}) %collective-permute-start) | collective-permute-done | bytes 32800 | tf_op jit(solution)/shard_map/ppermute | solution.py:413
  13.2 0.3 all-to-all-done.in_ref
  13.4 2.9 %shard_map.185 = (bf16[32,8,2176]{2,1,0:T(8,128)(2,1)}, f32[128,128]{1,0:T(8,128)S(1)}, bf16[2,128,128]{2,1,0:T(8,128)(2,1)S(1)}) custom-call(bf16[4,336,128]{2,1,0:T(8,128)(2,1)S(1)} %all-to-all-done.in_ref, bf16[256,4096]{1,0:T(8,128)(2,1)} %w_ref.1, f32[1,128]{1,0:T(1,128)S(1)} %pad_bitcast_fusion.rate_ref, f32[1,256]{1,0:T(1,128)S(1)} %reshape_reshape.3.skip_ref, ...), custom_call_target="tpu_custom_call" | custom-call | flops 400000000 | bytes 4000000 | tf_op jit(solution)/shard_map/pallas_call | solution.py:417
  16.4 9.9 %all-to-all-start.1 = ((bf16[32,8,2176]{2,1,0:T(8,128)(2,1)}), bf16[32,8,2176]{2,1,0:T(8,128)(2,1)S(1)}, u32[]{:S(2)}, u32[]{:S(2)}) async-start(bf16[32,8,2176]{2,1,0:T(8,128)(2,1)} %get-tuple-element.17), calls=%async_computation.1 | async-start | bytes 2228224 | tf_op jit(solution)/shard_map/all_to_all | solution.py:435
  26.3 4.0 %collective-permute-start.1 = (bf16[2,128,128]{2,1,0:T(8,128)(2,1)S(1)}, bf16[2,128,128]{2,1,0:T(8,128)(2,1)S(1)}, u32[]{:S(2)}, u32[]{:S(2)}) collective-permute-start(bf16[2,128,128]{2,1,0:T(8,128)(2,1)S(1)} %get-tuple-element.18.pair_ref), channel_id=1, source_target_pairs={{0,2},{1,3},{2,0},{3,1},{4,6},{5,7},{6,4},{7,5},{8,10},{9,11},{10,... | collective-permute-start | bytes 196616 | tf_op jit(solution)/shard_map/ppermute | solution.py:434
  30.3 2.4 %shard_map.187 = (bf16[272,128]{1,0:T(8,128)(2,1)S(1)}, bf16[272,128]{1,0:T(8,128)(2,1)S(1)}, bf16[2,128,128]{2,1,0:T(8,128)(2,1)S(1)}) custom-call(s32[1]{0:T(128)} %bitcast.3.where_ref, s32[2]{0:T(128)} %len_ref.3, s32[2]{0:T(128)} %acc_ref.1, bf16[4,336,128]{2,1,0:T(8,128)(2,1)S(1)} %all-to-all-done.in_ref, ...), custom_call_target="tpu_custom_call" | custom-call | tf_op jit(solution)/shard_map/pallas_call | solution.py:438
  32.7 3.4 %collective-permute-start.4 = (bf16[272,128]{1,0:T(8,128)(2,1)S(1)}, bf16[272,128]{1,0:T(8,128)(2,1)S(1)}, u32[]{:S(2)}, u32[]{:S(2)}) collective-permute-start(bf16[272,128]{1,0:T(8,128)(2,1)S(1)} %get-tuple-element.24), channel_id=1, source_target_pairs={{0,3},{1,0},{2,1},{3,2},{4,7},{5,4},{6,5},{7,6},{8,11},{9,8},{10,9... | collective-permute-start | bytes 208904 | tf_op jit(solution)/shard_map/ppermute | solution.py:449
  36.1 0.0 collective-permute-done.1.farther_ref
  36.1 2.3 %shard_map.188 = (bf16[272,128]{1,0:T(8,128)(2,1)S(1)}, bf16[272,128]{1,0:T(8,128)(2,1)S(1)}) custom-call(s32[1]{0:T(128)} %bitcast.3.where_ref, s32[2]{0:T(128)} %len_ref.3, bf16[2,128,128]{2,1,0:T(8,128)(2,1)S(1)} %collective-permute-done.1.farther_ref, bf16[2,128,128]{2,1,0:T(8,128)(2,1)S(1)} %get-tuple-element.21.state_ref, bf16[2,1024,128]{2,1,0:T(8,128)(2,1)} %k_ref.3, ...), custom_call_target="tpu_custom_call" | custom-call | tf_op jit(solution)/shard_map/pallas_call | solution.py:445
  38.4 2.5 %collective-permute-start.2 = (bf16[272,128]{1,0:T(8,128)(2,1)S(1)}, bf16[272,128]{1,0:T(8,128)(2,1)S(1)}, u32[]{:S(2)}, u32[]{:S(2)}) collective-permute-start(bf16[272,128]{1,0:T(8,128)(2,1)S(1)} %get-tuple-element.22), channel_id=1, source_target_pairs={{0,1},{1,2},{2,3},{3,0},{4,5},{5,6},{6,7},{7,4},{8,9},{9,10},{10,1... | collective-permute-start | bytes 208904 | tf_op jit(solution)/shard_map/ppermute | solution.py:449
  40.8 4.6 %collective-permute-start.3 = (bf16[272,128]{1,0:T(8,128)(2,1)S(1)}, bf16[272,128]{1,0:T(8,128)(2,1)S(1)}, u32[]{:S(2)}, u32[]{:S(2)}) collective-permute-start(bf16[272,128]{1,0:T(8,128)(2,1)S(1)} %get-tuple-element.23), channel_id=1, source_target_pairs={{0,2},{1,3},{2,0},{3,1},{4,6},{5,7},{6,4},{7,5},{8,10},{9,11},{10,... | collective-permute-start | bytes 208904 | tf_op jit(solution)/shard_map/ppermute | solution.py:449
  45.4 0.0 collective-permute-done.4.last_ref
  45.4 0.3 collective-permute-done.2.next_ref
  45.7 3.2 %collective-permute-done.3.across_ref = bf16[272,128]{1,0:T(8,128)(2,1)S(1)} collective-permute-done((bf16[272,128]{1,0:T(8,128)(2,1)S(1)}, bf16[272,128]{1,0:T(8,128)(2,1)S(1)}, u32[]{:S(2)}, u32[]{:S(2)}) %collective-permute-start.3) | collective-permute-done | bytes 69664 | tf_op jit(solution)/shard_map/ppermute | solution.py:449
  48.9 1.1 %shard_map.189 = (bf16[2,16,512]{2,1,0:T(8,128)(2,1)}, bf16[2,16,32,64]{3,2,1,0:T(8,128)(2,1)}) custom-call(s32[1]{0:T(128)} %bitcast.3.where_ref, bf16[272,128]{1,0:T(8,128)(2,1)S(1)} %get-tuple-element.20.near_ref, bf16[272,128]{1,0:T(8,128)(2,1)S(1)} %collective-permute-done.2.next_ref, bf16[272,128]{1,0:T(8,128)(2,1)S(1)} %collective-permute-done.3.across_ref, ...), custom_call_target="tpu_custom_call" | custom-call | tf_op jit(solution)/shard_map/pallas_call | solution.py:452
  50.0 5.0 %all-to-all-done.1.in_ref = bf16[32,8,2176]{2,1,0:T(8,128)(2,1)S(1)} async-done(((bf16[32,8,2176]{2,1,0:T(8,128)(2,1)}), bf16[32,8,2176]{2,1,0:T(8,128)(2,1)S(1)}, u32[]{:S(2)}, u32[]{:S(2)}) %all-to-all-start.1) | async-done | bytes 1114144 | tf_op jit(solution)/shard_map/all_to_all | solution.py:435
  55.0 0.8 %shard_map.186 = bf16[2,2,4096]{2,1,0:T(2,128)(2,1)} custom-call(bf16[32,8,2176]{2,1,0:T(8,128)(2,1)S(1)} %all-to-all-done.1.in_ref), custom_call_target="tpu_custom_call" | custom-call | flops 1000000 | bytes 1500000 | tf_op jit(solution)/shard_map/pallas_call | solution.py:458
  (1 shorter events, 0.0 us)
Async XLA Ops:
  0.6 10.1 %copy-start = (f32[16]{0:T(128)S(1)}, f32[16]{0:T(128)}, u32[]{:S(2)}) copy-start(f32[16]{0:T(128)} %param.22) | copy-start | bytes 196
  0.6 10.2 %copy-start.1 = (f32[16]{0:T(128)S(1)}, f32[16]{0:T(128)}, u32[]{:S(2)}) copy-start(f32[16]{0:T(128)} %param.23) | copy-start | bytes 196
  2.5 10.9 %all-to-all-start = ((bf16[4,336,128]{2,1,0:T(8,128)(2,1)}), bf16[4,336,128]{2,1,0:T(8,128)(2,1)S(1)}, u32[]{:S(2)}, u32[]{:S(2)}) async-start(bf16[4,336,128]{2,1,0:T(8,128)(2,1)} %get-tuple-element.15), calls=%async_computation | async-start | bytes 688128 | tf_op jit(solution)/shard_map/all_to_all | solution.py:411
  7.4 5.8 %collective-permute-start = (bf16[128,128]{1,0:T(8,128)(2,1)S(1)}, bf16[128,128]{1,0:T(8,128)(2,1)S(1)}, u32[]{:S(2)}, u32[]{:S(2)}) collective-permute-start(bf16[128,128]{1,0:T(8,128)(2,1)S(1)} %get-tuple-element.16.mine_ref), channel_id=1, source_target_pairs={{0,1},{1,2},{2,3},{3,0},{4,5},{5,6},{6,7},{7,4},{8,9},{9,10},{10,1... | collective-permute-start | bytes 98312 | tf_op jit(solution)/shard_map/ppermute | solution.py:413
  16.4 38.7 %all-to-all-start.1 = ((bf16[32,8,2176]{2,1,0:T(8,128)(2,1)}), bf16[32,8,2176]{2,1,0:T(8,128)(2,1)S(1)}, u32[]{:S(2)}, u32[]{:S(2)}) async-start(bf16[32,8,2176]{2,1,0:T(8,128)(2,1)} %get-tuple-element.17), calls=%async_computation.1 | async-start | bytes 2228224 | tf_op jit(solution)/shard_map/all_to_all | solution.py:435
  26.3 9.8 %collective-permute-start.1 = (bf16[2,128,128]{2,1,0:T(8,128)(2,1)S(1)}, bf16[2,128,128]{2,1,0:T(8,128)(2,1)S(1)}, u32[]{:S(2)}, u32[]{:S(2)}) collective-permute-start(bf16[2,128,128]{2,1,0:T(8,128)(2,1)S(1)} %get-tuple-element.18.pair_ref), channel_id=1, source_target_pairs={{0,2},{1,3},{2,0},{3,1},{4,6},{5,7},{6,4},{7,5},{8,10},{9,11},{10,... | collective-permute-start | bytes 196616 | tf_op jit(solution)/shard_map/ppermute | solution.py:434
  32.7 12.7 %collective-permute-start.4 = (bf16[272,128]{1,0:T(8,128)(2,1)S(1)}, bf16[272,128]{1,0:T(8,128)(2,1)S(1)}, u32[]{:S(2)}, u32[]{:S(2)}) collective-permute-start(bf16[272,128]{1,0:T(8,128)(2,1)S(1)} %get-tuple-element.24), channel_id=1, source_target_pairs={{0,3},{1,0},{2,1},{3,2},{4,7},{5,4},{6,5},{7,6},{8,11},{9,8},{10,9... | collective-permute-start | bytes 208904 | tf_op jit(solution)/shard_map/ppermute | solution.py:449
  38.4 7.3 %collective-permute-start.2 = (bf16[272,128]{1,0:T(8,128)(2,1)S(1)}, bf16[272,128]{1,0:T(8,128)(2,1)S(1)}, u32[]{:S(2)}, u32[]{:S(2)}) collective-permute-start(bf16[272,128]{1,0:T(8,128)(2,1)S(1)} %get-tuple-element.22), channel_id=1, source_target_pairs={{0,1},{1,2},{2,3},{3,0},{4,5},{5,6},{6,7},{7,4},{8,9},{9,10},{10,1... | collective-permute-start | bytes 208904 | tf_op jit(solution)/shard_map/ppermute | solution.py:449
  40.8 8.1 %collective-permute-start.3 = (bf16[272,128]{1,0:T(8,128)(2,1)S(1)}, bf16[272,128]{1,0:T(8,128)(2,1)S(1)}, u32[]{:S(2)}, u32[]{:S(2)}) collective-permute-start(bf16[272,128]{1,0:T(8,128)(2,1)S(1)} %get-tuple-element.23), channel_id=1, source_target_pairs={{0,2},{1,3},{2,0},{3,1},{4,6},{5,7},{6,4},{7,5},{8,10},{9,11},{10,... | collective-permute-start | bytes 208904 | tf_op jit(solution)/shard_map/ppermute | solution.py:449
